TPU v7x, 32 devices: a whole 2x2x4 slice. The times are simulated.
32 devices in a mesh: section: 4 (over y, x), tp: 4 (over z), dp: 2 (over core).
Axes of the slice: x: 2, y: 2, z: 4, core: 2. Of those that a mesh axis runs over, the one named last changes fastest.
Arguments:
- stash: bfloat16 [4, 2, 320, 48, 384], P('section', 'dp', None, 'tp'), may hold values from -24 to 24
- grad_out: bfloat16 [4, 2, 320, 6144], P('section', 'dp', None, 'tp'), may hold values from -6 to 6
- doc_lengths: int32 [4, 2, 8], P('section', 'dp'), may hold values from 1 to 160, 320 in all within a row
Outputs:
- qkv_grad: bfloat16 [4, 2, 320, 48, 384], P('section', 'dp', None, 'tp')
- bias_grad: float32 [4, 48, 384], P('section', 'tp')
Inputs may be any that keep to these rules, and one draw needn't show every extreme that they name: `doc_lengths`: the 8 lengths of one micro-batch sum to 320, and in each micro-batch one of them is exactly 160.
All inputs are finite; a program needn't handle non-finite values.
Results may differ from a plain program's by a relative error of at most 0.012.
Values may be sent and summed in bfloat16 or wider, within the bound.
No kernel may reach another device: no remote copies, remote signals or barrier semaphores. Data moves between devices by JAX's collectives and lax.ppermute only.
A program may use at most 64 MiB of HBM per device.

v0:
```python
import math

import jax
import jax.numpy as jnp
from jax import lax
from jax.sharding import PartitionSpec as P


def segment_of(lengths, row_count):
    doc_ends = jnp.cumsum(lengths)
    position = jnp.arange(row_count, dtype=jnp.int32)
    return jnp.sum((position[:, None] >= doc_ends[None, :]).astype(jnp.int32), axis=1)


def attention_grads(packed, grad_rows, lengths):
    row_count, head_count, pack_width = packed.shape
    head_size = pack_width // 3
    inv_root = 1.0 / math.sqrt(head_size)
    queries = packed[:, :, :head_size]
    keys_in = packed[:, :, head_size : 2 * head_size]
    values_in = packed[:, :, 2 * head_size :]
    grad_heads = grad_rows.reshape(row_count, head_count, head_size)
    segment = segment_of(lengths, row_count)
    position = jnp.arange(row_count, dtype=jnp.int32)
    allowed = (segment[:, None] == segment[None, :]) & (position[None, :] <= position[:, None])
    scores = (
        jnp.einsum("qhd,khd->hqk", queries, keys_in, preferred_element_type=jnp.float32) * inv_root
    )
    masked = jnp.where(allowed[None], scores, -jnp.inf)
    row_top = jnp.max(masked, axis=-1, keepdims=True)
    raised = jnp.exp(masked - row_top)
    attn_prob = raised / jnp.sum(raised, axis=-1, keepdims=True)
    prob_low = attn_prob.astype(jnp.bfloat16)
    attn_out = jnp.einsum("hqk,khd->qhd", prob_low, values_in, preferred_element_type=jnp.float32)
    row_dot = jnp.einsum("qhd,qhd->hq", grad_heads.astype(jnp.float32), attn_out)
    prob_grad = jnp.einsum(
        "qhd,khd->hqk", grad_heads, values_in, preferred_element_type=jnp.float32
    )
    score_grad = attn_prob * (prob_grad - row_dot[:, :, None]) * inv_root
    score_low = score_grad.astype(jnp.bfloat16)
    query_grad = jnp.einsum("hqk,khd->qhd", score_low, keys_in, preferred_element_type=jnp.float32)
    key_grad = jnp.einsum("hqk,qhd->khd", score_low, queries, preferred_element_type=jnp.float32)
    value_grad = jnp.einsum(
        "hqk,qhd->khd", prob_low, grad_heads, preferred_element_type=jnp.float32
    )
    return jnp.concatenate([query_grad, key_grad, value_grad], axis=-1)


def send_back(received):
    return lax.all_to_all(jnp.flip(received, 0), "section", split_axis=0, concat_axis=0, tiled=True)


def mirror_fetch(stash):
    packed = stash[0, 0]
    row_count, head_count, pack_width = packed.shape
    section_count = lax.axis_size("section")
    blocks = packed.reshape(section_count, row_count // section_count, head_count, pack_width)
    returned = send_back(lax.all_to_all(blocks, "section", split_axis=0, concat_axis=0, tiled=True))
    return returned.reshape(row_count, head_count, pack_width)


def body(stash, grad_out, doc_lengths):
    fetched = mirror_fetch(stash)
    grads = attention_grads(fetched, grad_out[0, 0], doc_lengths[0, 0])
    qkv_grad = grads.astype(jnp.bfloat16)[None, None]
    bias_local = jnp.sum(grads, axis=0)
    bias_total = lax.psum(bias_local, "dp")
    bias_grad = (bias_total / lax.axis_size("dp"))[None]
    return (qkv_grad, bias_grad)


def solution(mesh):
    in_specs = (
        P("section", "dp", None, "tp", None),
        P("section", "dp", None, "tp"),
        P("section", "dp", None),
    )
    out_specs = (P("section", "dp", None, "tp", None), P("section", "tp", None))
    return jax.shard_map(body, mesh=mesh, in_specs=in_specs, out_specs=out_specs, check_vma=False)
```

profile of v0, /device:TPU:0, one launch (start us, length us, event | category | flops | bytes accessed | tf_op | source)
XLA Modules:
  0.0 98.1 jit_solution(7951624747856560318)
XLA Ops:
  0.6 2.1 %copy.29 = bf16[4,80,12,384]{3,1,2,0:T(8,128)(2,1)S(1)} copy(bf16[4,80,12,384]{3,1,0,2:T(8,128)(2,1)} %bitcast.36) | data formatting | bytes 5898240 | tf_op jit(solution)/shard_map/reshape;squeeze | solution.py:57
  2.8 39.7 %all_to_all.10 = bf16[4,80,12,384]{3,1,2,0:T(8,128)(2,1)S(1)} all-to-all(bf16[4,80,12,384]{3,1,2,0:T(8,128)(2,1)S(1)} %copy.29), channel_id=1, replica_groups=mesh['section'=4,'tp'=4,'dp'=2] {'section'}, dimensions={0} | all-to-all | bytes 5898240 | tf_op jit(solution)/shard_map/all_to_all | solution.py:58
  42.4 1.9 %rev.4 = bf16[4,80,12,384]{3,1,2,0:T(8,128)(2,1)} reverse(bf16[4,80,12,384]{3,1,2,0:T(8,128)(2,1)S(1)} %all_to_all.10), dimensions={0} | reverse | bytes 5898240 | tf_op jit(solution)/shard_map/jit(_flip)/rev | solution.py:50
  44.3 3.7 %all-to-all-start.1 = ((bf16[4,80,12,384]{3,1,2,0:T(8,128)(2,1)}), bf16[4,80,12,384]{3,1,2,0:T(8,128)(2,1)S(1)}, u32[]{:S(2)}, u32[]{:S(2)}) async-start(bf16[4,80,12,384]{3,1,2,0:T(8,128)(2,1)} %rev.4), calls=%async_computation.1 | async-start | bytes 5898240 | tf_op jit(solution)/shard_map/all_to_all | solution.py:50
  48.0 0.0 copy-start.2
  48.0 2.4 %copy.48 = bf16[1,1,320,1536]{2,3,0,1:T(8,128)(2,1)} copy(bf16[1,1,320,1536]{3,2,1,0:T(8,128)(2,1)} %param.4) | data formatting | bytes 1966080
  50.4 2.3 %copy.31 = bf16[1,1,320,1536]{2,3,1,0:T(8,128)(2,1)} copy(bf16[1,1,320,1536]{3,2,1,0:T(8,128)(2,1)} %param.4) | data formatting | bytes 1966080 | tf_op args[1]
  52.7 0.0 copy-done.2
  52.7 0.2 reduce-window.8
  52.9 0.1 convert_reduce_fusion
  53.0 0.1 fusion.13
  53.1 27.8 %all-to-all-done.1 = bf16[4,80,12,384]{3,1,2,0:T(8,128)(2,1)S(1)} async-done(((bf16[4,80,12,384]{3,1,2,0:T(8,128)(2,1)}), bf16[4,80,12,384]{3,1,2,0:T(8,128)(2,1)S(1)}, u32[]{:S(2)}, u32[]{:S(2)}) %all-to-all-start.1) | async-done | bytes 2949152 | tf_op jit(solution)/shard_map/all_to_all | solution.py:50
  81.0 0.4 copy.30
  81.4 0.9 fusion.9
  82.3 1.9 %fusion.16 = (f32[12,320]{1,0:T(8,128)S(1)}, f32[12,320,320]{1,2,0:T(8,128)S(1)}) fusion(f32[12,320,320]{1,2,0:T(8,128)S(1)} %fusion.9, pred[320,320]{0,1:T(8,128)(4,1)S(1)} %fusion.13), kind=kOutput, calls=%fused_computation.33 | output fusion | flops 7373119 | bytes 9948160 | tf_op jit(solution)/shard_map/sub | solution.py:31
  84.2 0.0 copy-start.1
  84.2 0.6 fusion.5
  84.9 0.6 copy-done.1
  85.5 0.0 copy-start
  85.5 1.1 %multiply_reduce_fusion = f32[12,320]{1,0:T(8,128)S(1)} fusion(bf16[12,320,128]{1,2,0:T(8,128)(2,1)S(1)} %bitcast.37, bf16[12,320,320]{1,2,0:T(8,128)(2,1)S(1)} %fusion.5, bf16[320,12,384]{2,0,1:T(8,128)(2,1)S(1)} %bitcast.30), kind=kOutput, calls=%fused_computation.12 | convolution fusion | flops 316043520 | bytes 5127168
  86.6 0.2 copy-done
  86.8 1.3 %multiply_convert_fusion = bf16[12,320,320]{1,2,0:T(8,128)(2,1)S(1)} fusion(f32[12,320]{1,0:T(8,128)S(1)} %multiply_reduce_fusion, bf16[320,12,128]{0,2,1:T(8,128)(2,1)S(1)} %bitcast.34, f32[12,320,320]{1,2,0:T(8,128)S(1)} %get-tuple-element.3, f32[12,320]{1,0:T(8,128)S(1)} %get-tuple-element.2, bf16[320,12,384]{2,0,1:T(8,128)(2,1)S(1)} %bitcast.31), kind=kOutput, calls=%fused_computation.2 | convolution fusion | flops 320716800 | bytes 10567680 | tf_op jit(solution)/shard_map/qhd,khd->hqk/dot_general | solution.py:36
  88.1 1.1 %convolution_bitcast_fusion.2 = f32[320,12,128]{2,0,1:T(8,128)S(1)} fusion(bf16[12,320,320]{1,2,0:T(8,128)(2,1)S(1)} %multiply_convert_fusion, bf16[320,12,384]{2,0,1:T(8,128)(2,1)S(1)} %bitcast.32), kind=kOutput, calls=%fused_computation.15 | convolution fusion | flops 314572800 | bytes 5898240 | tf_op jit(solution)/shard_map/hqk,khd->qhd/dot_general | solution.py:41
  89.2 0.9 convolution_bitcast_fusion.1
  90.1 0.9 convolution_bitcast_fusion
  91.1 0.4 convert_bitcast_fusion
  91.5 0.4 maximum_reduce_fusion
  91.8 0.1 convert_bitcast_fusion.2
  92.0 3.4 %psum.7 = f32[12,384]{1,0:T(8,128)S(1)} all-reduce(f32[12,384]{1,0:T(8,128)S(1)} %maximum_reduce_fusion), channel_id=1, replica_groups=mesh['section'=4,'tp'=4,'dp'=2] {'dp'}, use_global_device_ids=true, to_apply=%region_5.6 | all-reduce | flops 4608 | bytes 36864 | tf_op jit(solution)/shard_map/psum | solution.py:67
  95.4 0.6 broadcast_in_dim.16
  96.1 2.0 %pad_maximum_fusion = bf16[1,1,320,12,384]{4,2,3,1,0:T(8,128)(2,1)} fusion(bf16[1,1,320,12,128]{4,2,3,1,0:T(8,128)(2,1)S(1)} %get-tuple-element.4, bf16[1,1,320,12,128]{4,2,3,1,0:T(8,128)(2,1)S(1)} %get-tuple-element.5, bf16[1,1,320,12,128]{4,2,3,1,0:T(8,128)(2,1)S(1)} %convert_bitcast_fusion.2), kind=kLoop, calls=%fused_computation.6 | loop fusion | flops 8847360 | bytes 5898240 | tf_op jit(solution)/shard_map/concatenate | solution.py:46
  (1 shorter events, 0.0 us)
Async XLA Ops:
  44.3 36.6 %all-to-all-start.1 = ((bf16[4,80,12,384]{3,1,2,0:T(8,128)(2,1)}), bf16[4,80,12,384]{3,1,2,0:T(8,128)(2,1)S(1)}, u32[]{:S(2)}, u32[]{:S(2)}) async-start(bf16[4,80,12,384]{3,1,2,0:T(8,128)(2,1)} %rev.4), calls=%async_computation.1 | async-start | bytes 5898240 | tf_op jit(solution)/shard_map/all_to_all | solution.py:50
  48.0 4.7 %copy-start.2 = (s32[1,1,8]{2,1,0:T(1,128)S(1)}, s32[1,1,8]{2,1,0:T(1,128)}, u32[]{:S(2)}) copy-start(s32[1,1,8]{2,1,0:T(1,128)} %param.5) | copy-start | bytes 100
  84.2 1.3 %copy-start.1 = (bf16[1,1,320,1536]{2,3,0,1:T(8,128)(2,1)S(1)}, bf16[1,1,320,1536]{2,3,0,1:T(8,128)(2,1)}, u32[]{:S(2)}) copy-start(bf16[1,1,320,1536]{2,3,0,1:T(8,128)(2,1)} %copy.48) | copy-start | bytes 2949124
  85.5 1.3 %copy-start = (bf16[1,1,320,1536]{2,3,1,0:T(8,128)(2,1)S(1)}, bf16[1,1,320,1536]{2,3,1,0:T(8,128)(2,1)}, u32[]{:S(2)}) copy-start(bf16[1,1,320,1536]{2,3,1,0:T(8,128)(2,1)} %copy.31) | copy-start | bytes 2949124
where the time goes:
time: 98.5 us; the launch traced here: 98.1 us
  blocking collectives  43.1 us (44%)
  waiting for transfers between devices  27.8 us (28%)
  local copies, waits for them, and re-layouts  10.6 us (11%)
  matrix products  6.24 us (6%)
  other arithmetic  5.86 us (6%)
  starting transfers between devices  3.68 us (4%)
    all_to_all x1, blocking collectives, mirror_fetch(): lax.all_to_all(blocks, 'section', split_axis=0, concat_axis=0, tiled=True)  39.7 us
    all_to_all x1, waiting for transfers between devices, send_back(): lax.all_to_all(jnp.flip(received, 0), 'section', split_axis=0, concat_axi...  27.8 us
    unnamed x8, local copies, waits for them, and re-layouts  5.56 us
    all_to_all x1, starting transfers between devices, send_back(): lax.all_to_all(jnp.flip(received, 0), 'section', split_axis=0, concat_axi...  3.68 us
    psum x1, blocking collectives, body(): bias_total = lax.psum(bias_local, 'dp')  3.42 us
    concatenate x3, other arithmetic, attention_grads(): return jnp.concatenate([query_grad, key_grad, value_grad], axis=-1)  2.57 us
    another operation x1, local copies, waits for them, and re-layouts, mirror_fetch(): packed.reshape(section_count, row_count // section_count, head_count, pac...  2.13 us
  transfers between devices with their start and end apart: 1, of which 1 were waited for; matrix products, arithmetic and copies ran while one was open for 5% of the time, Pallas kernels for 0%

commit v1 on v0

v1 whole, which is shorter than its diff:
```python
import functools
import math

import jax
import jax.numpy as jnp
from jax import lax
from jax.experimental import pallas as pl
from jax.experimental.pallas import tpu as pltpu
from jax.sharding import PartitionSpec as P

MASKED = -1e30


def grads_kernel(lengths_ref, packed_ref, grad_ref, *refs):
    out_ref, bias_ref = refs[-2:]
    row_count = packed_ref.shape[1]
    head_size = packed_ref.shape[2] // 3
    inv_root = 1.0 / math.sqrt(head_size)
    query_at = lax.broadcasted_iota(jnp.int32, (1, row_count), 1)
    doc_start = jnp.zeros((1, row_count), jnp.int32)
    doc_end = jnp.int32(0)
    for doc in range(lengths_ref.shape[0]):
        doc_end = doc_end + lengths_ref[doc]
        doc_start = jnp.where(query_at >= doc_end, doc_end, doc_start)
    key_at = lax.broadcasted_iota(jnp.int32, (row_count, row_count), 0)
    allowed = (key_at >= doc_start) & (key_at <= query_at)

    queries = packed_ref[0, :, :head_size]
    keys_in = packed_ref[0, :, head_size : 2 * head_size]
    values_in = packed_ref[0, :, 2 * head_size :]
    grad_rows = grad_ref[...]
    rows_by_rows = (((1,), (1,)), ((), ()))
    plain = (((1,), (0,)), ((), ()))
    columns = (((0,), (0,)), ((), ()))
    dot = functools.partial(lax.dot_general, preferred_element_type=jnp.float32)

    scores = dot(keys_in, queries, rows_by_rows) * inv_root
    masked = jnp.where(allowed, scores, MASKED)
    raised = jnp.exp(masked - jnp.max(masked, axis=0, keepdims=True))
    prob = raised * (1.0 / jnp.sum(raised, axis=0, keepdims=True))
    prob_low = prob.astype(jnp.bfloat16)
    prob_grad = dot(values_in, grad_rows, rows_by_rows)
    row_dot = jnp.sum(prob_low.astype(jnp.float32) * prob_grad, axis=0, keepdims=True)
    score_low = (prob * (prob_grad - row_dot) * inv_root).astype(jnp.bfloat16)
    grads = (
        dot(score_low, keys_in, columns),
        dot(score_low, queries, plain),
        dot(prob_low, grad_rows, plain),
    )
    for part, grad in enumerate(grads):
        span = slice(part * head_size, (part + 1) * head_size)
        out_ref[0, :, span] = grad.astype(jnp.bfloat16)
        bias_ref[0, :, span] = jnp.sum(grad, axis=0, keepdims=True)


def chunk_grads(packed, grad_rows, lengths, head_count, first_head, previous):
    chunk_heads, row_count, pack_width = packed.shape
    head_size = pack_width // 3
    in_specs = [
        pl.BlockSpec((1, row_count, pack_width), lambda h, _: (h, 0, 0)),
        pl.BlockSpec((row_count, head_size), lambda h, _: (0, first_head + h)),
    ]
    operands = [packed, grad_rows]
    aliases = {}
    if previous is not None:
        in_specs.append(pl.BlockSpec(memory_space=pl.ANY))
        operands.append(previous)
        aliases = {3: 0}
    return pl.pallas_call(
        grads_kernel,
        grid_spec=pltpu.PrefetchScalarGridSpec(
            num_scalar_prefetch=1,
            grid=(chunk_heads,),
            in_specs=in_specs,
            out_specs=[
                pl.BlockSpec((1, row_count, pack_width), lambda h, _: (first_head + h, 0, 0)),
                pl.BlockSpec((1, 1, pack_width), lambda h, _: (h, 0, 0)),
            ],
        ),
        out_shape=[
            jax.ShapeDtypeStruct((head_count, row_count, pack_width), jnp.bfloat16),
            jax.ShapeDtypeStruct((chunk_heads, 1, pack_width), jnp.float32),
        ],
        input_output_aliases=aliases,
        name=f"grads_at_{first_head}",
    )(lengths, *operands)


def chunk_sizes(head_count):
    sizes = []
    rest, size = head_count, 1
    while rest > 0:
        size = min(size, rest)
        sizes.append(size)
        rest -= size
        size *= 3
    return sizes[::-1]


def replica_sum(value, axis):
    count = lax.axis_size(axis)
    if count & (count - 1):
        return lax.psum(value, axis)
    stride = 1
    while stride < count:
        value = value + lax.ppermute(value, axis, [(i, i ^ stride) for i in range(count)])
        stride *= 2
    return value


def body(stash, grad_out, doc_lengths):
    by_head = jnp.transpose(stash[0, 0], (1, 0, 2))
    head_count = by_head.shape[0]
    section_count = lax.axis_size("section")
    mirror = [(i, section_count - 1 - i) for i in range(section_count)]
    sizes = chunk_sizes(head_count)
    firsts = [sum(sizes[:i]) for i in range(len(sizes))]
    arrived = []
    for index, (first, size) in enumerate(zip(firsts, sizes)):
        with jax.named_scope(f"chunk{index}"):
            arrived.append(lax.ppermute(by_head[first : first + size], "section", mirror))
    grads, bias_parts = None, []
    for first, packed in zip(firsts, arrived):
        grads, bias = chunk_grads(
            packed, grad_out[0, 0], doc_lengths[0, 0], head_count, first, grads
        )
        bias_parts.append(bias)
    bias_total = replica_sum(jnp.concatenate(bias_parts, axis=0), "dp")
    bias_grad = jnp.transpose(bias_total / lax.axis_size("dp"), (1, 0, 2))
    return (jnp.transpose(grads, (1, 0, 2))[None, None], bias_grad)


def solution(mesh):
    in_specs = (
        P("section", "dp", None, "tp", None),
        P("section", "dp", None, "tp"),
        P("section", "dp", None),
    )
    out_specs = (P("section", "dp", None, "tp", None), P("section", "tp", None))
    return jax.shard_map(body, mesh=mesh, in_specs=in_specs, out_specs=out_specs, check_vma=False)
```

time: 98.5 us -> 78.8 us (0.80)
  blocking collectives: 43.1 us -> 0 us
  Pallas kernels: 0 us -> 18.3 us
  waiting for transfers between devices: 27.8 us -> 43.5 us
  matrix products: 6.24 us -> 0 us
  other arithmetic: 5.86 us -> 0.63 us
  starting transfers between devices: 3.68 us -> 6.98 us
  local copies, waits for them, and re-layouts: 10.6 us -> 8.21 us
    ppermute x0 -> x4, waiting for transfers between devices: none -> 43.5 us  [the longest x3 42.3 us: body(): arrived.append(lax.ppermute(by_head[first:first + size], 'section', mirror))]
    all_to_all x1 -> x0, blocking collectives: 39.7 us -> none  [mirror_fetch(): lax.all_to_all(blocks, 'section', split_axis=0, concat_axis=0, tiled=True)]
    all_to_all x1 -> x0, waiting for transfers between devices: 27.8 us -> none  [send_back(): lax.all_to_all(jnp.flip(received, 0), 'section', split_axis=0, concat_axi...]
    pallas_call x0 -> x3, Pallas kernels: none -> 18.3 us  [chunk_grads(): pl.pallas_call(grads_kernel, grid_spec=pltpu.PrefetchScalarGridSpec(num_s...]
    ppermute x0 -> x4, starting transfers between devices: none -> 6.98 us  [the longest x3 6.98 us: body(): arrived.append(lax.ppermute(by_head[first:first + size], 'section', mirror))]
    dot_general x5 -> x0, matrix products: 5.18 us -> none  [the longest x1 1.28 us: attention_grads(): jnp.einsum('qhd,khd->hqk', grad_heads, values_in, preferred_element_type=...]
    slice x0 -> x3, local copies, waits for them, and re-layouts: none -> 4.64 us  [body(): arrived.append(lax.ppermute(by_head[first:first + size], 'section', mirror))]
    all_to_all x1 -> x0, starting transfers between devices: 3.68 us -> none  [send_back(): lax.all_to_all(jnp.flip(received, 0), 'section', split_axis=0, concat_axi...]
  transfers between devices with their start and end apart: 1 -> 4, of which waited for: 1 -> 3; matrix products, arithmetic and copies ran while one was open for 5% -> 5% of each run, Pallas kernels for 0% -> 19%
where the time goes in v1:
time: 78.8 us; the launch traced here: 78.3 us
  waiting for transfers between devices  43.5 us (55%)
  Pallas kernels  18.3 us (23%)
  local copies, waits for them, and re-layouts  8.21 us (10%)
  starting transfers between devices  6.98 us (9%)
    ppermute x3, waiting for transfers between devices, body(): arrived.append(lax.ppermute(by_head[first:first + size], 'section', mirror))  42.3 us
    pallas_call x3, Pallas kernels, chunk_grads(): pl.pallas_call(grads_kernel, grid_spec=pltpu.PrefetchScalarGridSpec(num_s...  18.3 us
    ppermute x3, starting transfers between devices, body(): arrived.append(lax.ppermute(by_head[first:first + size], 'section', mirror))  6.98 us
    slice x3, local copies, waits for them, and re-layouts, body(): arrived.append(lax.ppermute(by_head[first:first + size], 'section', mirror))  4.64 us
    unnamed x8, local copies, waits for them, and re-layouts  2.88 us
  transfers between devices with their start and end apart: 4, of which 3 were waited for; matrix products, arithmetic and copies ran while one was open for 5% of the time, Pallas kernels for 19%

profile of v1, /device:TPU:0, one launch (start us, length us, event | category | flops | bytes accessed | tf_op | source)
XLA Modules:
  0.0 78.3 jit_solution(13834517239323267588)
XLA Ops:
  0.6 1.7 %slice.14 = bf16[8,320,384]{2,1,0:T(8,128)(2,1)S(1)} slice(bf16[12,320,384]{2,1,0:T(8,128)(2,1)} %bitcast.14), slice={[0:8], [0:320], [0:384]} | slice | bytes 3932160 | tf_op jit(solution)/shard_map/chunk0/slice | solution.py:121
  2.4 4.0 %collective-permute-start.2 = (bf16[8,320,384]{2,1,0:T(8,128)(2,1)S(1)}, bf16[8,320,384]{2,1,0:T(8,128)(2,1)S(1)}, u32[]{:S(2)}, u32[]{:S(2)}) collective-permute-start(bf16[8,320,384]{2,1,0:T(8,128)(2,1)S(1)} %slice.14), channel_id=1, source_target_pairs={{0,24},{8,16},{16,8},{24,0},{1,25},{9,17},{17,9},{25,1},{2,26},{10... | collective-permute-start | bytes 5898248 | tf_op jit(solution)/shard_map/chunk0/ppermute | solution.py:121
  6.4 1.2 %slice.13 = bf16[3,320,384]{2,1,0:T(8,128)(2,1)S(1)} slice(bf16[12,320,384]{2,1,0:T(8,128)(2,1)} %bitcast.15), slice={[8:11], [0:320], [0:384]} | slice | bytes 1474560 | tf_op jit(solution)/shard_map/chunk1/slice | solution.py:121
  7.6 0.1 collective-permute-start.1
  7.6 1.7 %slice.12 = bf16[1,320,384]{2,1,0:T(8,128)(2,1)} slice(bf16[12,320,384]{2,1,0:T(8,128)(2,1)} %bitcast.16), slice={[11:12], [0:320], [0:384]} | slice | bytes 491520 | tf_op jit(solution)/shard_map/chunk2/slice | solution.py:121
  9.3 2.9 %collective-permute-start = (bf16[1,320,384]{2,1,0:T(8,128)(2,1)}, bf16[1,320,384]{2,1,0:T(8,128)(2,1)}, u32[]{:S(2)}, u32[]{:S(2)}) collective-permute-start(bf16[1,320,384]{2,1,0:T(8,128)(2,1)} %slice.12), channel_id=1, source_target_pairs={{0,24},{8,16},{16,8},{24,0},{1,25},{9,17},{17,9},{25,1},{2,26},{10... | collective-permute-start | bytes 737288 | tf_op jit(solution)/shard_map/chunk2/ppermute | solution.py:121
  12.3 37.8 %collective-permute-done.2.packed_ref = bf16[8,320,384]{2,1,0:T(8,128)(2,1)S(1)} collective-permute-done((bf16[8,320,384]{2,1,0:T(8,128)(2,1)S(1)}, bf16[8,320,384]{2,1,0:T(8,128)(2,1)S(1)}, u32[]{:S(2)}, u32[]{:S(2)}) %collective-permute-start.2) | collective-permute-done | bytes 1966112 | tf_op jit(solution)/shard_map/chunk0/ppermute | solution.py:121
  50.0 0.0 copy-start
  50.0 1.3 %copy-done = bf16[8,320,384]{2,1,0:T(8,128)(2,1)} copy-done((bf16[8,320,384]{2,1,0:T(8,128)(2,1)}, bf16[8,320,384]{2,1,0:T(8,128)(2,1)S(1)}, u32[]{:S(2)}) %copy-start) | copy-done | bytes 1966104
  51.3 10.0 %grads_at_0.1 = (bf16[12,320,384]{2,1,0:T(8,128)(2,1)}, f32[8,1,384]{2,1,0:T(1,128)}) custom-call(s32[8]{0:T(128)} %bitcast.17, bf16[8,320,384]{2,1,0:T(8,128)(2,1)} %copy-done, bf16[320,1536]{1,0:T(8,128)(2,1)} %bitcast.11), custom_call_target="tpu_custom_call" | custom-call | tf_op jit(solution)/shard_map/grads_at_0/pallas_call | solution.py:69
  61.3 0.0 copy-start.2
  61.3 4.5 %collective-permute-done.1.packed_ref = bf16[3,320,384]{2,1,0:T(8,128)(2,1)S(1)} collective-permute-done((bf16[3,320,384]{2,1,0:T(8,128)(2,1)S(1)}, bf16[3,320,384]{2,1,0:T(8,128)(2,1)S(1)}, u32[]{:S(2)}, u32[]{:S(2)}) %collective-permute-start.1) | collective-permute-done | bytes 737312 | tf_op jit(solution)/shard_map/chunk1/ppermute | solution.py:121
  65.8 0.0 copy-start.1
  65.8 0.9 %copy-done.1 = bf16[3,320,384]{2,1,0:T(8,128)(2,1)} copy-done((bf16[3,320,384]{2,1,0:T(8,128)(2,1)}, bf16[3,320,384]{2,1,0:T(8,128)(2,1)S(1)}, u32[]{:S(2)}) %copy-start.1) | copy-done | bytes 737304
  66.7 5.1 %grads_at_8.1 = (bf16[12,320,384]{2,1,0:T(8,128)(2,1)}, f32[3,1,384]{2,1,0:T(1,128)}) custom-call(s32[8]{0:T(128)} %bitcast.18, bf16[3,320,384]{2,1,0:T(8,128)(2,1)} %copy-done.1, bf16[320,1536]{1,0:T(8,128)(2,1)} %bitcast.12, bf16[12,320,384]{2,1,0:T(8,128)(2,1)} %get-tuple-element.8.refs_0_), custom_call_target="tpu_custom_call", output_to_operand_aliasing={{0}: (3, {})} | custom-call | tf_op jit(solution)/shard_map/grads_at_8/pallas_call | solution.py:69
  71.9 0.0 copy-done.2
  71.9 0.7 constant_dynamic-update-slice_fusion.1
  72.6 0.0 collective-permute-done.packed_ref
  72.6 3.2 %grads_at_11.1 = (bf16[12,320,384]{2,1,0:T(8,128)(2,1)}, f32[1,1,384]{2,1,0:T(1,128)}) custom-call(s32[8]{0:T(128)} %bitcast.19, bf16[1,320,384]{2,1,0:T(8,128)(2,1)} %collective-permute-done.packed_ref, bf16[320,1536]{1,0:T(8,128)(2,1)} %bitcast.13, bf16[12,320,384]{2,1,0:T(8,128)(2,1)} %get-tuple-element.9.refs_0_), custom_call_target="tpu_custom_call", output_to_operand_aliasing={{0}: (3, {})} | custom-call | tf_op jit(solution)/shard_map/grads_at_11/pallas_call | solution.py:69
  75.8 0.7 constant_dynamic-update-slice_fusion
  76.4 0.0 collective-permute-start.3
  76.4 1.2 %collective-permute-done.3 = f32[12,1,384]{2,1,0:T(1,128)S(1)} collective-permute-done((f32[12,1,384]{2,1,0:T(1,128)S(1)}, f32[12,1,384]{2,1,0:T(1,128)S(1)}, u32[]{:S(2)}, u32[]{:S(2)}) %collective-permute-start.3) | collective-permute-done | bytes 18464 | tf_op jit(solution)/shard_map/ppermute | solution.py:106
  77.6 0.6 multiply_bitcast_fusion
  (1 shorter events, 0.0 us)
Async XLA Ops:
  2.4 47.7 %collective-permute-start.2 = (bf16[8,320,384]{2,1,0:T(8,128)(2,1)S(1)}, bf16[8,320,384]{2,1,0:T(8,128)(2,1)S(1)}, u32[]{:S(2)}, u32[]{:S(2)}) collective-permute-start(bf16[8,320,384]{2,1,0:T(8,128)(2,1)S(1)} %slice.14), channel_id=1, source_target_pairs={{0,24},{8,16},{16,8},{24,0},{1,25},{9,17},{17,9},{25,1},{2,26},{10... | collective-permute-start | bytes 5898248 | tf_op jit(solution)/shard_map/chunk0/ppermute | solution.py:121
  7.6 58.3 %collective-permute-start.1 = (bf16[3,320,384]{2,1,0:T(8,128)(2,1)S(1)}, bf16[3,320,384]{2,1,0:T(8,128)(2,1)S(1)}, u32[]{:S(2)}, u32[]{:S(2)}) collective-permute-start(bf16[3,320,384]{2,1,0:T(8,128)(2,1)S(1)} %slice.13), channel_id=1, source_target_pairs={{0,24},{8,16},{16,8},{24,0},{1,25},{9,17},{17,9},{25,1},{2,26},{10... | collective-permute-start | bytes 2211848 | tf_op jit(solution)/shard_map/chunk1/ppermute | solution.py:121
  9.3 63.2 %collective-permute-start = (bf16[1,320,384]{2,1,0:T(8,128)(2,1)}, bf16[1,320,384]{2,1,0:T(8,128)(2,1)}, u32[]{:S(2)}, u32[]{:S(2)}) collective-permute-start(bf16[1,320,384]{2,1,0:T(8,128)(2,1)} %slice.12), channel_id=1, source_target_pairs={{0,24},{8,16},{16,8},{24,0},{1,25},{9,17},{17,9},{25,1},{2,26},{10... | collective-permute-start | bytes 737288 | tf_op jit(solution)/shard_map/chunk2/ppermute | solution.py:121
  50.0 1.3 %copy-start = (bf16[8,320,384]{2,1,0:T(8,128)(2,1)}, bf16[8,320,384]{2,1,0:T(8,128)(2,1)S(1)}, u32[]{:S(2)}) copy-start(bf16[8,320,384]{2,1,0:T(8,128)(2,1)S(1)} %collective-permute-done.2.packed_ref) | copy-start | bytes 5898244
  61.3 10.5 %copy-start.2 = (f32[8,1,384]{2,1,0:T(1,128)S(1)}, f32[8,1,384]{2,1,0:T(1,128)}, u32[]{:S(2)}) copy-start(f32[8,1,384]{2,1,0:T(1,128)} %get-tuple-element.11) | copy-start | bytes 36868
  65.8 0.9 %copy-start.1 = (bf16[3,320,384]{2,1,0:T(8,128)(2,1)}, bf16[3,320,384]{2,1,0:T(8,128)(2,1)S(1)}, u32[]{:S(2)}) copy-start(bf16[3,320,384]{2,1,0:T(8,128)(2,1)S(1)} %collective-permute-done.1.packed_ref) | copy-start | bytes 2211844
  76.4 1.2 %collective-permute-start.3 = (f32[12,1,384]{2,1,0:T(1,128)S(1)}, f32[12,1,384]{2,1,0:T(1,128)S(1)}, u32[]{:S(2)}, u32[]{:S(2)}) collective-permute-start(f32[12,1,384]{2,1,0:T(1,128)S(1)} %constant_dynamic-update-slice_fusion), channel_id=1, source_target_pairs={{0,1},{1,0},{2,3},{3,2},{4,5},{5,4},{6,7},{7,6},{8,9},{9,8},{10,11... | collective-permute-start | bytes 55304 | tf_op jit(solution)/shard_map/ppermute | solution.py:106

commit v2 on v1

v2 whole, which is shorter than its diff:
```python
import functools
import math

import jax
import jax.numpy as jnp
from jax import lax
from jax.experimental import pallas as pl
from jax.experimental.pallas import tpu as pltpu
from jax.sharding import PartitionSpec as P

MASKED = -1e30
KERNEL_VMEM = 16 * 1024 * 1024


def doc_starts(lengths_ref, row_count):
    query_at = lax.broadcasted_iota(jnp.int32, (1, row_count), 1)
    doc_start = jnp.zeros((1, row_count), jnp.int32)
    doc_end = jnp.int32(0)
    for doc in range(lengths_ref.shape[0]):
        doc_end = doc_end + lengths_ref[doc]
        doc_start = jnp.where(query_at >= doc_end, doc_end, doc_start)
    return doc_start


def head_grads(packed, grad_rows, doc_start):
    row_count, pack_width = packed.shape
    head_size = pack_width // 3
    inv_root = 1.0 / math.sqrt(head_size)
    query_at = lax.broadcasted_iota(jnp.int32, (1, row_count), 1)
    key_at = lax.broadcasted_iota(jnp.int32, (row_count, row_count), 0)
    allowed = (key_at >= doc_start) & (key_at <= query_at)
    queries = packed[:, :head_size]
    keys_in = packed[:, head_size : 2 * head_size]
    values_in = packed[:, 2 * head_size :]
    rows_by_rows = (((1,), (1,)), ((), ()))
    plain = (((1,), (0,)), ((), ()))
    columns = (((0,), (0,)), ((), ()))
    dot = functools.partial(lax.dot_general, preferred_element_type=jnp.float32)

    scores = dot(keys_in, queries, rows_by_rows) * inv_root
    masked = jnp.where(allowed, scores, MASKED)
    raised = jnp.exp(masked - jnp.max(masked, axis=0, keepdims=True))
    prob = raised * (1.0 / jnp.sum(raised, axis=0, keepdims=True))
    prob_low = prob.astype(jnp.bfloat16)
    prob_grad = dot(values_in, grad_rows, rows_by_rows)
    row_dot = jnp.sum(prob_low.astype(jnp.float32) * prob_grad, axis=0, keepdims=True)
    score_low = (prob * (prob_grad - row_dot) * inv_root).astype(jnp.bfloat16)
    return (
        dot(score_low, keys_in, columns),
        dot(score_low, queries, plain),
        dot(prob_low, grad_rows, plain),
    )


def write_head(grads, out_ref, out_head, bias_ref, bias_head):
    for part, grad in enumerate(grads):
        head_size = grad.shape[1]
        span = slice(part * head_size, (part + 1) * head_size)
        out_ref[out_head, :, span] = grad.astype(jnp.bfloat16)
        bias_ref[bias_head, :, span] = jnp.sum(grad, axis=0, keepdims=True)


def chunk_kernel(lengths_ref, packed_ref, grad_ref, *refs, first_head):
    out_ref, bias_ref = refs[-2:]
    row_count, pack_width = packed_ref.shape[1:]
    head_size = pack_width // 3
    head = pl.program_id(0)
    grad_at = pl.multiple_of((first_head + head) * head_size, head_size)
    grads = head_grads(
        packed_ref[head], grad_ref[:, pl.ds(grad_at, head_size)], doc_starts(lengths_ref, row_count)
    )
    write_head(grads, out_ref, 0, bias_ref, head)


def last_kernel(lengths_ref, packed_ref, grad_ref, *refs):
    bias_parts, (out_ref, bias_ref) = refs[:-2], refs[-2:]
    row_count, pack_width = packed_ref.shape[1:]
    head_size = pack_width // 3
    head_at = 0
    for part_ref in bias_parts:
        bias_ref[head_at : head_at + part_ref.shape[0]] = part_ref[...]
        head_at += part_ref.shape[0]
    grads = head_grads(
        packed_ref[0],
        grad_ref[:, head_at * head_size : (head_at + 1) * head_size],
        doc_starts(lengths_ref, row_count),
    )
    write_head(grads, out_ref, 0, bias_ref, head_at)


def store_kernel(head_ref, _, out_ref, semaphore):
    at = out_ref.shape[0] - head_ref.shape[0]
    copy = pltpu.make_async_copy(head_ref, out_ref.at[pl.ds(at, head_ref.shape[0])], semaphore)
    copy.start()
    copy.wait()


def in_vmem(array):
    return pltpu.with_memory_space_constraint(array, pltpu.VMEM)


VMEM_SPEC = pl.BlockSpec(memory_space=pltpu.VMEM)
SMEM_SPEC = pl.BlockSpec(memory_space=pltpu.SMEM)
ANY_SPEC = pl.BlockSpec(memory_space=pl.ANY)


def chunk_grads(packed, grad_rows, lengths, head_count, first_head, previous):
    chunk_heads, row_count, pack_width = packed.shape
    in_specs = [SMEM_SPEC, VMEM_SPEC, VMEM_SPEC]
    operands = [lengths, in_vmem(packed), in_vmem(grad_rows)]
    aliases = {}
    if previous is not None:
        in_specs.append(ANY_SPEC)
        operands.append(previous)
        aliases = {3: 0}
    return pl.pallas_call(
        functools.partial(chunk_kernel, first_head=first_head),
        grid=(chunk_heads,),
        in_specs=in_specs,
        out_specs=[
            pl.BlockSpec((1, row_count, pack_width), lambda h: (first_head + h, 0, 0)),
            VMEM_SPEC,
        ],
        out_shape=[
            jax.ShapeDtypeStruct((head_count, row_count, pack_width), jnp.bfloat16),
            pltpu.VMEM((chunk_heads, 1, pack_width), jnp.float32),
        ],
        input_output_aliases=aliases,
        compiler_params=pltpu.CompilerParams(vmem_limit_bytes=KERNEL_VMEM),
    )(*operands)


def last_grads(packed, grad_rows, lengths, bias_parts):
    _, row_count, pack_width = packed.shape
    head_count = 1 + sum(part.shape[0] for part in bias_parts)
    return pl.pallas_call(
        last_kernel,
        in_specs=[SMEM_SPEC] + [VMEM_SPEC] * (2 + len(bias_parts)),
        out_specs=[VMEM_SPEC, VMEM_SPEC],
        out_shape=[
            pltpu.VMEM((1, row_count, pack_width), jnp.bfloat16),
            pltpu.VMEM((head_count, 1, pack_width), jnp.float32),
        ],
        compiler_params=pltpu.CompilerParams(vmem_limit_bytes=KERNEL_VMEM),
        name="last_grads",
    )(lengths, in_vmem(packed), in_vmem(grad_rows), *[in_vmem(part) for part in bias_parts])


def store_last(head, grads):
    return pl.pallas_call(
        store_kernel,
        in_specs=[VMEM_SPEC, ANY_SPEC],
        out_specs=ANY_SPEC,
        out_shape=jax.ShapeDtypeStruct(grads.shape, grads.dtype),
        scratch_shapes=[pltpu.SemaphoreType.DMA],
        input_output_aliases={1: 0},
        compiler_params=pltpu.CompilerParams(vmem_limit_bytes=KERNEL_VMEM),
        name="store_last",
    )(in_vmem(head), grads)


def chunk_sizes(head_count):
    tail = [2, 1, 1]
    if head_count < sum(tail) + 2:
        return [1] * head_count
    return [1, head_count - sum(tail) - 1] + tail


def replica_sum(value, axis):
    count = lax.axis_size(axis)
    if count & (count - 1):
        return lax.psum(value, axis)
    stride = 1
    while stride < count:
        value = value + lax.ppermute(value, axis, [(i, i ^ stride) for i in range(count)])
        stride *= 2
    return value


def body(stash, grad_out, doc_lengths):
    by_head = jnp.transpose(stash[0, 0], (1, 0, 2))
    head_count = by_head.shape[0]
    section_count = lax.axis_size("section")
    mirror = [(i, section_count - 1 - i) for i in range(section_count)]
    sizes = chunk_sizes(head_count)
    firsts = [sum(sizes[:i]) for i in range(len(sizes))]
    arrived = []
    for first, size in zip(firsts, sizes):
        piece, by_head = lax.optimization_barrier((by_head[first : first + size], by_head))
        arrived.append(lax.ppermute(piece, "section", mirror))
    grad_rows, lengths = grad_out[0, 0], doc_lengths[0, 0]
    grads, bias_parts = None, []
    for first, packed in zip(firsts[:-1], arrived):
        grads, bias = chunk_grads(packed, grad_rows, lengths, head_count, first, grads)
        bias_parts.append(bias)
    last, bias_own = last_grads(arrived[-1], grad_rows, lengths, bias_parts)
    bias_total = replica_sum(bias_own, "dp")
    grads = store_last(last, grads)
    bias_grad = jnp.transpose(bias_total / lax.axis_size("dp"), (1, 0, 2))
    return (jnp.transpose(grads, (1, 0, 2))[None, None], bias_grad)


def solution(mesh):
    in_specs = (
        P("section", "dp", None, "tp", None),
        P("section", "dp", None, "tp"),
        P("section", "dp", None),
    )
    out_specs = (P("section", "dp", None, "tp", None), P("section", "tp", None))
    return jax.shard_map(body, mesh=mesh, in_specs=in_specs, out_specs=out_specs, check_vma=False)
```

time: 78.8 us -> 79.4 us (level)
  starting transfers between devices: 6.98 us -> 10.1 us
  local copies, waits for them, and re-layouts: 8.21 us -> 5.72 us
  waiting for transfers between devices: 43.5 us -> 45.6 us
  Pallas kernels: 18.3 us -> 16.4 us
    ppermute x3 -> x5, starting transfers between devices: 6.98 us -> 10 us  [body(): arrived.append(lax.ppermute(piece, 'section', mirror))]
    unnamed x8 -> x4, local copies, waits for them, and re-layouts: 2.88 us -> 0.01 us
    ppermute x3 -> x5, waiting for transfers between devices: 42.3 us -> 45.1 us  [body(): arrived.append(lax.ppermute(piece, 'section', mirror))]
    pallas_call x3 -> x6, Pallas kernels: 18.3 us -> 16.4 us  [the longest x4 14.3 us: chunk_grads(): pl.pallas_call(functools.partial(chunk_kernel, first_head=first_head), gr...]
    slice x3 -> x5, local copies, waits for them, and re-layouts: 4.64 us -> 5.71 us  [body(): by_head[first:first + size]]
  transfers between devices with their start and end apart: 4 -> 6, of which waited for: 3 -> 2; matrix products, arithmetic and copies ran while one was open for 5% -> 4% of each run, Pallas kernels for 19% -> 19%
where the time goes in v2:
time: 79.4 us; the launch traced here: 79.2 us
  waiting for transfers between devices  45.6 us (57%)
  Pallas kernels  16.4 us (21%)
  starting transfers between devices  10.1 us (13%)
  local copies, waits for them, and re-layouts  5.72 us (7%)
    ppermute x5, waiting for transfers between devices, body(): arrived.append(lax.ppermute(piece, 'section', mirror))  45.1 us
    pallas_call x4, Pallas kernels, chunk_grads(): pl.pallas_call(functools.partial(chunk_kernel, first_head=first_head), gr...  14.3 us
    ppermute x5, starting transfers between devices, body(): arrived.append(lax.ppermute(piece, 'section', mirror))  10 us
    slice x5, local copies, waits for them, and re-layouts, body(): by_head[first:first + size]  5.71 us
  transfers between devices with their start and end apart: 6, of which 2 were waited for; matrix products, arithmetic and copies ran while one was open for 4% of the time, Pallas kernels for 19%

profile of v2, /device:TPU:0, one launch (start us, length us, event | category | flops | bytes accessed | tf_op | source)
XLA Modules:
  0.0 79.2 jit_solution(241079149757615451)
XLA Ops:
  0.6 0.0 copy-start
  0.6 0.0 copy-start.1
  0.6 1.1 %slice.20 = bf16[1,320,384]{2,1,0:T(8,128)(2,1)S(1)} slice(bf16[12,320,384]{2,1,0:T(8,128)(2,1)} %bitcast.21), slice={[0:1], [0:320], [0:384]} | slice | bytes 491520 | tf_op jit(solution)/shard_map/slice | solution.py:189
  1.7 1.6 %slice.16 = bf16[7,320,384]{2,1,0:T(8,128)(2,1)S(1)} slice(bf16[12,320,384]{2,1,0:T(8,128)(2,1)} %bitcast.22), slice={[1:8], [0:320], [0:384]} | slice | bytes 3440640 | tf_op jit(solution)/shard_map/slice | solution.py:189
  3.3 4.0 %collective-permute-start.2 = (bf16[7,320,384]{2,1,0:T(8,128)(2,1)S(1)}, bf16[7,320,384]{2,1,0:T(8,128)(2,1)S(1)}, u32[]{:S(2)}, u32[]{:S(2)}) collective-permute-start(bf16[7,320,384]{2,1,0:T(8,128)(2,1)S(1)} %slice.16), channel_id=1, source_target_pairs={{0,24},{8,16},{16,8},{24,0},{1,25},{9,17},{17,9},{25,1},{2,26},{10... | collective-permute-start | bytes 5160968 | tf_op jit(solution)/shard_map/ppermute | solution.py:190
  7.3 1.1 %slice.17 = bf16[2,320,384]{2,1,0:T(8,128)(2,1)S(1)} slice(bf16[12,320,384]{2,1,0:T(8,128)(2,1)} %bitcast.23), slice={[8:10], [0:320], [0:384]} | slice | bytes 983040 | tf_op jit(solution)/shard_map/slice | solution.py:189
  8.4 0.1 collective-permute-start.3
  8.5 2.9 %collective-permute-start.1 = (bf16[1,320,384]{2,1,0:T(8,128)(2,1)S(1)}, bf16[1,320,384]{2,1,0:T(8,128)(2,1)S(1)}, u32[]{:S(2)}, u32[]{:S(2)}) collective-permute-start(bf16[1,320,384]{2,1,0:T(8,128)(2,1)S(1)} %slice.20), channel_id=1, source_target_pairs={{0,24},{8,16},{16,8},{24,0},{1,25},{9,17},{17,9},{25,1},{2,26},{10... | collective-permute-start | bytes 737288 | tf_op jit(solution)/shard_map/ppermute | solution.py:190
  11.4 1.0 %slice.18 = bf16[1,320,384]{2,1,0:T(8,128)(2,1)S(1)} slice(bf16[12,320,384]{2,1,0:T(8,128)(2,1)} %bitcast.24), slice={[10:11], [0:320], [0:384]} | slice | bytes 491520 | tf_op jit(solution)/shard_map/slice | solution.py:189
  12.4 0.1 collective-permute-start.4
  12.5 1.0 %slice.19 = bf16[1,320,384]{2,1,0:T(8,128)(2,1)S(1)} slice(bf16[12,320,384]{2,1,0:T(8,128)(2,1)} %bitcast.25), slice={[11:12], [0:320], [0:384]} | slice | bytes 491520 | tf_op jit(solution)/shard_map/slice | solution.py:189
  13.5 2.9 %collective-permute-start = (bf16[1,320,384]{2,1,0:T(8,128)(2,1)S(1)}, bf16[1,320,384]{2,1,0:T(8,128)(2,1)S(1)}, u32[]{:S(2)}, u32[]{:S(2)}) collective-permute-start(bf16[1,320,384]{2,1,0:T(8,128)(2,1)S(1)} %slice.19), channel_id=1, source_target_pairs={{0,24},{8,16},{16,8},{24,0},{1,25},{9,17},{17,9},{25,1},{2,26},{10... | collective-permute-start | bytes 737288 | tf_op jit(solution)/shard_map/ppermute | solution.py:190
  16.4 45.1 %collective-permute-done.1.packed_ref = bf16[1,320,384]{2,1,0:T(8,128)(2,1)S(1)} collective-permute-done((bf16[1,320,384]{2,1,0:T(8,128)(2,1)S(1)}, bf16[1,320,384]{2,1,0:T(8,128)(2,1)S(1)}, u32[]{:S(2)}, u32[]{:S(2)}) %collective-permute-start.1) | collective-permute-done | bytes 245792 | tf_op jit(solution)/shard_map/ppermute | solution.py:190
  61.5 0.0 copy-done
  61.5 0.0 copy-done.1
  61.5 2.1 %shard_map.50 = (bf16[12,320,384]{2,1,0:T(8,128)(2,1)}, f32[1,1,384]{2,1,0:T(1,128)S(1)}) custom-call(s32[8]{0:T(128)S(1)} %bitcast.15, bf16[1,320,384]{2,1,0:T(8,128)(2,1)S(1)} %collective-permute-done.1.packed_ref, bf16[320,1536]{1,0:T(8,128)(2,1)S(1)} %bitcast.10), custom_call_target="tpu_custom_call" | custom-call | tf_op jit(solution)/shard_map/pallas_call | solution.py:116
  63.6 0.0 collective-permute-done.2.packed_ref
  63.6 7.3 %shard_map.51 = (bf16[12,320,384]{2,1,0:T(8,128)(2,1)}, f32[7,1,384]{2,1,0:T(1,128)S(1)}) custom-call(s32[8]{0:T(128)S(1)} %bitcast.16, bf16[7,320,384]{2,1,0:T(8,128)(2,1)S(1)} %collective-permute-done.2.packed_ref, bf16[320,1536]{1,0:T(8,128)(2,1)S(1)} %bitcast.11, bf16[12,320,384]{2,1,0:T(8,128)(2,1)} %get-tuple-element.29.refs_0_), custom_call_target="tpu_custom_call", output_to_operand_aliasing={{0}: (3, {})} | custom-call | tf_op jit(solution)/shard_map/pallas_call | solution.py:116
  70.9 0.0 collective-permute-done.3.packed_ref
  70.9 2.9 %shard_map.52 = (bf16[12,320,384]{2,1,0:T(8,128)(2,1)}, f32[2,1,384]{2,1,0:T(1,128)S(1)}) custom-call(s32[8]{0:T(128)S(1)} %bitcast.17, bf16[2,320,384]{2,1,0:T(8,128)(2,1)S(1)} %collective-permute-done.3.packed_ref, bf16[320,1536]{1,0:T(8,128)(2,1)S(1)} %bitcast.12, bf16[12,320,384]{2,1,0:T(8,128)(2,1)} %get-tuple-element.32.refs_0_), custom_call_target="tpu_custom_call", output_to_operand_aliasing={{0}: (3, {})} | custom-call | tf_op jit(solution)/shard_map/pallas_call | solution.py:116
  73.8 0.0 collective-permute-done.4.packed_ref
  73.8 2.1 %shard_map.53 = (bf16[12,320,384]{2,1,0:T(8,128)(2,1)}, f32[1,1,384]{2,1,0:T(1,128)S(1)}) custom-call(s32[8]{0:T(128)S(1)} %bitcast.18, bf16[1,320,384]{2,1,0:T(8,128)(2,1)S(1)} %collective-permute-done.4.packed_ref, bf16[320,1536]{1,0:T(8,128)(2,1)S(1)} %bitcast.13, bf16[12,320,384]{2,1,0:T(8,128)(2,1)} %get-tuple-element.35.refs_0_), custom_call_target="tpu_custom_call", output_to_operand_aliasing={{0}: (3, {})} | custom-call | tf_op jit(solution)/shard_map/pallas_call | solution.py:116
  75.9 0.0 collective-permute-done.packed_ref
  75.9 1.4 %last_grads.1 = (bf16[1,320,384]{2,1,0:T(8,128)(2,1)S(1)}, f32[12,1,384]{2,1,0:T(1,128)S(1)}) custom-call(s32[8]{0:T(128)S(1)} %bitcast.19, bf16[1,320,384]{2,1,0:T(8,128)(2,1)S(1)} %collective-permute-done.packed_ref, bf16[320,1536]{1,0:T(8,128)(2,1)S(1)} %bitcast.14, f32[1,1,384]{2,1,0:T(1,128)S(1)} %get-tuple-element.27.refs_0_, ...), custom_call_target="tpu_custom_call" | custom-call | tf_op jit(solution)/shard_map/last_grads/pallas_call | solution.py:136
  77.3 0.1 collective-permute-start.5
  77.4 0.7 store_last.1
  78.1 0.5 collective-permute-done.5
  78.5 0.6 multiply_bitcast_fusion
Async XLA Ops:
  0.6 60.9 %copy-start = (bf16[1,1,320,1536]{3,2,1,0:T(8,128)(2,1)S(1)}, bf16[1,1,320,1536]{3,2,1,0:T(8,128)(2,1)}, u32[]{:S(2)}) copy-start(bf16[1,1,320,1536]{3,2,1,0:T(8,128)(2,1)} %param.4) | copy-start | bytes 2949124
  0.6 60.9 %copy-start.1 = (s32[1,1,8]{2,1,0:T(1,128)S(1)}, s32[1,1,8]{2,1,0:T(1,128)}, u32[]{:S(2)}) copy-start(s32[1,1,8]{2,1,0:T(1,128)} %param.5) | copy-start | bytes 100
  3.3 60.3 %collective-permute-start.2 = (bf16[7,320,384]{2,1,0:T(8,128)(2,1)S(1)}, bf16[7,320,384]{2,1,0:T(8,128)(2,1)S(1)}, u32[]{:S(2)}, u32[]{:S(2)}) collective-permute-start(bf16[7,320,384]{2,1,0:T(8,128)(2,1)S(1)} %slice.16), channel_id=1, source_target_pairs={{0,24},{8,16},{16,8},{24,0},{1,25},{9,17},{17,9},{25,1},{2,26},{10... | collective-permute-start | bytes 5160968 | tf_op jit(solution)/shard_map/ppermute | solution.py:190
  8.4 62.5 %collective-permute-start.3 = (bf16[2,320,384]{2,1,0:T(8,128)(2,1)S(1)}, bf16[2,320,384]{2,1,0:T(8,128)(2,1)S(1)}, u32[]{:S(2)}, u32[]{:S(2)}) collective-permute-start(bf16[2,320,384]{2,1,0:T(8,128)(2,1)S(1)} %slice.17), channel_id=1, source_target_pairs={{0,24},{8,16},{16,8},{24,0},{1,25},{9,17},{17,9},{25,1},{2,26},{10... | collective-permute-start | bytes 1474568 | tf_op jit(solution)/shard_map/ppermute | solution.py:190
  8.5 53.0 %collective-permute-start.1 = (bf16[1,320,384]{2,1,0:T(8,128)(2,1)S(1)}, bf16[1,320,384]{2,1,0:T(8,128)(2,1)S(1)}, u32[]{:S(2)}, u32[]{:S(2)}) collective-permute-start(bf16[1,320,384]{2,1,0:T(8,128)(2,1)S(1)} %slice.20), channel_id=1, source_target_pairs={{0,24},{8,16},{16,8},{24,0},{1,25},{9,17},{17,9},{25,1},{2,26},{10... | collective-permute-start | bytes 737288 | tf_op jit(solution)/shard_map/ppermute | solution.py:190
  12.4 61.5 %collective-permute-start.4 = (bf16[1,320,384]{2,1,0:T(8,128)(2,1)S(1)}, bf16[1,320,384]{2,1,0:T(8,128)(2,1)S(1)}, u32[]{:S(2)}, u32[]{:S(2)}) collective-permute-start(bf16[1,320,384]{2,1,0:T(8,128)(2,1)S(1)} %slice.18), channel_id=1, source_target_pairs={{0,24},{8,16},{16,8},{24,0},{1,25},{9,17},{17,9},{25,1},{2,26},{10... | collective-permute-start | bytes 737288 | tf_op jit(solution)/shard_map/ppermute | solution.py:190
  13.5 62.4 %collective-permute-start = (bf16[1,320,384]{2,1,0:T(8,128)(2,1)S(1)}, bf16[1,320,384]{2,1,0:T(8,128)(2,1)S(1)}, u32[]{:S(2)}, u32[]{:S(2)}) collective-permute-start(bf16[1,320,384]{2,1,0:T(8,128)(2,1)S(1)} %slice.19), channel_id=1, source_target_pairs={{0,24},{8,16},{16,8},{24,0},{1,25},{9,17},{17,9},{25,1},{2,26},{10... | collective-permute-start | bytes 737288 | tf_op jit(solution)/shard_map/ppermute | solution.py:190
  77.3 1.3 %collective-permute-start.5 = (f32[12,1,384]{2,1,0:T(1,128)S(1)}, f32[12,1,384]{2,1,0:T(1,128)S(1)}, u32[]{:S(2)}, u32[]{:S(2)}) collective-permute-start(f32[12,1,384]{2,1,0:T(1,128)S(1)} %get-tuple-element.39), channel_id=1, source_target_pairs={{0,1},{1,0},{2,3},{3,2},{4,5},{5,4},{6,7},{7,6},{8,9},{9,8},{10,11... | collective-permute-start | bytes 55304 | tf_op jit(solution)/shard_map/ppermute | solution.py:175

commit v3 on v2

--- a/solution.py
+++ b/solution.py
@@ -9,6 +9,7 @@
 from jax.sharding import PartitionSpec as P
 
 MASKED = -1e30
+TILE = 128
 KERNEL_VMEM = 16 * 1024 * 1024
 
 
@@ -22,33 +23,45 @@
     return doc_start
 
 
-def head_grads(packed, grad_rows, doc_start):
-    row_count, pack_width = packed.shape
-    head_size = pack_width // 3
-    inv_root = 1.0 / math.sqrt(head_size)
-    query_at = lax.broadcasted_iota(jnp.int32, (1, row_count), 1)
-    key_at = lax.broadcasted_iota(jnp.int32, (row_count, row_count), 0)
+ROWS_BY_ROWS = (((1,), (1,)), ((), ()))
+PLAIN = (((1,), (0,)), ((), ()))
+COLUMNS = (((0,), (0,)), ((), ()))
+dot = functools.partial(lax.dot_general, preferred_element_type=jnp.float32)
+
+
+def split_pack(packed):
+    head_size = packed.shape[1] // 3
+    return (
+        packed[:, :head_size],
+        packed[:, head_size : 2 * head_size],
+        packed[:, 2 * head_size :],
+    )
+
+
+def tile_weights(queries, keys_in, values_in, grad_rows, doc_start, first_query):
+    inv_root = 1.0 / math.sqrt(queries.shape[1])
+    shape = (keys_in.shape[0], queries.shape[0])
+    query_at = first_query + lax.broadcasted_iota(jnp.int32, (1, shape[1]), 1)
+    key_at = lax.broadcasted_iota(jnp.int32, shape, 0)
     allowed = (key_at >= doc_start) & (key_at <= query_at)
-    queries = packed[:, :head_size]
-    keys_in = packed[:, head_size : 2 * head_size]
-    values_in = packed[:, 2 * head_size :]
-    rows_by_rows = (((1,), (1,)), ((), ()))
-    plain = (((1,), (0,)), ((), ()))
-    columns = (((0,), (0,)), ((), ()))
-    dot = functools.partial(lax.dot_general, preferred_element_type=jnp.float32)
-
-    scores = dot(keys_in, queries, rows_by_rows) * inv_root
+    scores = dot(keys_in, queries, ROWS_BY_ROWS) * inv_root
     masked = jnp.where(allowed, scores, MASKED)
     raised = jnp.exp(masked - jnp.max(masked, axis=0, keepdims=True))
     prob = raised * (1.0 / jnp.sum(raised, axis=0, keepdims=True))
     prob_low = prob.astype(jnp.bfloat16)
-    prob_grad = dot(values_in, grad_rows, rows_by_rows)
+    prob_grad = dot(values_in, grad_rows, ROWS_BY_ROWS)
     row_dot = jnp.sum(prob_low.astype(jnp.float32) * prob_grad, axis=0, keepdims=True)
     score_low = (prob * (prob_grad - row_dot) * inv_root).astype(jnp.bfloat16)
+    return prob_low, score_low
+
+
+def head_grads(packed, grad_rows, doc_start):
+    queries, keys_in, values_in = split_pack(packed)
+    prob_low, score_low = tile_weights(queries, keys_in, values_in, grad_rows, doc_start, 0)
     return (
-        dot(score_low, keys_in, columns),
-        dot(score_low, queries, plain),
-        dot(prob_low, grad_rows, plain),
+        dot(score_low, keys_in, COLUMNS),
+        dot(score_low, queries, PLAIN),
+        dot(prob_low, grad_rows, PLAIN),
     )
 
 
@@ -72,20 +85,64 @@
     write_head(grads, out_ref, 0, bias_ref, head)
 
 
-def last_kernel(lengths_ref, packed_ref, grad_ref, *refs):
+def early_kernel(lengths_ref, early_ref, grad_ref, _, query_ref, sums_ref, bias_ref, *, head):
+    row_count, pack_width = early_ref.shape[1:]
+    head_size = pack_width // 3
+    queries, keys_in, values_in = split_pack(early_ref[0])
+    grad_rows = grad_ref[:row_count, head * head_size : (head + 1) * head_size]
+    doc_start = doc_starts(lengths_ref, row_count)
+    tiles = [slice(at, at + TILE) for at in range(0, row_count, TILE)]
+    key_grads, value_grads = [0.0] * len(tiles), [0.0] * len(tiles)
+    bias = jnp.zeros((1, head_size), jnp.float32)
+    for index, tile in enumerate(tiles):
+        seen = slice(0, tile.stop)
+        prob_low, score_low = tile_weights(
+            queries[tile], keys_in[seen], values_in[seen], grad_rows[tile], doc_start[:, tile], tile.start
+        )
+        query_grad = dot(score_low, keys_in[seen], COLUMNS)
+        query_ref[tile] = query_grad.astype(jnp.bfloat16)
+        bias += jnp.sum(query_grad, axis=0, keepdims=True)
+        for past in range(index + 1):
+            key_grads[past] += dot(score_low[tiles[past]], queries[tile], PLAIN)
+            value_grads[past] += dot(prob_low[tiles[past]], grad_rows[tile], PLAIN)
+    bias_ref[...] = bias
+    for index, tile in enumerate(tiles):
+        sums_ref[tile, :head_size] = key_grads[index]
+        sums_ref[tile, head_size:] = value_grads[index]
+
+
+def late_kernel(lengths_ref, early_ref, late_ref, grad_ref, query_ref, sums_ref, early_bias_ref, *refs):
     bias_parts, (out_ref, bias_ref) = refs[:-2], refs[-2:]
-    row_count, pack_width = packed_ref.shape[1:]
-    head_size = pack_width // 3
+    split = early_ref.shape[1]
+    row_count = split + late_ref.shape[1]
+    head_size = early_ref.shape[2] // 3
+    head = sum(part_ref.shape[0] for part_ref in bias_parts)
+    queries = late_ref[0, :, :head_size]
+    grad_rows = grad_ref[split:, head * head_size : (head + 1) * head_size]
+    keys_in, values_in = (
+        jnp.concatenate([ref[0, :, part * head_size : (part + 1) * head_size] for ref in (early_ref, late_ref)], axis=0)
+        for part in (1, 2)
+    )
+    prob_low, score_low = tile_weights(
+        queries, keys_in, values_in, grad_rows, doc_starts(lengths_ref, row_count)[:, split:], split
+    )
+    query_grad = dot(score_low, keys_in, COLUMNS)
+    out_ref[0, :split, :head_size] = query_ref[...]
+    out_ref[0, split:, :head_size] = query_grad.astype(jnp.bfloat16)
+    bias_ref[head, :, :head_size] = early_bias_ref[...] + jnp.sum(query_grad, axis=0, keepdims=True)
+    added = (dot(score_low, queries, PLAIN), dot(prob_low, grad_rows, PLAIN))
+    for part, late in enumerate(added):
+        span = slice((part + 1) * head_size, (part + 2) * head_size)
+        early = sums_ref[:, part * head_size : (part + 1) * head_size] + late[:split]
+        out_ref[0, :split, span] = early.astype(jnp.bfloat16)
+        out_ref[0, split:, span] = late[split:].astype(jnp.bfloat16)
+        bias_ref[head, :, span] = jnp.sum(early, axis=0, keepdims=True) + jnp.sum(
+            late[split:], axis=0, keepdims=True
+        )
     head_at = 0
     for part_ref in bias_parts:
         bias_ref[head_at : head_at + part_ref.shape[0]] = part_ref[...]
         head_at += part_ref.shape[0]
-    grads = head_grads(
-        packed_ref[0],
-        grad_ref[:, head_at * head_size : (head_at + 1) * head_size],
-        doc_starts(lengths_ref, row_count),
-    )
-    write_head(grads, out_ref, 0, bias_ref, head_at)
 
 
 def store_kernel(head_ref, _, out_ref, semaphore):
@@ -130,20 +187,38 @@
     )(*operands)
 
 
-def last_grads(packed, grad_rows, lengths, bias_parts):
+def early_grads(packed, grad_rows, lengths, head, after):
     _, row_count, pack_width = packed.shape
+    head_size = pack_width // 3
+    return pl.pallas_call(
+        functools.partial(early_kernel, head=head),
+        in_specs=[SMEM_SPEC] + [VMEM_SPEC] * 3,
+        out_specs=[VMEM_SPEC] * 3,
+        out_shape=[
+            pltpu.VMEM((row_count, head_size), jnp.bfloat16),
+            pltpu.VMEM((row_count, 2 * head_size), jnp.float32),
+            pltpu.VMEM((1, head_size), jnp.float32),
+        ],
+        compiler_params=pltpu.CompilerParams(vmem_limit_bytes=KERNEL_VMEM),
+        name="early_grads",
+    )(lengths, in_vmem(packed), in_vmem(grad_rows), in_vmem(after))
+
+
+def late_grads(early, late, grad_rows, lengths, started, bias_parts):
     head_count = 1 + sum(part.shape[0] for part in bias_parts)
-    return pl.pallas_call(
-        last_kernel,
-        in_specs=[SMEM_SPEC] + [VMEM_SPEC] * (2 + len(bias_parts)),
+    row_count, pack_width = grad_rows.shape[0], early.shape[2]
+    operands = [early, late, grad_rows, *started, *bias_parts]
+    return pl.pallas_call(
+        late_kernel,
+        in_specs=[SMEM_SPEC] + [VMEM_SPEC] * len(operands),
         out_specs=[VMEM_SPEC, VMEM_SPEC],
         out_shape=[
             pltpu.VMEM((1, row_count, pack_width), jnp.bfloat16),
             pltpu.VMEM((head_count, 1, pack_width), jnp.float32),
         ],
         compiler_params=pltpu.CompilerParams(vmem_limit_bytes=KERNEL_VMEM),
-        name="last_grads",
-    )(lengths, in_vmem(packed), in_vmem(grad_rows), *[in_vmem(part) for part in bias_parts])
+        name="late_grads",
+    )(lengths, *[in_vmem(operand) for operand in operands])
 
 
 def store_last(head, grads):
@@ -160,7 +235,7 @@
 
 
 def chunk_sizes(head_count):
-    tail = [2, 1, 1]
+    tail = [2, 1]
     if head_count < sum(tail) + 2:
         return [1] * head_count
     return [1, head_count - sum(tail) - 1] + tail
@@ -182,20 +257,27 @@
     head_count = by_head.shape[0]
     section_count = lax.axis_size("section")
     mirror = [(i, section_count - 1 - i) for i in range(section_count)]
-    sizes = chunk_sizes(head_count)
+    row_count = by_head.shape[1]
+    split = (row_count - 1) // TILE * TILE
+    last = head_count - 1
+    sizes = chunk_sizes(last)
     firsts = [sum(sizes[:i]) for i in range(len(sizes))]
+    pieces = [(slice(first, first + size), slice(None)) for first, size in zip(firsts, sizes)]
+    pieces += [(slice(last, None), slice(0, split)), (slice(last, None), slice(split, None))]
+    grad_rows, lengths = grad_out[0, 0], doc_lengths[0, 0]
     arrived = []
-    for first, size in zip(firsts, sizes):
-        piece, by_head = lax.optimization_barrier((by_head[first : first + size], by_head))
-        arrived.append(lax.ppermute(piece, "section", mirror))
-    grad_rows, lengths = grad_out[0, 0], doc_lengths[0, 0]
+    for piece in pieces:
+        packed, by_head = lax.optimization_barrier((by_head[piece], by_head))
+        arrived.append(lax.ppermute(packed, "section", mirror))
     grads, bias_parts = None, []
-    for first, packed in zip(firsts[:-1], arrived):
+    for first, packed in zip(firsts, arrived):
         grads, bias = chunk_grads(packed, grad_rows, lengths, head_count, first, grads)
         bias_parts.append(bias)
-    last, bias_own = last_grads(arrived[-1], grad_rows, lengths, bias_parts)
+    early, late = arrived[-2:]
+    started = early_grads(early, grad_rows, lengths, last, bias_parts[-1])
+    final, bias_own = late_grads(early, late, grad_rows, lengths, started, bias_parts)
     bias_total = replica_sum(bias_own, "dp")
-    grads = store_last(last, grads)
+    grads = store_last(final, grads)
     bias_grad = jnp.transpose(bias_total / lax.axis_size("dp"), (1, 0, 2))
     return (jnp.transpose(grads, (1, 0, 2))[None, None], bias_grad)
 

time: 79.4 us -> 83.5 us (1.052)
  starting transfers between devices: 10.1 us -> 13 us
  Pallas kernels: 16.4 us -> 17.5 us
    ppermute x5 -> x6, starting transfers between devices: 10 us -> 13 us  [body(): arrived.append(lax.ppermute(packed, 'section', mirror))]
    pallas_call x1 -> x2, Pallas kernels: 1.39 us -> 2.43 us  [the longest x1 1.3 us: early_grads(): pl.pallas_call(functools.partial(early_kernel, head=head), in_specs=[SMEM...]
    slice x5 -> x6, local copies, waits for them, and re-layouts: 5.71 us -> 6.49 us  [body(): packed, by_head = lax.optimization_barrier((by_head[piece], by_head))]
    ppermute x5 -> x6, waiting for transfers between devices: 45.1 us -> 44.4 us  [body(): arrived.append(lax.ppermute(packed, 'section', mirror))]
  transfers between devices with their start and end apart: 6 -> 7, of which waited for: 2 -> 2; matrix products, arithmetic and copies ran while one was open for 4% -> 5% of each run, Pallas kernels for 19% -> 20%
where the time goes in v3:
time: 83.5 us; the launch traced here: 83.1 us
  waiting for transfers between devices  44.8 us (54%)
  Pallas kernels  17.5 us (21%)
  starting transfers between devices  13 us (16%)
  local copies, waits for them, and re-layouts  6.5 us (8%)
    ppermute x6, waiting for transfers between devices, body(): arrived.append(lax.ppermute(packed, 'section', mirror))  44.4 us
    pallas_call x4, Pallas kernels, chunk_grads(): pl.pallas_call(functools.partial(chunk_kernel, first_head=first_head), gr...  14.3 us
    ppermute x6, starting transfers between devices, body(): arrived.append(lax.ppermute(packed, 'section', mirror))  13 us
    slice x6, local copies, waits for them, and re-layouts, body(): packed, by_head = lax.optimization_barrier((by_head[piece], by_head))  6.49 us
  transfers between devices with their start and end apart: 7, of which 2 were waited for; matrix products, arithmetic and copies ran while one was open for 5% of the time, Pallas kernels for 20%

profile of v3, /device:TPU:0, one launch (start us, length us, event | category | flops | bytes accessed | tf_op | source)
XLA Modules:
  0.0 83.1 jit_solution(8477931751979454573)
XLA Ops:
  0.6 0.0 copy-start
  0.6 0.0 copy-start.1
  0.6 1.1 %slice.24 = bf16[1,320,384]{2,1,0:T(8,128)(2,1)S(1)} slice(bf16[12,320,384]{2,1,0:T(8,128)(2,1)} %bitcast.23), slice={[0:1], [0:320], [0:384]} | slice | bytes 491520 | tf_op jit(solution)/shard_map/slice | solution.py:270
  1.7 1.6 %slice.19 = bf16[7,320,384]{2,1,0:T(8,128)(2,1)S(1)} slice(bf16[12,320,384]{2,1,0:T(8,128)(2,1)} %bitcast.24), slice={[1:8], [0:320], [0:384]} | slice | bytes 3440640 | tf_op jit(solution)/shard_map/slice | solution.py:270
  3.3 4.0 %collective-permute-start.4 = (bf16[7,320,384]{2,1,0:T(8,128)(2,1)S(1)}, bf16[7,320,384]{2,1,0:T(8,128)(2,1)S(1)}, u32[]{:S(2)}, u32[]{:S(2)}) collective-permute-start(bf16[7,320,384]{2,1,0:T(8,128)(2,1)S(1)} %slice.19), channel_id=1, source_target_pairs={{0,24},{8,16},{16,8},{24,0},{1,25},{9,17},{17,9},{25,1},{2,26},{10... | collective-permute-start | bytes 5160968 | tf_op jit(solution)/shard_map/ppermute | solution.py:271
  7.3 1.1 %slice.20 = bf16[2,320,384]{2,1,0:T(8,128)(2,1)S(1)} slice(bf16[12,320,384]{2,1,0:T(8,128)(2,1)} %bitcast.25), slice={[8:10], [0:320], [0:384]} | slice | bytes 983040 | tf_op jit(solution)/shard_map/slice | solution.py:270
  8.4 0.1 collective-permute-start.3
  8.5 2.9 %collective-permute-start.5 = (bf16[1,320,384]{2,1,0:T(8,128)(2,1)S(1)}, bf16[1,320,384]{2,1,0:T(8,128)(2,1)S(1)}, u32[]{:S(2)}, u32[]{:S(2)}) collective-permute-start(bf16[1,320,384]{2,1,0:T(8,128)(2,1)S(1)} %slice.24), channel_id=1, source_target_pairs={{0,24},{8,16},{16,8},{24,0},{1,25},{9,17},{17,9},{25,1},{2,26},{10... | collective-permute-start | bytes 737288 | tf_op jit(solution)/shard_map/ppermute | solution.py:271
  11.4 1.0 %slice.21 = bf16[1,320,384]{2,1,0:T(8,128)(2,1)S(1)} slice(bf16[12,320,384]{2,1,0:T(8,128)(2,1)} %bitcast.26), slice={[10:11], [0:320], [0:384]} | slice | bytes 491520 | tf_op jit(solution)/shard_map/slice | solution.py:270
  12.4 0.1 collective-permute-start.2
  12.5 0.9 %slice.22 = bf16[1,256,384]{2,1,0:T(8,128)(2,1)S(1)} slice(bf16[12,320,384]{2,1,0:T(8,128)(2,1)} %bitcast.27), slice={[11:12], [0:256], [0:384]} | slice | bytes 393216 | tf_op jit(solution)/shard_map/slice | solution.py:270
  13.5 2.9 %collective-permute-start = (bf16[1,256,384]{2,1,0:T(8,128)(2,1)S(1)}, bf16[1,256,384]{2,1,0:T(8,128)(2,1)S(1)}, u32[]{:S(2)}, u32[]{:S(2)}) collective-permute-start(bf16[1,256,384]{2,1,0:T(8,128)(2,1)S(1)} %slice.22), channel_id=1, source_target_pairs={{0,24},{8,16},{16,8},{24,0},{1,25},{9,17},{17,9},{25,1},{2,26},{10... | collective-permute-start | bytes 589832 | tf_op jit(solution)/shard_map/ppermute | solution.py:271
  16.4 0.8 slice.23
  17.2 44.3 %collective-permute-done.5.packed_ref = bf16[1,320,384]{2,1,0:T(8,128)(2,1)S(1)} collective-permute-done((bf16[1,320,384]{2,1,0:T(8,128)(2,1)S(1)}, bf16[1,320,384]{2,1,0:T(8,128)(2,1)S(1)}, u32[]{:S(2)}, u32[]{:S(2)}) %collective-permute-start.5) | collective-permute-done | bytes 245792 | tf_op jit(solution)/shard_map/ppermute | solution.py:271
  61.5 2.9 %collective-permute-start.1 = (bf16[1,64,384]{2,1,0:T(8,128)(2,1)S(1)}, bf16[1,64,384]{2,1,0:T(8,128)(2,1)S(1)}, u32[]{:S(2)}, u32[]{:S(2)}) collective-permute-start(bf16[1,64,384]{2,1,0:T(8,128)(2,1)S(1)} %slice.23), channel_id=1, source_target_pairs={{0,24},{8,16},{16,8},{24,0},{1,25},{9,17},{17,9},{25,1},{2,26},{10... | collective-permute-start | bytes 147464 | tf_op jit(solution)/shard_map/ppermute | solution.py:271
  64.5 0.0 copy-done
  64.5 0.0 copy-done.1
  64.5 2.1 %shard_map.50 = (bf16[12,320,384]{2,1,0:T(8,128)(2,1)}, f32[1,1,384]{2,1,0:T(1,128)S(1)}) custom-call(s32[8]{0:T(128)S(1)} %bitcast.16, bf16[1,320,384]{2,1,0:T(8,128)(2,1)S(1)} %collective-permute-done.5.packed_ref, bf16[320,1536]{1,0:T(8,128)(2,1)S(1)} %bitcast.10), custom_call_target="tpu_custom_call" | custom-call | tf_op jit(solution)/shard_map/pallas_call | solution.py:173
  66.5 0.0 collective-permute-done.4.packed_ref
  66.5 7.3 %shard_map.51 = (bf16[12,320,384]{2,1,0:T(8,128)(2,1)}, f32[7,1,384]{2,1,0:T(1,128)S(1)}) custom-call(s32[8]{0:T(128)S(1)} %bitcast.17, bf16[7,320,384]{2,1,0:T(8,128)(2,1)S(1)} %collective-permute-done.4.packed_ref, bf16[320,1536]{1,0:T(8,128)(2,1)S(1)} %bitcast.11, bf16[12,320,384]{2,1,0:T(8,128)(2,1)} %get-tuple-element.37.refs_0_), custom_call_target="tpu_custom_call", output_to_operand_aliasing={{0}: (3, {})} | custom-call | tf_op jit(solution)/shard_map/pallas_call | solution.py:173
  73.8 0.0 collective-permute-done.3.packed_ref
  73.8 2.9 %shard_map.52 = (bf16[12,320,384]{2,1,0:T(8,128)(2,1)}, f32[2,1,384]{2,1,0:T(1,128)S(1)}) custom-call(s32[8]{0:T(128)S(1)} %bitcast.18, bf16[2,320,384]{2,1,0:T(8,128)(2,1)S(1)} %collective-permute-done.3.packed_ref, bf16[320,1536]{1,0:T(8,128)(2,1)S(1)} %bitcast.12, bf16[12,320,384]{2,1,0:T(8,128)(2,1)} %get-tuple-element.38.refs_0_), custom_call_target="tpu_custom_call", output_to_operand_aliasing={{0}: (3, {})} | custom-call | tf_op jit(solution)/shard_map/pallas_call | solution.py:173
  76.7 0.0 collective-permute-done.2.packed_ref
  76.7 2.1 %shard_map.53 = (bf16[12,320,384]{2,1,0:T(8,128)(2,1)}, f32[1,1,384]{2,1,0:T(1,128)S(1)}) custom-call(s32[8]{0:T(128)S(1)} %bitcast.19, bf16[1,320,384]{2,1,0:T(8,128)(2,1)S(1)} %collective-permute-done.2.packed_ref, bf16[320,1536]{1,0:T(8,128)(2,1)S(1)} %bitcast.13, bf16[12,320,384]{2,1,0:T(8,128)(2,1)} %get-tuple-element.39.refs_0_), custom_call_target="tpu_custom_call", output_to_operand_aliasing={{0}: (3, {})} | custom-call | tf_op jit(solution)/shard_map/pallas_call | solution.py:173
  78.8 0.0 collective-permute-done.early_ref
  78.8 1.3 %early_grads.1 = (bf16[256,128]{1,0:T(8,128)(2,1)S(1)}, f32[256,256]{1,0:T(8,128)S(1)}, f32[1,128]{1,0:T(1,128)S(1)}) custom-call(s32[8]{0:T(128)S(1)} %bitcast.20, bf16[1,256,384]{2,1,0:T(8,128)(2,1)S(1)} %collective-permute-done.early_ref, bf16[320,1536]{1,0:T(8,128)(2,1)S(1)} %bitcast.14, f32[1,1,384]{2,1,0:T(1,128)S(1)} %get-tuple-element.40._.refs_3_), custom_call_target="tpu_custom_call" | custom-call | tf_op jit(solution)/shard_map/early_grads/pallas_call | solution.py:193
  80.1 0.0 collective-permute-done.1.late_ref
  80.1 1.1 %late_grads.1 = (bf16[1,320,384]{2,1,0:T(8,128)(2,1)S(1)}, f32[12,1,384]{2,1,0:T(1,128)S(1)}) custom-call(s32[8]{0:T(128)S(1)} %bitcast.21, bf16[1,256,384]{2,1,0:T(8,128)(2,1)S(1)} %collective-permute-done.early_ref, bf16[1,64,384]{2,1,0:T(8,128)(2,1)S(1)} %collective-permute-done.1.late_ref, bf16[320,1536]{1,0:T(8,128)(2,1)S(1)} %bitcast.15, ...), custom_call_target="tpu_custom_call" | custom-call | tf_op jit(solution)/shard_map/late_grads/pallas_call | solution.py:211
  81.3 0.1 collective-permute-start.6
  81.3 0.7 store_last.1
  82.0 0.5 collective-permute-done.6
  82.5 0.6 multiply_bitcast_fusion
Async XLA Ops:
  0.6 63.8 %copy-start = (bf16[1,1,320,1536]{3,2,1,0:T(8,128)(2,1)S(1)}, bf16[1,1,320,1536]{3,2,1,0:T(8,128)(2,1)}, u32[]{:S(2)}) copy-start(bf16[1,1,320,1536]{3,2,1,0:T(8,128)(2,1)} %param.4) | copy-start | bytes 2949124
  0.6 63.8 %copy-start.1 = (s32[1,1,8]{2,1,0:T(1,128)S(1)}, s32[1,1,8]{2,1,0:T(1,128)}, u32[]{:S(2)}) copy-start(s32[1,1,8]{2,1,0:T(1,128)} %param.5) | copy-start | bytes 100
  3.3 63.2 %collective-permute-start.4 = (bf16[7,320,384]{2,1,0:T(8,128)(2,1)S(1)}, bf16[7,320,384]{2,1,0:T(8,128)(2,1)S(1)}, u32[]{:S(2)}, u32[]{:S(2)}) collective-permute-start(bf16[7,320,384]{2,1,0:T(8,128)(2,1)S(1)} %slice.19), channel_id=1, source_target_pairs={{0,24},{8,16},{16,8},{24,0},{1,25},{9,17},{17,9},{25,1},{2,26},{10... | collective-permute-start | bytes 5160968 | tf_op jit(solution)/shard_map/ppermute | solution.py:271
  8.4 65.4 %collective-permute-start.3 = (bf16[2,320,384]{2,1,0:T(8,128)(2,1)S(1)}, bf16[2,320,384]{2,1,0:T(8,128)(2,1)S(1)}, u32[]{:S(2)}, u32[]{:S(2)}) collective-permute-start(bf16[2,320,384]{2,1,0:T(8,128)(2,1)S(1)} %slice.20), channel_id=1, source_target_pairs={{0,24},{8,16},{16,8},{24,0},{1,25},{9,17},{17,9},{25,1},{2,26},{10... | collective-permute-start | bytes 1474568 | tf_op jit(solution)/shard_map/ppermute | solution.py:271
  8.5 53.0 %collective-permute-start.5 = (bf16[1,320,384]{2,1,0:T(8,128)(2,1)S(1)}, bf16[1,320,384]{2,1,0:T(8,128)(2,1)S(1)}, u32[]{:S(2)}, u32[]{:S(2)}) collective-permute-start(bf16[1,320,384]{2,1,0:T(8,128)(2,1)S(1)} %slice.24), channel_id=1, source_target_pairs={{0,24},{8,16},{16,8},{24,0},{1,25},{9,17},{17,9},{25,1},{2,26},{10... | collective-permute-start | bytes 737288 | tf_op jit(solution)/shard_map/ppermute | solution.py:271
  12.4 64.4 %collective-permute-start.2 = (bf16[1,320,384]{2,1,0:T(8,128)(2,1)S(1)}, bf16[1,320,384]{2,1,0:T(8,128)(2,1)S(1)}, u32[]{:S(2)}, u32[]{:S(2)}) collective-permute-start(bf16[1,320,384]{2,1,0:T(8,128)(2,1)S(1)} %slice.21), channel_id=1, source_target_pairs={{0,24},{8,16},{16,8},{24,0},{1,25},{9,17},{17,9},{25,1},{2,26},{10... | collective-permute-start | bytes 737288 | tf_op jit(solution)/shard_map/ppermute | solution.py:271
  13.5 65.3 %collective-permute-start = (bf16[1,256,384]{2,1,0:T(8,128)(2,1)S(1)}, bf16[1,256,384]{2,1,0:T(8,128)(2,1)S(1)}, u32[]{:S(2)}, u32[]{:S(2)}) collective-permute-start(bf16[1,256,384]{2,1,0:T(8,128)(2,1)S(1)} %slice.22), channel_id=1, source_target_pairs={{0,24},{8,16},{16,8},{24,0},{1,25},{9,17},{17,9},{25,1},{2,26},{10... | collective-permute-start | bytes 589832 | tf_op jit(solution)/shard_map/ppermute | solution.py:271
  61.5 18.6 %collective-permute-start.1 = (bf16[1,64,384]{2,1,0:T(8,128)(2,1)S(1)}, bf16[1,64,384]{2,1,0:T(8,128)(2,1)S(1)}, u32[]{:S(2)}, u32[]{:S(2)}) collective-permute-start(bf16[1,64,384]{2,1,0:T(8,128)(2,1)S(1)} %slice.23), channel_id=1, source_target_pairs={{0,24},{8,16},{16,8},{24,0},{1,25},{9,17},{17,9},{25,1},{2,26},{10... | collective-permute-start | bytes 147464 | tf_op jit(solution)/shard_map/ppermute | solution.py:271
  81.3 1.3 %collective-permute-start.6 = (f32[12,1,384]{2,1,0:T(1,128)S(1)}, f32[12,1,384]{2,1,0:T(1,128)S(1)}, u32[]{:S(2)}, u32[]{:S(2)}) collective-permute-start(f32[12,1,384]{2,1,0:T(1,128)S(1)} %get-tuple-element.49), channel_id=1, source_target_pairs={{0,1},{1,0},{2,3},{3,2},{4,5},{5,4},{6,7},{7,6},{8,9},{9,8},{10,11... | collective-permute-start | bytes 55304 | tf_op jit(solution)/shard_map/ppermute | solution.py:250

commit v4 on v3

--- a/solution.py
+++ b/solution.py
@@ -73,24 +73,28 @@
         bias_ref[bias_head, :, span] = jnp.sum(grad, axis=0, keepdims=True)
 
 
-def chunk_kernel(lengths_ref, packed_ref, grad_ref, *refs, first_head):
-    out_ref, bias_ref = refs[-2:]
-    row_count, pack_width = packed_ref.shape[1:]
-    head_size = pack_width // 3
+def chunk_kernel(packed_ref, grad_ref, start_ref, _, out_ref, bias_ref, *, first_head):
+    head_size = packed_ref.shape[2] // 3
     head = pl.program_id(0)
     grad_at = pl.multiple_of((first_head + head) * head_size, head_size)
-    grads = head_grads(
-        packed_ref[head], grad_ref[:, pl.ds(grad_at, head_size)], doc_starts(lengths_ref, row_count)
-    )
+    grads = head_grads(packed_ref[head], grad_ref[:, pl.ds(grad_at, head_size)], start_ref[...])
     write_head(grads, out_ref, 0, bias_ref, head)
 
 
-def early_kernel(lengths_ref, early_ref, grad_ref, _, query_ref, sums_ref, bias_ref, *, head):
+def first_kernel(lengths_ref, packed_ref, grad_ref, out_ref, bias_ref, start_ref):
+    @pl.when(pl.program_id(0) == 0)
+    def _():
+        start_ref[...] = doc_starts(lengths_ref, packed_ref.shape[1])
+
+    chunk_kernel(packed_ref, grad_ref, start_ref, None, out_ref, bias_ref, first_head=0)
+
+
+def early_kernel(early_ref, grad_ref, start_ref, _, query_ref, sums_ref, bias_ref, *, head):
     row_count, pack_width = early_ref.shape[1:]
     head_size = pack_width // 3
     queries, keys_in, values_in = split_pack(early_ref[0])
     grad_rows = grad_ref[:row_count, head * head_size : (head + 1) * head_size]
-    doc_start = doc_starts(lengths_ref, row_count)
+    doc_start = start_ref[...]
     tiles = [slice(at, at + TILE) for at in range(0, row_count, TILE)]
     key_grads, value_grads = [0.0] * len(tiles), [0.0] * len(tiles)
     bias = jnp.zeros((1, head_size), jnp.float32)
@@ -111,10 +115,9 @@
         sums_ref[tile, head_size:] = value_grads[index]
 
 
-def late_kernel(lengths_ref, early_ref, late_ref, grad_ref, query_ref, sums_ref, early_bias_ref, *refs):
+def late_kernel(early_ref, late_ref, grad_ref, start_ref, query_ref, sums_ref, early_bias_ref, *refs):
     bias_parts, (out_ref, bias_ref) = refs[:-2], refs[-2:]
     split = early_ref.shape[1]
-    row_count = split + late_ref.shape[1]
     head_size = early_ref.shape[2] // 3
     head = sum(part_ref.shape[0] for part_ref in bias_parts)
     queries = late_ref[0, :, :head_size]
@@ -124,7 +127,7 @@
         for part in (1, 2)
     )
     prob_low, score_low = tile_weights(
-        queries, keys_in, values_in, grad_rows, doc_starts(lengths_ref, row_count)[:, split:], split
+        queries, keys_in, values_in, grad_rows, start_ref[:, split:], split
     )
     query_grad = dot(score_low, keys_in, COLUMNS)
     out_ref[0, :split, :head_size] = query_ref[...]
@@ -161,38 +164,47 @@
 ANY_SPEC = pl.BlockSpec(memory_space=pl.ANY)
 
 
-def chunk_grads(packed, grad_rows, lengths, head_count, first_head, previous):
+def chunk_grads(packed, grad_rows, lengths, head_count, first_head, start_row, previous):
     chunk_heads, row_count, pack_width = packed.shape
-    in_specs = [SMEM_SPEC, VMEM_SPEC, VMEM_SPEC]
-    operands = [lengths, in_vmem(packed), in_vmem(grad_rows)]
-    aliases = {}
-    if previous is not None:
-        in_specs.append(ANY_SPEC)
-        operands.append(previous)
-        aliases = {3: 0}
-    return pl.pallas_call(
+    blocks = [in_vmem(packed), in_vmem(grad_rows)]
+    out_specs = [
+        pl.BlockSpec((1, row_count, pack_width), lambda h: (first_head + h, 0, 0)),
+        VMEM_SPEC,
+    ]
+    out_shape = [
+        jax.ShapeDtypeStruct((head_count, row_count, pack_width), jnp.bfloat16),
+        pltpu.VMEM((chunk_heads, 1, pack_width), jnp.float32),
+    ]
+    options = dict(
+        grid=(chunk_heads,),
+        compiler_params=pltpu.CompilerParams(vmem_limit_bytes=KERNEL_VMEM),
+        name=f"grads_at_{first_head}",
+    )
+    if previous is None:
+        return pl.pallas_call(
+            first_kernel,
+            in_specs=[SMEM_SPEC, VMEM_SPEC, VMEM_SPEC],
+            out_specs=out_specs + [VMEM_SPEC],
+            out_shape=out_shape + [pltpu.VMEM((1, row_count), jnp.int32)],
+            **options,
+        )(lengths, *blocks)
+    grads, bias = pl.pallas_call(
         functools.partial(chunk_kernel, first_head=first_head),
-        grid=(chunk_heads,),
-        in_specs=in_specs,
-        out_specs=[
-            pl.BlockSpec((1, row_count, pack_width), lambda h: (first_head + h, 0, 0)),
-            VMEM_SPEC,
-        ],
-        out_shape=[
-            jax.ShapeDtypeStruct((head_count, row_count, pack_width), jnp.bfloat16),
-            pltpu.VMEM((chunk_heads, 1, pack_width), jnp.float32),
-        ],
-        input_output_aliases=aliases,
-        compiler_params=pltpu.CompilerParams(vmem_limit_bytes=KERNEL_VMEM),
-    )(*operands)
-
-
-def early_grads(packed, grad_rows, lengths, head, after):
+        in_specs=[VMEM_SPEC, VMEM_SPEC, VMEM_SPEC, ANY_SPEC],
+        out_specs=out_specs,
+        out_shape=out_shape,
+        input_output_aliases={3: 0},
+        **options,
+    )(*blocks, in_vmem(start_row), previous)
+    return grads, bias, start_row
+
+
+def early_grads(packed, grad_rows, start_row, head, after):
     _, row_count, pack_width = packed.shape
     head_size = pack_width // 3
     return pl.pallas_call(
         functools.partial(early_kernel, head=head),
-        in_specs=[SMEM_SPEC] + [VMEM_SPEC] * 3,
+        in_specs=[VMEM_SPEC] * 4,
         out_specs=[VMEM_SPEC] * 3,
         out_shape=[
             pltpu.VMEM((row_count, head_size), jnp.bfloat16),
@@ -201,16 +213,16 @@
         ],
         compiler_params=pltpu.CompilerParams(vmem_limit_bytes=KERNEL_VMEM),
         name="early_grads",
-    )(lengths, in_vmem(packed), in_vmem(grad_rows), in_vmem(after))
-
-
-def late_grads(early, late, grad_rows, lengths, started, bias_parts):
+    )(in_vmem(packed), in_vmem(grad_rows), in_vmem(start_row), in_vmem(after))
+
+
+def late_grads(early, late, grad_rows, start_row, started, bias_parts):
     head_count = 1 + sum(part.shape[0] for part in bias_parts)
     row_count, pack_width = grad_rows.shape[0], early.shape[2]
-    operands = [early, late, grad_rows, *started, *bias_parts]
+    operands = [early, late, grad_rows, start_row, *started, *bias_parts]
     return pl.pallas_call(
         late_kernel,
-        in_specs=[SMEM_SPEC] + [VMEM_SPEC] * len(operands),
+        in_specs=[VMEM_SPEC] * len(operands),
         out_specs=[VMEM_SPEC, VMEM_SPEC],
         out_shape=[
             pltpu.VMEM((1, row_count, pack_width), jnp.bfloat16),
@@ -218,7 +230,7 @@
         ],
         compiler_params=pltpu.CompilerParams(vmem_limit_bytes=KERNEL_VMEM),
         name="late_grads",
-    )(lengths, *[in_vmem(operand) for operand in operands])
+    )(*[in_vmem(operand) for operand in operands])
 
 
 def store_last(head, grads):
@@ -269,13 +281,15 @@
     for piece in pieces:
         packed, by_head = lax.optimization_barrier((by_head[piece], by_head))
         arrived.append(lax.ppermute(packed, "section", mirror))
-    grads, bias_parts = None, []
+    grads, start_row, bias_parts = None, None, []
     for first, packed in zip(firsts, arrived):
-        grads, bias = chunk_grads(packed, grad_rows, lengths, head_count, first, grads)
+        grads, bias, start_row = chunk_grads(
+            packed, grad_rows, lengths, head_count, first, start_row, grads
+        )
         bias_parts.append(bias)
     early, late = arrived[-2:]
-    started = early_grads(early, grad_rows, lengths, last, bias_parts[-1])
-    final, bias_own = late_grads(early, late, grad_rows, lengths, started, bias_parts)
+    started = early_grads(early, grad_rows, start_row, last, bias_parts[-1])
+    final, bias_own = late_grads(early, late, grad_rows, start_row, started, bias_parts)
     bias_total = replica_sum(bias_own, "dp")
     grads = store_last(final, grads)
     bias_grad = jnp.transpose(bias_total / lax.axis_size("dp"), (1, 0, 2))

time: 83.5 us -> 80.6 us (0.965)
  Pallas kernels: 17.5 us -> 14.6 us
    pallas_call x6, Pallas kernels: 16.8 us -> 13.9 us  [the longest x3 10.5 us: chunk_grads(): pl.pallas_call(functools.partial(chunk_kernel, first_head=first_head), in...]
  transfers between devices with their start and end apart: 7 -> 7, of which waited for: 2 -> 2; matrix products, arithmetic and copies ran while one was open for 5% -> 5% of each run, Pallas kernels for 20% -> 17%
where the time goes in v4:
time: 80.6 us; the launch traced here: 80.3 us
  waiting for transfers between devices  44.8 us (56%)
  Pallas kernels  14.6 us (18%)
  starting transfers between devices  13 us (16%)
  local copies, waits for them, and re-layouts  6.5 us (8%)
    ppermute x6, waiting for transfers between devices, body(): arrived.append(lax.ppermute(packed, 'section', mirror))  44.4 us
    ppermute x6, starting transfers between devices, body(): arrived.append(lax.ppermute(packed, 'section', mirror))  13 us
    pallas_call x3, Pallas kernels, chunk_grads(): pl.pallas_call(functools.partial(chunk_kernel, first_head=first_head), in...  10.5 us
    slice x6, local copies, waits for them, and re-layouts, body(): packed, by_head = lax.optimization_barrier((by_head[piece], by_head))  6.49 us
    pallas_call x1, Pallas kernels, chunk_grads(): pl.pallas_call(first_kernel, in_specs=[SMEM_SPEC, VMEM_SPEC, VMEM_SPEC],...  2.07 us
  transfers between devices with their start and end apart: 7, of which 2 were waited for; matrix products, arithmetic and copies ran while one was open for 5% of the time, Pallas kernels for 17%

profile of v4, /device:TPU:0, one launch (start us, length us, event | category | flops | bytes accessed | tf_op | source)
XLA Modules:
  0.0 80.3 jit_solution(9010838990055837495)
XLA Ops:
  0.6 0.0 copy-start
  0.6 0.0 copy-start.1
  0.6 1.1 %slice.24 = bf16[1,320,384]{2,1,0:T(8,128)(2,1)S(1)} slice(bf16[12,320,384]{2,1,0:T(8,128)(2,1)} %bitcast.18), slice={[0:1], [0:320], [0:384]} | slice | bytes 491520 | tf_op jit(solution)/shard_map/slice | solution.py:282
  1.7 1.6 %slice.19 = bf16[7,320,384]{2,1,0:T(8,128)(2,1)S(1)} slice(bf16[12,320,384]{2,1,0:T(8,128)(2,1)} %bitcast.19), slice={[1:8], [0:320], [0:384]} | slice | bytes 3440640 | tf_op jit(solution)/shard_map/slice | solution.py:282
  3.3 4.0 %collective-permute-start.5 = (bf16[7,320,384]{2,1,0:T(8,128)(2,1)S(1)}, bf16[7,320,384]{2,1,0:T(8,128)(2,1)S(1)}, u32[]{:S(2)}, u32[]{:S(2)}) collective-permute-start(bf16[7,320,384]{2,1,0:T(8,128)(2,1)S(1)} %slice.19), channel_id=1, source_target_pairs={{0,24},{8,16},{16,8},{24,0},{1,25},{9,17},{17,9},{25,1},{2,26},{10... | collective-permute-start | bytes 5160968 | tf_op jit(solution)/shard_map/ppermute | solution.py:283
  7.3 1.1 %slice.20 = bf16[2,320,384]{2,1,0:T(8,128)(2,1)S(1)} slice(bf16[12,320,384]{2,1,0:T(8,128)(2,1)} %bitcast.20), slice={[8:10], [0:320], [0:384]} | slice | bytes 983040 | tf_op jit(solution)/shard_map/slice | solution.py:282
  8.4 0.1 collective-permute-start.4
  8.5 2.9 %collective-permute-start.2 = (bf16[1,320,384]{2,1,0:T(8,128)(2,1)S(1)}, bf16[1,320,384]{2,1,0:T(8,128)(2,1)S(1)}, u32[]{:S(2)}, u32[]{:S(2)}) collective-permute-start(bf16[1,320,384]{2,1,0:T(8,128)(2,1)S(1)} %slice.24), channel_id=1, source_target_pairs={{0,24},{8,16},{16,8},{24,0},{1,25},{9,17},{17,9},{25,1},{2,26},{10... | collective-permute-start | bytes 737288 | tf_op jit(solution)/shard_map/ppermute | solution.py:283
  11.4 1.0 %slice.21 = bf16[1,320,384]{2,1,0:T(8,128)(2,1)S(1)} slice(bf16[12,320,384]{2,1,0:T(8,128)(2,1)} %bitcast.21), slice={[10:11], [0:320], [0:384]} | slice | bytes 491520 | tf_op jit(solution)/shard_map/slice | solution.py:282
  12.4 0.1 collective-permute-start.3
  12.5 0.9 %slice.22 = bf16[1,256,384]{2,1,0:T(8,128)(2,1)S(1)} slice(bf16[12,320,384]{2,1,0:T(8,128)(2,1)} %bitcast.22), slice={[11:12], [0:256], [0:384]} | slice | bytes 393216 | tf_op jit(solution)/shard_map/slice | solution.py:282
  13.5 2.9 %collective-permute-start = (bf16[1,256,384]{2,1,0:T(8,128)(2,1)S(1)}, bf16[1,256,384]{2,1,0:T(8,128)(2,1)S(1)}, u32[]{:S(2)}, u32[]{:S(2)}) collective-permute-start(bf16[1,256,384]{2,1,0:T(8,128)(2,1)S(1)} %slice.22), channel_id=1, source_target_pairs={{0,24},{8,16},{16,8},{24,0},{1,25},{9,17},{17,9},{25,1},{2,26},{10... | collective-permute-start | bytes 589832 | tf_op jit(solution)/shard_map/ppermute | solution.py:283
  16.4 0.8 %slice.23 = bf16[1,64,384]{2,1,0:T(8,128)(2,1)S(1)} slice(bf16[12,320,384]{2,1,0:T(8,128)(2,1)} %bitcast.23), slice={[11:12], [256:320], [0:384]} | slice | bytes 98304 | tf_op jit(solution)/shard_map/slice | solution.py:282
  17.2 44.3 %collective-permute-done.2.packed_ref = bf16[1,320,384]{2,1,0:T(8,128)(2,1)S(1)} collective-permute-done((bf16[1,320,384]{2,1,0:T(8,128)(2,1)S(1)}, bf16[1,320,384]{2,1,0:T(8,128)(2,1)S(1)}, u32[]{:S(2)}, u32[]{:S(2)}) %collective-permute-start.2) | collective-permute-done | bytes 245792 | tf_op jit(solution)/shard_map/ppermute | solution.py:283
  61.5 2.9 %collective-permute-start.1 = (bf16[1,64,384]{2,1,0:T(8,128)(2,1)S(1)}, bf16[1,64,384]{2,1,0:T(8,128)(2,1)S(1)}, u32[]{:S(2)}, u32[]{:S(2)}) collective-permute-start(bf16[1,64,384]{2,1,0:T(8,128)(2,1)S(1)} %slice.23), channel_id=1, source_target_pairs={{0,24},{8,16},{16,8},{24,0},{1,25},{9,17},{17,9},{25,1},{2,26},{10... | collective-permute-start | bytes 147464 | tf_op jit(solution)/shard_map/ppermute | solution.py:283
  64.5 0.0 copy-done
  64.5 0.0 copy-done.1
  64.5 2.1 %grads_at_0.1 = (bf16[12,320,384]{2,1,0:T(8,128)(2,1)}, f32[1,1,384]{2,1,0:T(1,128)S(1)}, s32[1,320]{1,0:T(1,128)S(1)}) custom-call(s32[8]{0:T(128)S(1)} %bitcast.16, bf16[1,320,384]{2,1,0:T(8,128)(2,1)S(1)} %collective-permute-done.2.packed_ref, bf16[320,1536]{1,0:T(8,128)(2,1)S(1)} %bitcast.10), custom_call_target="tpu_custom_call" | custom-call | tf_op jit(solution)/shard_map/grads_at_0/pallas_call | solution.py:184
  66.5 0.0 collective-permute-done.5.packed_ref
  66.5 6.6 %grads_at_1.1 = (bf16[12,320,384]{2,1,0:T(8,128)(2,1)}, f32[7,1,384]{2,1,0:T(1,128)S(1)}) custom-call(bf16[7,320,384]{2,1,0:T(8,128)(2,1)S(1)} %collective-permute-done.5.packed_ref, bf16[320,1536]{1,0:T(8,128)(2,1)S(1)} %bitcast.11, s32[1,320]{1,0:T(1,128)S(1)} %get-tuple-element.35.start_ref, ...), custom_call_target="tpu_custom_call", output_to_operand_aliasing={{0}: (3, {})} | custom-call | tf_op jit(solution)/shard_map/grads_at_1/pallas_call | solution.py:191
  73.1 0.0 collective-permute-done.4.packed_ref
  73.1 2.4 %grads_at_8.1 = (bf16[12,320,384]{2,1,0:T(8,128)(2,1)}, f32[2,1,384]{2,1,0:T(1,128)S(1)}) custom-call(bf16[2,320,384]{2,1,0:T(8,128)(2,1)S(1)} %collective-permute-done.4.packed_ref, bf16[320,1536]{1,0:T(8,128)(2,1)S(1)} %bitcast.12, s32[1,320]{1,0:T(1,128)S(1)} %get-tuple-element.35.start_ref, ...), custom_call_target="tpu_custom_call", output_to_operand_aliasing={{0}: (3, {})} | custom-call | tf_op jit(solution)/shard_map/grads_at_8/pallas_call | solution.py:191
  75.5 0.0 collective-permute-done.3.packed_ref
  75.5 1.5 %grads_at_10.1 = (bf16[12,320,384]{2,1,0:T(8,128)(2,1)}, f32[1,1,384]{2,1,0:T(1,128)S(1)}) custom-call(bf16[1,320,384]{2,1,0:T(8,128)(2,1)S(1)} %collective-permute-done.3.packed_ref, bf16[320,1536]{1,0:T(8,128)(2,1)S(1)} %bitcast.13, s32[1,320]{1,0:T(1,128)S(1)} %get-tuple-element.35.start_ref, ...), custom_call_target="tpu_custom_call", output_to_operand_aliasing={{0}: (3, {})} | custom-call | tf_op jit(solution)/shard_map/grads_at_10/pallas_call | solution.py:191
  77.1 0.0 collective-permute-done.early_ref
  77.1 0.8 early_grads.1
  77.8 0.0 collective-permute-done.1.late_ref
  77.8 0.6 late_grads.1
  78.4 0.1 collective-permute-start.6
  78.5 0.7 store_last.1
  79.2 0.5 collective-permute-done.6
  79.7 0.6 multiply_bitcast_fusion
Async XLA Ops:
  0.6 63.8 %copy-start = (bf16[1,1,320,1536]{3,2,1,0:T(8,128)(2,1)S(1)}, bf16[1,1,320,1536]{3,2,1,0:T(8,128)(2,1)}, u32[]{:S(2)}) copy-start(bf16[1,1,320,1536]{3,2,1,0:T(8,128)(2,1)} %param.4) | copy-start | bytes 2949124
  0.6 63.8 %copy-start.1 = (s32[1,1,8]{2,1,0:T(1,128)S(1)}, s32[1,1,8]{2,1,0:T(1,128)}, u32[]{:S(2)}) copy-start(s32[1,1,8]{2,1,0:T(1,128)} %param.5) | copy-start | bytes 100
  3.3 63.2 %collective-permute-start.5 = (bf16[7,320,384]{2,1,0:T(8,128)(2,1)S(1)}, bf16[7,320,384]{2,1,0:T(8,128)(2,1)S(1)}, u32[]{:S(2)}, u32[]{:S(2)}) collective-permute-start(bf16[7,320,384]{2,1,0:T(8,128)(2,1)S(1)} %slice.19), channel_id=1, source_target_pairs={{0,24},{8,16},{16,8},{24,0},{1,25},{9,17},{17,9},{25,1},{2,26},{10... | collective-permute-start | bytes 5160968 | tf_op jit(solution)/shard_map/ppermute | solution.py:283
  8.4 64.7 %collective-permute-start.4 = (bf16[2,320,384]{2,1,0:T(8,128)(2,1)S(1)}, bf16[2,320,384]{2,1,0:T(8,128)(2,1)S(1)}, u32[]{:S(2)}, u32[]{:S(2)}) collective-permute-start(bf16[2,320,384]{2,1,0:T(8,128)(2,1)S(1)} %slice.20), channel_id=1, source_target_pairs={{0,24},{8,16},{16,8},{24,0},{1,25},{9,17},{17,9},{25,1},{2,26},{10... | collective-permute-start | bytes 1474568 | tf_op jit(solution)/shard_map/ppermute | solution.py:283
  8.5 53.0 %collective-permute-start.2 = (bf16[1,320,384]{2,1,0:T(8,128)(2,1)S(1)}, bf16[1,320,384]{2,1,0:T(8,128)(2,1)S(1)}, u32[]{:S(2)}, u32[]{:S(2)}) collective-permute-start(bf16[1,320,384]{2,1,0:T(8,128)(2,1)S(1)} %slice.24), channel_id=1, source_target_pairs={{0,24},{8,16},{16,8},{24,0},{1,25},{9,17},{17,9},{25,1},{2,26},{10... | collective-permute-start | bytes 737288 | tf_op jit(solution)/shard_map/ppermute | solution.py:283
  12.4 63.1 %collective-permute-start.3 = (bf16[1,320,384]{2,1,0:T(8,128)(2,1)S(1)}, bf16[1,320,384]{2,1,0:T(8,128)(2,1)S(1)}, u32[]{:S(2)}, u32[]{:S(2)}) collective-permute-start(bf16[1,320,384]{2,1,0:T(8,128)(2,1)S(1)} %slice.21), channel_id=1, source_target_pairs={{0,24},{8,16},{16,8},{24,0},{1,25},{9,17},{17,9},{25,1},{2,26},{10... | collective-permute-start | bytes 737288 | tf_op jit(solution)/shard_map/ppermute | solution.py:283
  13.5 63.6 %collective-permute-start = (bf16[1,256,384]{2,1,0:T(8,128)(2,1)S(1)}, bf16[1,256,384]{2,1,0:T(8,128)(2,1)S(1)}, u32[]{:S(2)}, u32[]{:S(2)}) collective-permute-start(bf16[1,256,384]{2,1,0:T(8,128)(2,1)S(1)} %slice.22), channel_id=1, source_target_pairs={{0,24},{8,16},{16,8},{24,0},{1,25},{9,17},{17,9},{25,1},{2,26},{10... | collective-permute-start | bytes 589832 | tf_op jit(solution)/shard_map/ppermute | solution.py:283
  61.5 16.3 %collective-permute-start.1 = (bf16[1,64,384]{2,1,0:T(8,128)(2,1)S(1)}, bf16[1,64,384]{2,1,0:T(8,128)(2,1)S(1)}, u32[]{:S(2)}, u32[]{:S(2)}) collective-permute-start(bf16[1,64,384]{2,1,0:T(8,128)(2,1)S(1)} %slice.23), channel_id=1, source_target_pairs={{0,24},{8,16},{16,8},{24,0},{1,25},{9,17},{17,9},{25,1},{2,26},{10... | collective-permute-start | bytes 147464 | tf_op jit(solution)/shard_map/ppermute | solution.py:283
  78.4 1.3 %collective-permute-start.6 = (f32[12,1,384]{2,1,0:T(1,128)S(1)}, f32[12,1,384]{2,1,0:T(1,128)S(1)}, u32[]{:S(2)}, u32[]{:S(2)}) collective-permute-start(f32[12,1,384]{2,1,0:T(1,128)S(1)} %get-tuple-element.51), channel_id=1, source_target_pairs={{0,1},{1,0},{2,3},{3,2},{4,5},{5,4},{6,7},{7,6},{8,9},{9,8},{10,11... | collective-permute-start | bytes 55304 | tf_op jit(solution)/shard_map/ppermute | solution.py:262

commit v5 on v4

v5 whole, which is shorter than its diff:
```python
import functools
import math

import jax
import jax.numpy as jnp
from jax import lax
from jax.experimental import pallas as pl
from jax.experimental.pallas import tpu as pltpu
from jax.sharding import PartitionSpec as P

MASKED = -1e30
TILE = 128
ROW_TILE = 16
KERNEL_VMEM = 16 * 1024 * 1024


def doc_starts(lengths_ref, row_count):
    query_at = lax.broadcasted_iota(jnp.int32, (1, row_count), 1)
    doc_start = jnp.zeros((1, row_count), jnp.int32)
    doc_end = jnp.int32(0)
    for doc in range(lengths_ref.shape[0]):
        doc_end = doc_end + lengths_ref[doc]
        doc_start = jnp.where(query_at >= doc_end, doc_end, doc_start)
    return doc_start


ROWS_BY_ROWS = (((1,), (1,)), ((), ()))
PLAIN = (((1,), (0,)), ((), ()))
COLUMNS = (((0,), (0,)), ((), ()))
dot = functools.partial(lax.dot_general, preferred_element_type=jnp.float32)


def split_pack(packed):
    head_size = packed.shape[1] // 3
    return (
        packed[:, :head_size],
        packed[:, head_size : 2 * head_size],
        packed[:, 2 * head_size :],
    )


def mask_rows(doc_start, first_query, first_key, key_count):
    shape = (key_count, doc_start.shape[1])
    query_at = first_query + lax.broadcasted_iota(jnp.int32, (1, shape[1]), 1)
    key_at = first_key + lax.broadcasted_iota(jnp.int32, shape, 0)
    return jnp.where((key_at >= doc_start) & (key_at <= query_at), 0.0, MASKED)


def tile_weights(queries, keys_in, values_in, grad_rows, mask):
    inv_root = 1.0 / math.sqrt(queries.shape[1])
    masked = dot(keys_in, queries, ROWS_BY_ROWS) + mask
    row_top = jnp.max(masked, axis=0, keepdims=True)
    raised = jnp.exp2((masked - row_top) * (inv_root * math.log2(math.e)))
    prob = raised * (1.0 / jnp.sum(raised, axis=0, keepdims=True))
    prob_grad = dot(values_in, grad_rows, ROWS_BY_ROWS)
    row_dot = jnp.sum(prob * prob_grad, axis=0, keepdims=True)
    score_grad = (prob * inv_root) * (prob_grad - row_dot)
    return prob.astype(jnp.bfloat16), score_grad.astype(jnp.bfloat16)


def head_grads(packed, grad_rows, doc_start):
    queries, keys_in, values_in = split_pack(packed)
    mask = mask_rows(doc_start, 0, 0, packed.shape[0])
    prob_low, score_low = tile_weights(queries, keys_in, values_in, grad_rows, mask)
    return (
        dot(score_low, keys_in, COLUMNS),
        dot(score_low, queries, PLAIN),
        dot(prob_low, grad_rows, PLAIN),
    )


def write_head(grads, out_ref, out_head, bias_ref, bias_head):
    for part, grad in enumerate(grads):
        head_size = grad.shape[1]
        span = slice(part * head_size, (part + 1) * head_size)
        out_ref[out_head, :, span] = grad.astype(jnp.bfloat16)
        bias_ref[bias_head, :, span] = jnp.sum(grad, axis=0, keepdims=True)


def chunk_kernel(packed_ref, grad_ref, start_ref, _, out_ref, bias_ref, *, first_head):
    head_size = packed_ref.shape[2] // 3
    head = pl.program_id(0)
    grad_at = pl.multiple_of((first_head + head) * head_size, head_size)
    grads = head_grads(packed_ref[head], grad_ref[:, pl.ds(grad_at, head_size)], start_ref[...])
    write_head(grads, out_ref, 0, bias_ref, head)


def first_kernel(lengths_ref, first_ref, rest_ref, grad_ref, out_ref, bias_ref, start_ref):
    head = pl.program_id(0)
    first_count = first_ref.shape[0]
    head_size = first_ref.shape[2] // 3

    @pl.when(head == 0)
    def _():
        start_ref[...] = doc_starts(lengths_ref, first_ref.shape[1])

    packed = jnp.where(
        head < first_count,
        first_ref[jnp.minimum(head, first_count - 1)],
        rest_ref[jnp.maximum(head - first_count, 0)],
    )
    grad_at = pl.multiple_of(head * head_size, head_size)
    grads = head_grads(packed, grad_ref[:, pl.ds(grad_at, head_size)], start_ref[...])
    write_head(grads, out_ref, 0, bias_ref, head)


def column_sum(rows):
    return jnp.sum(rows, axis=0, keepdims=True)


def early_kernel(early_ref, grad_ref, start_ref, _, query_ref, sums_ref, bias_ref, mask_ref, *, head):
    row_count, pack_width = early_ref.shape[1:]
    head_size = pack_width // 3
    queries, keys_in, values_in = split_pack(early_ref[0])
    grad_rows = grad_ref[:row_count, head * head_size : (head + 1) * head_size]
    doc_start = start_ref[...]
    tiles = [slice(at, min(at + TILE, row_count)) for at in range(0, row_count, TILE)]
    key_grads, value_grads = [0.0] * len(tiles), [0.0] * len(tiles)
    query_bias = jnp.zeros((1, head_size), jnp.float32)
    for index, tile in enumerate(tiles):
        seen = slice(0, tile.stop)
        mask = mask_rows(doc_start[:, tile], tile.start, 0, tile.stop)
        prob_low, score_low = tile_weights(
            queries[tile], keys_in[seen], values_in[seen], grad_rows[tile], mask
        )
        query_grad = dot(score_low, keys_in[seen], COLUMNS)
        query_ref[tile] = query_grad.astype(jnp.bfloat16)
        query_bias += column_sum(query_grad)
        for past in range(index + 1):
            key_grads[past] += dot(score_low[tiles[past]], queries[tile], PLAIN)
            value_grads[past] += dot(prob_low[tiles[past]], grad_rows[tile], PLAIN)
    bias_ref[:, :head_size] = query_bias
    for part, grads in enumerate((key_grads, value_grads)):
        for tile, grad in zip(tiles, grads):
            sums_ref[tile, part * head_size : (part + 1) * head_size] = grad
        bias_ref[:, (part + 1) * head_size : (part + 2) * head_size] = sum(map(column_sum, grads))
    first_key = doc_start.shape[1] - mask_ref.shape[0]
    mask_ref[...] = mask_rows(doc_start[:, row_count:], row_count, first_key, mask_ref.shape[0])


def late_kernel(early_ref, late_ref, grad_ref, mask_ref, early_bias_ref, *refs):
    bias_parts, (query_ref, added_ref, bias_ref) = refs[:-3], refs[-3:]
    split = early_ref.shape[1]
    first_key = split + late_ref.shape[1] - mask_ref.shape[0]
    head_size = early_ref.shape[2] // 3
    head = sum(part_ref.shape[0] for part_ref in bias_parts)
    queries = late_ref[0, :, :head_size]
    grad_rows = grad_ref[split:, head * head_size : (head + 1) * head_size]
    keys_in, values_in = (
        jnp.concatenate([early_ref[0, first_key:, span], late_ref[0, :, span]], axis=0)
        for span in (slice(head_size, 2 * head_size), slice(2 * head_size, None))
    )
    prob_low, score_low = tile_weights(queries, keys_in, values_in, grad_rows, mask_ref[...])
    query_grad = dot(score_low, keys_in, COLUMNS)
    key_grad = dot(score_low, queries, PLAIN)
    value_grad = dot(prob_low, grad_rows, PLAIN)
    for part, grad in enumerate((query_grad, key_grad, value_grad)):
        span = slice(part * head_size, (part + 1) * head_size)
        bias_ref[head, :, span] = early_bias_ref[:, span] + column_sum(grad)
    query_ref[...] = query_grad.astype(jnp.bfloat16)
    added_ref[:, :head_size] = key_grad
    added_ref[:, head_size:] = value_grad
    head_at = 0
    for part_ref in bias_parts:
        bias_ref[head_at : head_at + part_ref.shape[0]] = part_ref[...]
        head_at += part_ref.shape[0]


def store_kernel(early_query_ref, sums_ref, late_query_ref, added_ref, _, out_ref, head_ref, semaphore):
    split, head_size = early_query_ref.shape
    first_key = head_ref.shape[1] - added_ref.shape[0]
    head_ref[0, :split, :head_size] = early_query_ref[...]
    head_ref[0, split:, :head_size] = late_query_ref[...]
    head_ref[0, :first_key, head_size:] = sums_ref[:first_key].astype(jnp.bfloat16)
    seen = split - first_key
    head_ref[0, first_key:split, head_size:] = (sums_ref[first_key:] + added_ref[:seen]).astype(
        jnp.bfloat16
    )
    head_ref[0, split:, head_size:] = added_ref[seen:].astype(jnp.bfloat16)
    at = out_ref.shape[0] - 1
    copy = pltpu.make_async_copy(head_ref, out_ref.at[pl.ds(at, 1)], semaphore)
    copy.start()
    copy.wait()


def in_vmem(array):
    return pltpu.with_memory_space_constraint(array, pltpu.VMEM)


VMEM_SPEC = pl.BlockSpec(memory_space=pltpu.VMEM)
SMEM_SPEC = pl.BlockSpec(memory_space=pltpu.SMEM)
ANY_SPEC = pl.BlockSpec(memory_space=pl.ANY)


def grads_outs(chunk_heads, head_count, first_head, row_count, pack_width):
    specs = [
        pl.BlockSpec((1, row_count, pack_width), lambda h: (first_head + h, 0, 0)),
        VMEM_SPEC,
    ]
    shapes = [
        jax.ShapeDtypeStruct((head_count, row_count, pack_width), jnp.bfloat16),
        pltpu.VMEM((chunk_heads, 1, pack_width), jnp.float32),
    ]
    return specs, shapes


def first_grads(first, rest, grad_rows, lengths, head_count):
    _, row_count, pack_width = first.shape
    chunk_heads = first.shape[0] + rest.shape[0]
    specs, shapes = grads_outs(chunk_heads, head_count, 0, row_count, pack_width)
    return pl.pallas_call(
        first_kernel,
        grid=(chunk_heads,),
        in_specs=[SMEM_SPEC, VMEM_SPEC, VMEM_SPEC, VMEM_SPEC],
        out_specs=specs + [VMEM_SPEC],
        out_shape=shapes + [pltpu.VMEM((1, row_count), jnp.int32)],
        compiler_params=pltpu.CompilerParams(vmem_limit_bytes=KERNEL_VMEM),
        name="first_grads",
    )(lengths, in_vmem(first), in_vmem(rest), in_vmem(grad_rows))


def chunk_grads(packed, grad_rows, start_row, first_head, previous):
    chunk_heads, row_count, pack_width = packed.shape
    specs, shapes = grads_outs(chunk_heads, previous.shape[0], first_head, row_count, pack_width)
    return pl.pallas_call(
        functools.partial(chunk_kernel, first_head=first_head),
        grid=(chunk_heads,),
        in_specs=[VMEM_SPEC, VMEM_SPEC, VMEM_SPEC, ANY_SPEC],
        out_specs=specs,
        out_shape=shapes,
        input_output_aliases={3: 0},
        compiler_params=pltpu.CompilerParams(vmem_limit_bytes=KERNEL_VMEM),
    )(in_vmem(packed), in_vmem(grad_rows), in_vmem(start_row), previous)


def early_grads(packed, grad_rows, start_row, head, after):
    _, split, pack_width = packed.shape
    row_count, head_size = grad_rows.shape[0], pack_width // 3
    longest = row_count // 2
    first_key = max(0, split + 1 - longest) // ROW_TILE * ROW_TILE
    return pl.pallas_call(
        functools.partial(early_kernel, head=head),
        in_specs=[VMEM_SPEC] * 4,
        out_specs=[VMEM_SPEC] * 4,
        out_shape=[
            pltpu.VMEM((split, head_size), jnp.bfloat16),
            pltpu.VMEM((split, 2 * head_size), jnp.float32),
            pltpu.VMEM((1, pack_width), jnp.float32),
            pltpu.VMEM((row_count - first_key, row_count - split), jnp.float32),
        ],
        compiler_params=pltpu.CompilerParams(vmem_limit_bytes=KERNEL_VMEM),
        name="early_grads",
    )(*map(in_vmem, (packed, grad_rows, start_row, after)))


def late_grads(early, late, grad_rows, mask, early_bias, bias_parts):
    head_count = 1 + sum(part.shape[0] for part in bias_parts)
    pack_width = early.shape[2]
    head_size = pack_width // 3
    operands = [early, late, grad_rows, mask, early_bias, *bias_parts]
    return pl.pallas_call(
        late_kernel,
        in_specs=[VMEM_SPEC] * len(operands),
        out_specs=[VMEM_SPEC] * 3,
        out_shape=[
            pltpu.VMEM((late.shape[1], head_size), jnp.bfloat16),
            pltpu.VMEM((mask.shape[0], 2 * head_size), jnp.float32),
            pltpu.VMEM((head_count, 1, pack_width), jnp.float32),
        ],
        compiler_params=pltpu.CompilerParams(vmem_limit_bytes=KERNEL_VMEM),
        name="late_grads",
    )(*map(in_vmem, operands))


def store_last(parts, grads):
    return pl.pallas_call(
        store_kernel,
        in_specs=[VMEM_SPEC] * len(parts) + [ANY_SPEC],
        out_specs=ANY_SPEC,
        out_shape=jax.ShapeDtypeStruct(grads.shape, grads.dtype),
        scratch_shapes=[pltpu.VMEM((1, *grads.shape[1:]), grads.dtype), pltpu.SemaphoreType.DMA],
        input_output_aliases={len(parts): 0},
        compiler_params=pltpu.CompilerParams(vmem_limit_bytes=KERNEL_VMEM),
        name="store_last",
    )(*map(in_vmem, parts), grads)


def chunk_sizes(head_count):
    tail = min(2, head_count // 2)
    return [1, head_count - 1 - tail, tail]


def replica_sum(value, axis):
    count = lax.axis_size(axis)
    if count & (count - 1):
        return lax.psum(value, axis)
    stride = 1
    while stride < count:
        value = value + lax.ppermute(value, axis, [(i, i ^ stride) for i in range(count)])
        stride *= 2
    return value


def body(stash, grad_out, doc_lengths):
    by_head = jnp.transpose(stash[0, 0], (1, 0, 2))
    head_count = by_head.shape[0]
    section_count = lax.axis_size("section")
    mirror = [(i, section_count - 1 - i) for i in range(section_count)]
    row_count = by_head.shape[1]
    split = row_count - row_count * 3 // 10 // ROW_TILE * ROW_TILE
    last = head_count - 1
    sizes = chunk_sizes(last)
    firsts = [sum(sizes[:i]) for i in range(len(sizes))]
    pieces = [(slice(first, first + size), slice(None)) for first, size in zip(firsts, sizes)]
    pieces += [(slice(last, None), slice(0, split)), (slice(last, None), slice(split, None))]
    grad_rows, lengths = grad_out[0, 0], doc_lengths[0, 0]
    arrived = []
    for piece in pieces:
        packed, by_head = lax.optimization_barrier((by_head[piece], by_head))
        arrived.append(lax.ppermute(packed, "section", mirror))
    grads, bias, start_row = first_grads(*arrived[:2], grad_rows, lengths, head_count)
    bias_parts = [bias]
    for first, packed in zip(firsts[2:], arrived[2:]):
        grads, bias = chunk_grads(packed, grad_rows, start_row, first, grads)
        bias_parts.append(bias)
    early, late = arrived[-2:]
    query_early, sums, early_bias, mask = early_grads(
        early, grad_rows, start_row, last, bias_parts[-1]
    )
    query_late, added, bias_own = late_grads(early, late, grad_rows, mask, early_bias, bias_parts)
    bias_total = replica_sum(bias_own, "dp")
    grads = store_last((query_early, sums, query_late, added), grads)
    bias_grad = jnp.transpose(bias_total / lax.axis_size("dp"), (1, 0, 2))
    return (jnp.transpose(grads, (1, 0, 2))[None, None], bias_grad)


def solution(mesh):
    in_specs = (
        P("section", "dp", None, "tp", None),
        P("section", "dp", None, "tp"),
        P("section", "dp", None),
    )
    out_specs = (P("section", "dp", None, "tp", None), P("section", "tp", None))
    return jax.shard_map(body, mesh=mesh, in_specs=in_specs, out_specs=out_specs, check_vma=False)
```

time: 80.6 us -> 81.9 us (1.016)
  waiting for transfers between devices: 44.8 us -> 51 us
  starting transfers between devices: 13 us -> 10 us
  Pallas kernels: 14.6 us -> 13.5 us
    ppermute x6 -> x5, waiting for transfers between devices: 44.4 us -> 50.6 us  [body(): arrived.append(lax.ppermute(packed, 'section', mirror))]
    ppermute x6 -> x5, starting transfers between devices: 13 us -> 9.97 us  [body(): arrived.append(lax.ppermute(packed, 'section', mirror))]
    pallas_call x5 -> x3, Pallas kernels: 13.3 us -> 12.3 us  [the longest x1 9.11 us: first_grads(): pl.pallas_call(first_kernel, grid=(chunk_heads,), in_specs=[SMEM_SPEC, VM...]
    slice x6 -> x5, local copies, waits for them, and re-layouts: 6.49 us -> 5.71 us  [body(): packed, by_head = lax.optimization_barrier((by_head[piece], by_head))]
  transfers between devices with their start and end apart: 7 -> 6, of which waited for: 2 -> 2; matrix products, arithmetic and copies ran while one was open for 5% -> 4% of each run, Pallas kernels for 17% -> 16%
where the time goes in v5:
time: 81.9 us; the launch traced here: 81.6 us
  waiting for transfers between devices  51 us (62%)
  Pallas kernels  13.5 us (16%)
  starting transfers between devices  10 us (12%)
  local copies, waits for them, and re-layouts  5.72 us (7%)
    ppermute x5, waiting for transfers between devices, body(): arrived.append(lax.ppermute(packed, 'section', mirror))  50.6 us
    ppermute x5, starting transfers between devices, body(): arrived.append(lax.ppermute(packed, 'section', mirror))  9.97 us
    pallas_call x1, Pallas kernels, first_grads(): pl.pallas_call(first_kernel, grid=(chunk_heads,), in_specs=[SMEM_SPEC, VM...  9.11 us
    slice x5, local copies, waits for them, and re-layouts, body(): packed, by_head = lax.optimization_barrier((by_head[piece], by_head))  5.71 us
    pallas_call x1, Pallas kernels, chunk_grads(): pl.pallas_call(functools.partial(chunk_kernel, first_head=first_head), gr...  2.38 us
  transfers between devices with their start and end apart: 6, of which 2 were waited for; matrix products, arithmetic and copies ran while one was open for 4% of the time, Pallas kernels for 16%

profile of v5, /device:TPU:0, one launch (start us, length us, event | category | flops | bytes accessed | tf_op | source)
XLA Modules:
  0.0 81.6 jit_solution(18424275703978338501)
XLA Ops:
  0.6 0.0 copy-start
  0.6 0.0 copy-start.1
  0.6 1.1 %slice.20 = bf16[1,320,384]{2,1,0:T(8,128)(2,1)S(1)} slice(bf16[12,320,384]{2,1,0:T(8,128)(2,1)} %bitcast.16), slice={[0:1], [0:320], [0:384]} | slice | bytes 491520 | tf_op jit(solution)/shard_map/slice | solution.py:319
  1.7 1.7 %slice.16 = bf16[8,320,384]{2,1,0:T(8,128)(2,1)S(1)} slice(bf16[12,320,384]{2,1,0:T(8,128)(2,1)} %bitcast.17), slice={[1:9], [0:320], [0:384]} | slice | bytes 3932160 | tf_op jit(solution)/shard_map/slice | solution.py:319
  3.5 4.0 %collective-permute-start.2 = (bf16[8,320,384]{2,1,0:T(8,128)(2,1)S(1)}, bf16[8,320,384]{2,1,0:T(8,128)(2,1)S(1)}, u32[]{:S(2)}, u32[]{:S(2)}) collective-permute-start(bf16[8,320,384]{2,1,0:T(8,128)(2,1)S(1)} %slice.16), channel_id=1, source_target_pairs={{0,24},{8,16},{16,8},{24,0},{1,25},{9,17},{17,9},{25,1},{2,26},{10... | collective-permute-start | bytes 5898248 | tf_op jit(solution)/shard_map/ppermute | solution.py:320
  7.4 1.1 %slice.17 = bf16[2,320,384]{2,1,0:T(8,128)(2,1)S(1)} slice(bf16[12,320,384]{2,1,0:T(8,128)(2,1)} %bitcast.18), slice={[9:11], [0:320], [0:384]} | slice | bytes 983040 | tf_op jit(solution)/shard_map/slice | solution.py:319
  8.5 0.1 collective-permute-start.3
  8.6 2.9 %collective-permute-start.1 = (bf16[1,320,384]{2,1,0:T(8,128)(2,1)S(1)}, bf16[1,320,384]{2,1,0:T(8,128)(2,1)S(1)}, u32[]{:S(2)}, u32[]{:S(2)}) collective-permute-start(bf16[1,320,384]{2,1,0:T(8,128)(2,1)S(1)} %slice.20), channel_id=1, source_target_pairs={{0,24},{8,16},{16,8},{24,0},{1,25},{9,17},{17,9},{25,1},{2,26},{10... | collective-permute-start | bytes 737288 | tf_op jit(solution)/shard_map/ppermute | solution.py:320
  11.5 0.9 %slice.18 = bf16[1,224,384]{2,1,0:T(8,128)(2,1)S(1)} slice(bf16[12,320,384]{2,1,0:T(8,128)(2,1)} %bitcast.19), slice={[11:12], [0:224], [0:384]} | slice | bytes 344064 | tf_op jit(solution)/shard_map/slice | solution.py:319
  12.5 0.1 collective-permute-start
  12.6 0.9 %slice.19 = bf16[1,96,384]{2,1,0:T(8,128)(2,1)S(1)} slice(bf16[12,320,384]{2,1,0:T(8,128)(2,1)} %bitcast.20), slice={[11:12], [224:320], [0:384]} | slice | bytes 147456 | tf_op jit(solution)/shard_map/slice | solution.py:319
  13.5 2.8 %collective-permute-start.4 = (bf16[1,96,384]{2,1,0:T(8,128)(2,1)S(1)}, bf16[1,96,384]{2,1,0:T(8,128)(2,1)S(1)}, u32[]{:S(2)}, u32[]{:S(2)}) collective-permute-start(bf16[1,96,384]{2,1,0:T(8,128)(2,1)S(1)} %slice.19), channel_id=1, source_target_pairs={{0,24},{8,16},{16,8},{24,0},{1,25},{9,17},{17,9},{25,1},{2,26},{10... | collective-permute-start | bytes 221192 | tf_op jit(solution)/shard_map/ppermute | solution.py:320
  16.3 50.6 %collective-permute-done.1.first_ref = bf16[1,320,384]{2,1,0:T(8,128)(2,1)S(1)} collective-permute-done((bf16[1,320,384]{2,1,0:T(8,128)(2,1)S(1)}, bf16[1,320,384]{2,1,0:T(8,128)(2,1)S(1)}, u32[]{:S(2)}, u32[]{:S(2)}) %collective-permute-start.1) | collective-permute-done | bytes 245792 | tf_op jit(solution)/shard_map/ppermute | solution.py:320
  66.9 0.0 collective-permute-done.2.rest_ref
  66.9 0.0 copy-done
  66.9 0.0 copy-done.1
  66.9 9.1 %first_grads.1 = (bf16[12,320,384]{2,1,0:T(8,128)(2,1)}, f32[9,1,384]{2,1,0:T(1,128)S(1)}, s32[1,320]{1,0:T(1,128)S(1)}) custom-call(s32[8]{0:T(128)S(1)} %bitcast.14, bf16[1,320,384]{2,1,0:T(8,128)(2,1)S(1)} %collective-permute-done.1.first_ref, bf16[8,320,384]{2,1,0:T(8,128)(2,1)S(1)} %collective-permute-done.2.rest_ref, bf16[320,1536]{1,0:T(8,128)(2,1)S(1)} %bitcast.10), custom_call_target="tpu_custom_call" | custom-call | tf_op jit(solution)/shard_map/first_grads/pallas_call | solution.py:211
  76.0 0.0 collective-permute-done.3.packed_ref
  76.0 2.4 %shard_map.50 = (bf16[12,320,384]{2,1,0:T(8,128)(2,1)}, f32[2,1,384]{2,1,0:T(1,128)S(1)}) custom-call(bf16[2,320,384]{2,1,0:T(8,128)(2,1)S(1)} %collective-permute-done.3.packed_ref, bf16[320,1536]{1,0:T(8,128)(2,1)S(1)} %bitcast.11, s32[1,320]{1,0:T(1,128)S(1)} %get-tuple-element.29.start_ref, ...), custom_call_target="tpu_custom_call", output_to_operand_aliasing={{0}: (3, {})} | custom-call | tf_op jit(solution)/shard_map/pallas_call | solution.py:225
  78.4 0.0 collective-permute-done.early_ref
  78.4 0.7 early_grads.1
  79.2 0.0 collective-permute-done.4.late_ref
  79.2 0.5 late_grads.1
  79.7 0.1 collective-permute-start.5
  79.8 0.8 store_last.1
  80.6 0.4 collective-permute-done.5
  81.0 0.6 multiply_bitcast_fusion
Async XLA Ops:
  0.6 66.3 %copy-start = (bf16[1,1,320,1536]{3,2,1,0:T(8,128)(2,1)S(1)}, bf16[1,1,320,1536]{3,2,1,0:T(8,128)(2,1)}, u32[]{:S(2)}) copy-start(bf16[1,1,320,1536]{3,2,1,0:T(8,128)(2,1)} %param.4) | copy-start | bytes 2949124
  0.6 66.3 %copy-start.1 = (s32[1,1,8]{2,1,0:T(1,128)S(1)}, s32[1,1,8]{2,1,0:T(1,128)}, u32[]{:S(2)}) copy-start(s32[1,1,8]{2,1,0:T(1,128)} %param.5) | copy-start | bytes 100
  3.5 63.5 %collective-permute-start.2 = (bf16[8,320,384]{2,1,0:T(8,128)(2,1)S(1)}, bf16[8,320,384]{2,1,0:T(8,128)(2,1)S(1)}, u32[]{:S(2)}, u32[]{:S(2)}) collective-permute-start(bf16[8,320,384]{2,1,0:T(8,128)(2,1)S(1)} %slice.16), channel_id=1, source_target_pairs={{0,24},{8,16},{16,8},{24,0},{1,25},{9,17},{17,9},{25,1},{2,26},{10... | collective-permute-start | bytes 5898248 | tf_op jit(solution)/shard_map/ppermute | solution.py:320
  8.5 67.5 %collective-permute-start.3 = (bf16[2,320,384]{2,1,0:T(8,128)(2,1)S(1)}, bf16[2,320,384]{2,1,0:T(8,128)(2,1)S(1)}, u32[]{:S(2)}, u32[]{:S(2)}) collective-permute-start(bf16[2,320,384]{2,1,0:T(8,128)(2,1)S(1)} %slice.17), channel_id=1, source_target_pairs={{0,24},{8,16},{16,8},{24,0},{1,25},{9,17},{17,9},{25,1},{2,26},{10... | collective-permute-start | bytes 1474568 | tf_op jit(solution)/shard_map/ppermute | solution.py:320
  8.6 58.3 %collective-permute-start.1 = (bf16[1,320,384]{2,1,0:T(8,128)(2,1)S(1)}, bf16[1,320,384]{2,1,0:T(8,128)(2,1)S(1)}, u32[]{:S(2)}, u32[]{:S(2)}) collective-permute-start(bf16[1,320,384]{2,1,0:T(8,128)(2,1)S(1)} %slice.20), channel_id=1, source_target_pairs={{0,24},{8,16},{16,8},{24,0},{1,25},{9,17},{17,9},{25,1},{2,26},{10... | collective-permute-start | bytes 737288 | tf_op jit(solution)/shard_map/ppermute | solution.py:320
  12.5 66.0 %collective-permute-start = (bf16[1,224,384]{2,1,0:T(8,128)(2,1)S(1)}, bf16[1,224,384]{2,1,0:T(8,128)(2,1)S(1)}, u32[]{:S(2)}, u32[]{:S(2)}) collective-permute-start(bf16[1,224,384]{2,1,0:T(8,128)(2,1)S(1)} %slice.18), channel_id=1, source_target_pairs={{0,24},{8,16},{16,8},{24,0},{1,25},{9,17},{17,9},{25,1},{2,26},{10... | collective-permute-start | bytes 516104 | tf_op jit(solution)/shard_map/ppermute | solution.py:320
  13.5 65.7 %collective-permute-start.4 = (bf16[1,96,384]{2,1,0:T(8,128)(2,1)S(1)}, bf16[1,96,384]{2,1,0:T(8,128)(2,1)S(1)}, u32[]{:S(2)}, u32[]{:S(2)}) collective-permute-start(bf16[1,96,384]{2,1,0:T(8,128)(2,1)S(1)} %slice.19), channel_id=1, source_target_pairs={{0,24},{8,16},{16,8},{24,0},{1,25},{9,17},{17,9},{25,1},{2,26},{10... | collective-permute-start | bytes 221192 | tf_op jit(solution)/shard_map/ppermute | solution.py:320
  79.7 1.3 %collective-permute-start.5 = (f32[12,1,384]{2,1,0:T(1,128)S(1)}, f32[12,1,384]{2,1,0:T(1,128)S(1)}, u32[]{:S(2)}, u32[]{:S(2)}) collective-permute-start(f32[12,1,384]{2,1,0:T(1,128)S(1)} %get-tuple-element.43), channel_id=1, source_target_pairs={{0,1},{1,0},{2,3},{3,2},{4,5},{5,4},{6,7},{7,6},{8,9},{9,8},{10,11... | collective-permute-start | bytes 55304 | tf_op jit(solution)/shard_map/ppermute | solution.py:299

commit v6 on v5

--- a/solution.py
+++ b/solution.py
@@ -285,6 +285,31 @@
     )(*map(in_vmem, parts), grads)
 
 
+def cut_kernel(source_ref, *refs, at):
+    out_ref, semaphore = refs[-2:]
+    window = tuple(pl.ds(start, size) for start, size in zip(at, out_ref.shape))
+    copy = pltpu.make_async_copy(source_ref.at[window], out_ref, semaphore)
+    copy.start()
+    copy.wait()
+
+
+def cut(source, at, shape, after):
+    operands = [pltpu.with_memory_space_constraint(source, pltpu.HBM)]
+    in_specs = [pl.BlockSpec(memory_space=pltpu.HBM)]
+    if after is not None:
+        operands.append(after)
+        in_specs.append(ANY_SPEC)
+    return pl.pallas_call(
+        functools.partial(cut_kernel, at=at),
+        in_specs=in_specs,
+        out_specs=VMEM_SPEC,
+        out_shape=pltpu.VMEM(shape, source.dtype),
+        scratch_shapes=[pltpu.SemaphoreType.DMA],
+        compiler_params=pltpu.CompilerParams(vmem_limit_bytes=KERNEL_VMEM),
+        name="cut",
+    )(*operands)
+
+
 def chunk_sizes(head_count):
     tail = min(2, head_count // 2)
     return [1, head_count - 1 - tail, tail]
@@ -311,13 +336,15 @@
     last = head_count - 1
     sizes = chunk_sizes(last)
     firsts = [sum(sizes[:i]) for i in range(len(sizes))]
-    pieces = [(slice(first, first + size), slice(None)) for first, size in zip(firsts, sizes)]
-    pieces += [(slice(last, None), slice(0, split)), (slice(last, None), slice(split, None))]
+    pieces = [(first, size, 0, row_count) for first, size in zip(firsts, sizes)]
+    pieces += [(last, 1, 0, split), (last, 1, split, row_count - split)]
     grad_rows, lengths = grad_out[0, 0], doc_lengths[0, 0]
     arrived = []
-    for piece in pieces:
-        packed, by_head = lax.optimization_barrier((by_head[piece], by_head))
+    packed = None
+    for head, heads, row, rows in pieces:
+        packed = cut(by_head, (head, row, 0), (heads, rows, by_head.shape[2]), packed)
         arrived.append(lax.ppermute(packed, "section", mirror))
+    grad_rows = cut(grad_rows, (0, 0), grad_rows.shape, packed)
     grads, bias, start_row = first_grads(*arrived[:2], grad_rows, lengths, head_count)
     bias_parts = [bias]
     for first, packed in zip(firsts[2:], arrived[2:]):

time: 81.9 us -> 81.7 us (level)
  Pallas kernels: 13.5 us -> 20.1 us
  local copies, waits for them, and re-layouts: 5.72 us -> 0.01 us
  waiting for transfers between devices: 51 us -> 49.7 us
    pallas_call x0 -> x6, Pallas kernels: none -> 6.58 us  [cut(): pl.pallas_call(functools.partial(cut_kernel, at=at), in_specs=in_specs, o...]
    slice x5 -> x0, local copies, waits for them, and re-layouts: 5.71 us -> none  [body(): packed, by_head = lax.optimization_barrier((by_head[piece], by_head))]
    ppermute x5, waiting for transfers between devices: 50.6 us -> 49.3 us  [body(): arrived.append(lax.ppermute(packed, 'section', mirror))]
  transfers between devices with their start and end apart: 6 -> 6, of which waited for: 2 -> 2; matrix products, arithmetic and copies ran while one was open for 4% -> 0% of each run, Pallas kernels for 16% -> 21%
where the time goes in v6:
time: 81.7 us; the launch traced here: 81.3 us
  waiting for transfers between devices  49.7 us (61%)
  Pallas kernels  20.1 us (25%)
  starting transfers between devices  10.1 us (12%)
    ppermute x5, waiting for transfers between devices, body(): arrived.append(lax.ppermute(packed, 'section', mirror))  49.3 us
    ppermute x5, starting transfers between devices, body(): arrived.append(lax.ppermute(packed, 'section', mirror))  10 us
    pallas_call x1, Pallas kernels, first_grads(): pl.pallas_call(first_kernel, grid=(chunk_heads,), in_specs=[SMEM_SPEC, VM...  9.12 us
    pallas_call x6, Pallas kernels, cut(): pl.pallas_call(functools.partial(cut_kernel, at=at), in_specs=in_specs, o...  6.58 us
    pallas_call x1, Pallas kernels, chunk_grads(): pl.pallas_call(functools.partial(chunk_kernel, first_head=first_head), gr...  2.38 us
  transfers between devices with their start and end apart: 6, of which 2 were waited for; matrix products, arithmetic and copies ran while one was open for 0% of the time, Pallas kernels for 21%

profile of v6, /device:TPU:0, one launch (start us, length us, event | category | flops | bytes accessed | tf_op | source)
XLA Modules:
  0.0 81.3 jit_solution(10918480241420100740)
XLA Ops:
  0.6 1.0 %cut.6.refs_0_ = bf16[1,320,384]{2,1,0:T(8,128)(2,1)S(1)} custom-call(bf16[12,320,384]{2,1,0:T(8,128)(2,1)} %bitcast.11), custom_call_target="tpu_custom_call" | custom-call | tf_op jit(solution)/shard_map/cut/pallas_call | solution.py:302
  1.6 1.6 %cut.7.refs_0_ = bf16[8,320,384]{2,1,0:T(8,128)(2,1)S(1)} custom-call(bf16[12,320,384]{2,1,0:T(8,128)(2,1)} %bitcast.12, bf16[1,320,384]{2,1,0:T(8,128)(2,1)S(1)} %cut.6.refs_0_), custom_call_target="tpu_custom_call" | custom-call | tf_op jit(solution)/shard_map/cut/pallas_call | solution.py:302
  3.2 4.0 %collective-permute-start.2 = (bf16[8,320,384]{2,1,0:T(8,128)(2,1)S(1)}, bf16[8,320,384]{2,1,0:T(8,128)(2,1)S(1)}, u32[]{:S(2)}, u32[]{:S(2)}) collective-permute-start(bf16[8,320,384]{2,1,0:T(8,128)(2,1)S(1)} %cut.7.refs_0_), channel_id=1, source_target_pairs={{0,24},{8,16},{16,8},{24,0},{1,25},{9,17},{17,9},{25,1},{2,26},{10... | collective-permute-start | bytes 5898248 | tf_op jit(solution)/shard_map/ppermute | solution.py:346
  7.1 1.0 %cut.8.refs_0_ = bf16[2,320,384]{2,1,0:T(8,128)(2,1)S(1)} custom-call(bf16[12,320,384]{2,1,0:T(8,128)(2,1)} %bitcast.13, bf16[8,320,384]{2,1,0:T(8,128)(2,1)S(1)} %cut.7.refs_0_), custom_call_target="tpu_custom_call" | custom-call | tf_op jit(solution)/shard_map/cut/pallas_call | solution.py:302
  8.2 0.1 collective-permute-start.3
  8.3 2.9 %collective-permute-start.1 = (bf16[1,320,384]{2,1,0:T(8,128)(2,1)S(1)}, bf16[1,320,384]{2,1,0:T(8,128)(2,1)S(1)}, u32[]{:S(2)}, u32[]{:S(2)}) collective-permute-start(bf16[1,320,384]{2,1,0:T(8,128)(2,1)S(1)} %cut.6.refs_0_), channel_id=1, source_target_pairs={{0,24},{8,16},{16,8},{24,0},{1,25},{9,17},{17,9},{25,1},{2,26},{10... | collective-permute-start | bytes 737288 | tf_op jit(solution)/shard_map/ppermute | solution.py:346
  11.2 0.9 %cut.9.refs_0_ = bf16[1,224,384]{2,1,0:T(8,128)(2,1)S(1)} custom-call(bf16[12,320,384]{2,1,0:T(8,128)(2,1)} %bitcast.14, bf16[2,320,384]{2,1,0:T(8,128)(2,1)S(1)} %cut.8.refs_0_), custom_call_target="tpu_custom_call" | custom-call | tf_op jit(solution)/shard_map/cut/pallas_call | solution.py:302
  12.1 0.0 copy-start
  12.1 0.1 collective-permute-start
  12.3 0.9 %cut.10.refs_0_ = bf16[1,96,384]{2,1,0:T(8,128)(2,1)S(1)} custom-call(bf16[12,320,384]{2,1,0:T(8,128)(2,1)} %bitcast.15, bf16[1,224,384]{2,1,0:T(8,128)(2,1)S(1)} %cut.9.refs_0_), custom_call_target="tpu_custom_call" | custom-call | tf_op jit(solution)/shard_map/cut/pallas_call | solution.py:302
  13.2 2.9 %collective-permute-start.4 = (bf16[1,96,384]{2,1,0:T(8,128)(2,1)S(1)}, bf16[1,96,384]{2,1,0:T(8,128)(2,1)S(1)}, u32[]{:S(2)}, u32[]{:S(2)}) collective-permute-start(bf16[1,96,384]{2,1,0:T(8,128)(2,1)S(1)} %cut.10.refs_0_), channel_id=1, source_target_pairs={{0,24},{8,16},{16,8},{24,0},{1,25},{9,17},{17,9},{25,1},{2,26},{10... | collective-permute-start | bytes 221192 | tf_op jit(solution)/shard_map/ppermute | solution.py:346
  16.1 1.2 %cut.11.grad_ref = bf16[320,1536]{1,0:T(8,128)(2,1)S(1)} custom-call(bf16[320,1536]{1,0:T(8,128)(2,1)} %bitcast.17, bf16[1,96,384]{2,1,0:T(8,128)(2,1)S(1)} %cut.10.refs_0_), custom_call_target="tpu_custom_call" | custom-call | tf_op jit(solution)/shard_map/cut/pallas_call | solution.py:302
  17.3 49.3 %collective-permute-done.1.first_ref = bf16[1,320,384]{2,1,0:T(8,128)(2,1)S(1)} collective-permute-done((bf16[1,320,384]{2,1,0:T(8,128)(2,1)S(1)}, bf16[1,320,384]{2,1,0:T(8,128)(2,1)S(1)}, u32[]{:S(2)}, u32[]{:S(2)}) %collective-permute-start.1) | collective-permute-done | bytes 245792 | tf_op jit(solution)/shard_map/ppermute | solution.py:346
  66.6 0.0 collective-permute-done.2.rest_ref
  66.6 0.0 copy-done
  66.6 9.1 %first_grads.1 = (bf16[12,320,384]{2,1,0:T(8,128)(2,1)}, f32[9,1,384]{2,1,0:T(1,128)S(1)}, s32[1,320]{1,0:T(1,128)S(1)}) custom-call(s32[8]{0:T(128)S(1)} %bitcast.10, bf16[1,320,384]{2,1,0:T(8,128)(2,1)S(1)} %collective-permute-done.1.first_ref, bf16[8,320,384]{2,1,0:T(8,128)(2,1)S(1)} %collective-permute-done.2.rest_ref, bf16[320,1536]{1,0:T(8,128)(2,1)S(1)} %cut.11.grad_ref), custom_call_target="tpu_custom_call" | custom-call | tf_op jit(solution)/shard_map/first_grads/pallas_call | solution.py:211
  75.7 0.0 collective-permute-done.3.packed_ref
  75.7 2.4 %shard_map.50 = (bf16[12,320,384]{2,1,0:T(8,128)(2,1)}, f32[2,1,384]{2,1,0:T(1,128)S(1)}) custom-call(bf16[2,320,384]{2,1,0:T(8,128)(2,1)S(1)} %collective-permute-done.3.packed_ref, bf16[320,1536]{1,0:T(8,128)(2,1)S(1)} %cut.11.grad_ref, s32[1,320]{1,0:T(1,128)S(1)} %get-tuple-element.14.start_ref, ...), custom_call_target="tpu_custom_call", output_to_operand_aliasing={{0}: (3, {})} | custom-call | tf_op jit(solution)/shard_map/pallas_call | solution.py:225
  78.1 0.0 collective-permute-done.early_ref
  78.1 0.7 early_grads.1
  78.9 0.0 collective-permute-done.4.late_ref
  78.9 0.5 late_grads.1
  79.4 0.1 collective-permute-start.5
  79.5 0.8 store_last.1
  80.3 0.4 collective-permute-done.5
  80.7 0.6 multiply_bitcast_fusion
Async XLA Ops:
  3.2 63.5 %collective-permute-start.2 = (bf16[8,320,384]{2,1,0:T(8,128)(2,1)S(1)}, bf16[8,320,384]{2,1,0:T(8,128)(2,1)S(1)}, u32[]{:S(2)}, u32[]{:S(2)}) collective-permute-start(bf16[8,320,384]{2,1,0:T(8,128)(2,1)S(1)} %cut.7.refs_0_), channel_id=1, source_target_pairs={{0,24},{8,16},{16,8},{24,0},{1,25},{9,17},{17,9},{25,1},{2,26},{10... | collective-permute-start | bytes 5898248 | tf_op jit(solution)/shard_map/ppermute | solution.py:346
  8.2 67.6 %collective-permute-start.3 = (bf16[2,320,384]{2,1,0:T(8,128)(2,1)S(1)}, bf16[2,320,384]{2,1,0:T(8,128)(2,1)S(1)}, u32[]{:S(2)}, u32[]{:S(2)}) collective-permute-start(bf16[2,320,384]{2,1,0:T(8,128)(2,1)S(1)} %cut.8.refs_0_), channel_id=1, source_target_pairs={{0,24},{8,16},{16,8},{24,0},{1,25},{9,17},{17,9},{25,1},{2,26},{10... | collective-permute-start | bytes 1474568 | tf_op jit(solution)/shard_map/ppermute | solution.py:346
  8.3 58.3 %collective-permute-start.1 = (bf16[1,320,384]{2,1,0:T(8,128)(2,1)S(1)}, bf16[1,320,384]{2,1,0:T(8,128)(2,1)S(1)}, u32[]{:S(2)}, u32[]{:S(2)}) collective-permute-start(bf16[1,320,384]{2,1,0:T(8,128)(2,1)S(1)} %cut.6.refs_0_), channel_id=1, source_target_pairs={{0,24},{8,16},{16,8},{24,0},{1,25},{9,17},{17,9},{25,1},{2,26},{10... | collective-permute-start | bytes 737288 | tf_op jit(solution)/shard_map/ppermute | solution.py:346
  12.1 54.5 %copy-start = (s32[1,1,8]{2,1,0:T(1,128)S(1)}, s32[1,1,8]{2,1,0:T(1,128)}, u32[]{:S(2)}) copy-start(s32[1,1,8]{2,1,0:T(1,128)} %param.5) | copy-start | bytes 100
  12.1 66.0 %collective-permute-start = (bf16[1,224,384]{2,1,0:T(8,128)(2,1)S(1)}, bf16[1,224,384]{2,1,0:T(8,128)(2,1)S(1)}, u32[]{:S(2)}, u32[]{:S(2)}) collective-permute-start(bf16[1,224,384]{2,1,0:T(8,128)(2,1)S(1)} %cut.9.refs_0_), channel_id=1, source_target_pairs={{0,24},{8,16},{16,8},{24,0},{1,25},{9,17},{17,9},{25,1},{2,26},{10... | collective-permute-start | bytes 516104 | tf_op jit(solution)/shard_map/ppermute | solution.py:346
  13.2 65.7 %collective-permute-start.4 = (bf16[1,96,384]{2,1,0:T(8,128)(2,1)S(1)}, bf16[1,96,384]{2,1,0:T(8,128)(2,1)S(1)}, u32[]{:S(2)}, u32[]{:S(2)}) collective-permute-start(bf16[1,96,384]{2,1,0:T(8,128)(2,1)S(1)} %cut.10.refs_0_), channel_id=1, source_target_pairs={{0,24},{8,16},{16,8},{24,0},{1,25},{9,17},{17,9},{25,1},{2,26},{10... | collective-permute-start | bytes 221192 | tf_op jit(solution)/shard_map/ppermute | solution.py:346
  79.4 1.3 %collective-permute-start.5 = (f32[12,1,384]{2,1,0:T(1,128)S(1)}, f32[12,1,384]{2,1,0:T(1,128)S(1)}, u32[]{:S(2)}, u32[]{:S(2)}) collective-permute-start(f32[12,1,384]{2,1,0:T(1,128)S(1)} %get-tuple-element.25), channel_id=1, source_target_pairs={{0,1},{1,0},{2,3},{3,2},{4,5},{5,4},{6,7},{7,6},{8,9},{9,8},{10,11... | collective-permute-start | bytes 55304 | tf_op jit(solution)/shard_map/ppermute | solution.py:324

commit v7 on v6

--- a/solution.py
+++ b/solution.py
@@ -52,10 +52,11 @@
     row_top = jnp.max(masked, axis=0, keepdims=True)
     raised = jnp.exp2((masked - row_top) * (inv_root * math.log2(math.e)))
     prob = raised * (1.0 / jnp.sum(raised, axis=0, keepdims=True))
+    prob_low = prob.astype(jnp.bfloat16)
     prob_grad = dot(values_in, grad_rows, ROWS_BY_ROWS)
-    row_dot = jnp.sum(prob * prob_grad, axis=0, keepdims=True)
+    row_dot = jnp.sum(prob_low.astype(jnp.float32) * prob_grad, axis=0, keepdims=True)
     score_grad = (prob * inv_root) * (prob_grad - row_dot)
-    return prob.astype(jnp.bfloat16), score_grad.astype(jnp.bfloat16)
+    return prob_low, score_grad.astype(jnp.bfloat16)
 
 
 def head_grads(packed, grad_rows, doc_start):

time: 81.7 us -> 82.1 us (level)
  no operation moved by 1% of the time
where the time goes in v7:
time: 82.1 us; the launch traced here: 81.8 us
  waiting for transfers between devices  49.7 us (61%)
  Pallas kernels  20.6 us (25%)
  starting transfers between devices  10.1 us (12%)
    ppermute x5, waiting for transfers between devices, body(): arrived.append(lax.ppermute(packed, 'section', mirror))  49.3 us
    ppermute x5, starting transfers between devices, body(): arrived.append(lax.ppermute(packed, 'section', mirror))  10 us
    pallas_call x1, Pallas kernels, first_grads(): pl.pallas_call(first_kernel, grid=(chunk_heads,), in_specs=[SMEM_SPEC, VM...  9.49 us
    pallas_call x6, Pallas kernels, cut(): pl.pallas_call(functools.partial(cut_kernel, at=at), in_specs=in_specs, o...  6.58 us
    pallas_call x1, Pallas kernels, chunk_grads(): pl.pallas_call(functools.partial(chunk_kernel, first_head=first_head), gr...  2.45 us
  transfers between devices with their start and end apart: 6, of which 2 were waited for; matrix products, arithmetic and copies ran while one was open for 0% of the time, Pallas kernels for 21%

profile of v7, /device:TPU:0, one launch (start us, length us, event | category | flops | bytes accessed | tf_op | source)
XLA Modules:
  0.0 81.8 jit_solution(4787008376274217110)
XLA Ops:
  0.6 1.0 %cut.6.refs_0_ = bf16[1,320,384]{2,1,0:T(8,128)(2,1)S(1)} custom-call(bf16[12,320,384]{2,1,0:T(8,128)(2,1)} %bitcast.11), custom_call_target="tpu_custom_call" | custom-call | tf_op jit(solution)/shard_map/cut/pallas_call | solution.py:303
  1.6 1.6 %cut.7.refs_0_ = bf16[8,320,384]{2,1,0:T(8,128)(2,1)S(1)} custom-call(bf16[12,320,384]{2,1,0:T(8,128)(2,1)} %bitcast.12, bf16[1,320,384]{2,1,0:T(8,128)(2,1)S(1)} %cut.6.refs_0_), custom_call_target="tpu_custom_call" | custom-call | tf_op jit(solution)/shard_map/cut/pallas_call | solution.py:303
  3.2 4.0 %collective-permute-start.2 = (bf16[8,320,384]{2,1,0:T(8,128)(2,1)S(1)}, bf16[8,320,384]{2,1,0:T(8,128)(2,1)S(1)}, u32[]{:S(2)}, u32[]{:S(2)}) collective-permute-start(bf16[8,320,384]{2,1,0:T(8,128)(2,1)S(1)} %cut.7.refs_0_), channel_id=1, source_target_pairs={{0,24},{8,16},{16,8},{24,0},{1,25},{9,17},{17,9},{25,1},{2,26},{10... | collective-permute-start | bytes 5898248 | tf_op jit(solution)/shard_map/ppermute | solution.py:347
  7.1 1.0 %cut.8.refs_0_ = bf16[2,320,384]{2,1,0:T(8,128)(2,1)S(1)} custom-call(bf16[12,320,384]{2,1,0:T(8,128)(2,1)} %bitcast.13, bf16[8,320,384]{2,1,0:T(8,128)(2,1)S(1)} %cut.7.refs_0_), custom_call_target="tpu_custom_call" | custom-call | tf_op jit(solution)/shard_map/cut/pallas_call | solution.py:303
  8.2 0.1 collective-permute-start.3
  8.3 2.9 %collective-permute-start.1 = (bf16[1,320,384]{2,1,0:T(8,128)(2,1)S(1)}, bf16[1,320,384]{2,1,0:T(8,128)(2,1)S(1)}, u32[]{:S(2)}, u32[]{:S(2)}) collective-permute-start(bf16[1,320,384]{2,1,0:T(8,128)(2,1)S(1)} %cut.6.refs_0_), channel_id=1, source_target_pairs={{0,24},{8,16},{16,8},{24,0},{1,25},{9,17},{17,9},{25,1},{2,26},{10... | collective-permute-start | bytes 737288 | tf_op jit(solution)/shard_map/ppermute | solution.py:347
  11.2 0.9 %cut.9.refs_0_ = bf16[1,224,384]{2,1,0:T(8,128)(2,1)S(1)} custom-call(bf16[12,320,384]{2,1,0:T(8,128)(2,1)} %bitcast.14, bf16[2,320,384]{2,1,0:T(8,128)(2,1)S(1)} %cut.8.refs_0_), custom_call_target="tpu_custom_call" | custom-call | tf_op jit(solution)/shard_map/cut/pallas_call | solution.py:303
  12.1 0.0 copy-start
  12.1 0.1 collective-permute-start
  12.3 0.9 %cut.10.refs_0_ = bf16[1,96,384]{2,1,0:T(8,128)(2,1)S(1)} custom-call(bf16[12,320,384]{2,1,0:T(8,128)(2,1)} %bitcast.15, bf16[1,224,384]{2,1,0:T(8,128)(2,1)S(1)} %cut.9.refs_0_), custom_call_target="tpu_custom_call" | custom-call | tf_op jit(solution)/shard_map/cut/pallas_call | solution.py:303
  13.2 2.9 %collective-permute-start.4 = (bf16[1,96,384]{2,1,0:T(8,128)(2,1)S(1)}, bf16[1,96,384]{2,1,0:T(8,128)(2,1)S(1)}, u32[]{:S(2)}, u32[]{:S(2)}) collective-permute-start(bf16[1,96,384]{2,1,0:T(8,128)(2,1)S(1)} %cut.10.refs_0_), channel_id=1, source_target_pairs={{0,24},{8,16},{16,8},{24,0},{1,25},{9,17},{17,9},{25,1},{2,26},{10... | collective-permute-start | bytes 221192 | tf_op jit(solution)/shard_map/ppermute | solution.py:347
  16.1 1.2 %cut.11.grad_ref = bf16[320,1536]{1,0:T(8,128)(2,1)S(1)} custom-call(bf16[320,1536]{1,0:T(8,128)(2,1)} %bitcast.17, bf16[1,96,384]{2,1,0:T(8,128)(2,1)S(1)} %cut.10.refs_0_), custom_call_target="tpu_custom_call" | custom-call | tf_op jit(solution)/shard_map/cut/pallas_call | solution.py:303
  17.3 49.3 %collective-permute-done.1.first_ref = bf16[1,320,384]{2,1,0:T(8,128)(2,1)S(1)} collective-permute-done((bf16[1,320,384]{2,1,0:T(8,128)(2,1)S(1)}, bf16[1,320,384]{2,1,0:T(8,128)(2,1)S(1)}, u32[]{:S(2)}, u32[]{:S(2)}) %collective-permute-start.1) | collective-permute-done | bytes 245792 | tf_op jit(solution)/shard_map/ppermute | solution.py:347
  66.6 0.0 collective-permute-done.2.rest_ref
  66.6 0.0 copy-done
  66.6 9.5 %first_grads.1 = (bf16[12,320,384]{2,1,0:T(8,128)(2,1)}, f32[9,1,384]{2,1,0:T(1,128)S(1)}, s32[1,320]{1,0:T(1,128)S(1)}) custom-call(s32[8]{0:T(128)S(1)} %bitcast.10, bf16[1,320,384]{2,1,0:T(8,128)(2,1)S(1)} %collective-permute-done.1.first_ref, bf16[8,320,384]{2,1,0:T(8,128)(2,1)S(1)} %collective-permute-done.2.rest_ref, bf16[320,1536]{1,0:T(8,128)(2,1)S(1)} %cut.11.grad_ref), custom_call_target="tpu_custom_call" | custom-call | tf_op jit(solution)/shard_map/first_grads/pallas_call | solution.py:212
  76.1 0.0 collective-permute-done.3.packed_ref
  76.1 2.4 %shard_map.50 = (bf16[12,320,384]{2,1,0:T(8,128)(2,1)}, f32[2,1,384]{2,1,0:T(1,128)S(1)}) custom-call(bf16[2,320,384]{2,1,0:T(8,128)(2,1)S(1)} %collective-permute-done.3.packed_ref, bf16[320,1536]{1,0:T(8,128)(2,1)S(1)} %cut.11.grad_ref, s32[1,320]{1,0:T(1,128)S(1)} %get-tuple-element.14.start_ref, ...), custom_call_target="tpu_custom_call", output_to_operand_aliasing={{0}: (3, {})} | custom-call | tf_op jit(solution)/shard_map/pallas_call | solution.py:226
  78.6 0.0 collective-permute-done.early_ref
  78.6 0.7 early_grads.1
  79.3 0.0 collective-permute-done.4.late_ref
  79.3 0.5 late_grads.1
  79.9 0.1 collective-permute-start.5
  80.0 0.8 store_last.1
  80.7 0.4 collective-permute-done.5
  81.1 0.6 multiply_bitcast_fusion
Async XLA Ops:
  3.2 63.5 %collective-permute-start.2 = (bf16[8,320,384]{2,1,0:T(8,128)(2,1)S(1)}, bf16[8,320,384]{2,1,0:T(8,128)(2,1)S(1)}, u32[]{:S(2)}, u32[]{:S(2)}) collective-permute-start(bf16[8,320,384]{2,1,0:T(8,128)(2,1)S(1)} %cut.7.refs_0_), channel_id=1, source_target_pairs={{0,24},{8,16},{16,8},{24,0},{1,25},{9,17},{17,9},{25,1},{2,26},{10... | collective-permute-start | bytes 5898248 | tf_op jit(solution)/shard_map/ppermute | solution.py:347
  8.2 67.9 %collective-permute-start.3 = (bf16[2,320,384]{2,1,0:T(8,128)(2,1)S(1)}, bf16[2,320,384]{2,1,0:T(8,128)(2,1)S(1)}, u32[]{:S(2)}, u32[]{:S(2)}) collective-permute-start(bf16[2,320,384]{2,1,0:T(8,128)(2,1)S(1)} %cut.8.refs_0_), channel_id=1, source_target_pairs={{0,24},{8,16},{16,8},{24,0},{1,25},{9,17},{17,9},{25,1},{2,26},{10... | collective-permute-start | bytes 1474568 | tf_op jit(solution)/shard_map/ppermute | solution.py:347
  8.3 58.3 %collective-permute-start.1 = (bf16[1,320,384]{2,1,0:T(8,128)(2,1)S(1)}, bf16[1,320,384]{2,1,0:T(8,128)(2,1)S(1)}, u32[]{:S(2)}, u32[]{:S(2)}) collective-permute-start(bf16[1,320,384]{2,1,0:T(8,128)(2,1)S(1)} %cut.6.refs_0_), channel_id=1, source_target_pairs={{0,24},{8,16},{16,8},{24,0},{1,25},{9,17},{17,9},{25,1},{2,26},{10... | collective-permute-start | bytes 737288 | tf_op jit(solution)/shard_map/ppermute | solution.py:347
  12.1 54.5 %copy-start = (s32[1,1,8]{2,1,0:T(1,128)S(1)}, s32[1,1,8]{2,1,0:T(1,128)}, u32[]{:S(2)}) copy-start(s32[1,1,8]{2,1,0:T(1,128)} %param.5) | copy-start | bytes 100
  12.1 66.4 %collective-permute-start = (bf16[1,224,384]{2,1,0:T(8,128)(2,1)S(1)}, bf16[1,224,384]{2,1,0:T(8,128)(2,1)S(1)}, u32[]{:S(2)}, u32[]{:S(2)}) collective-permute-start(bf16[1,224,384]{2,1,0:T(8,128)(2,1)S(1)} %cut.9.refs_0_), channel_id=1, source_target_pairs={{0,24},{8,16},{16,8},{24,0},{1,25},{9,17},{17,9},{25,1},{2,26},{10... | collective-permute-start | bytes 516104 | tf_op jit(solution)/shard_map/ppermute | solution.py:347
  13.2 66.1 %collective-permute-start.4 = (bf16[1,96,384]{2,1,0:T(8,128)(2,1)S(1)}, bf16[1,96,384]{2,1,0:T(8,128)(2,1)S(1)}, u32[]{:S(2)}, u32[]{:S(2)}) collective-permute-start(bf16[1,96,384]{2,1,0:T(8,128)(2,1)S(1)} %cut.10.refs_0_), channel_id=1, source_target_pairs={{0,24},{8,16},{16,8},{24,0},{1,25},{9,17},{17,9},{25,1},{2,26},{10... | collective-permute-start | bytes 221192 | tf_op jit(solution)/shard_map/ppermute | solution.py:347
  79.9 1.3 %collective-permute-start.5 = (f32[12,1,384]{2,1,0:T(1,128)S(1)}, f32[12,1,384]{2,1,0:T(1,128)S(1)}, u32[]{:S(2)}, u32[]{:S(2)}) collective-permute-start(f32[12,1,384]{2,1,0:T(1,128)S(1)} %get-tuple-element.25), channel_id=1, source_target_pairs={{0,1},{1,0},{2,3},{3,2},{4,5},{5,4},{6,7},{7,6},{8,9},{9,8},{10,11... | collective-permute-start | bytes 55304 | tf_op jit(solution)/shard_map/ppermute | solution.py:325

commit v8 on v6

--- a/solution.py
+++ b/solution.py
@@ -46,16 +46,25 @@
     return jnp.where((key_at >= doc_start) & (key_at <= query_at), 0.0, MASKED)
 
 
+def exponent_scale(head_size):
+    return math.log2(math.e) / math.sqrt(head_size)
+
+
+def low_weights(prob, prob_grad, head_size):
+    prob_low = prob.astype(jnp.bfloat16)
+    row_dot = jnp.sum(prob_low.astype(jnp.float32) * prob_grad, axis=0, keepdims=True)
+    score_grad = (prob * (1.0 / math.sqrt(head_size))) * (prob_grad - row_dot)
+    return prob_low, score_grad.astype(jnp.bfloat16)
+
+
 def tile_weights(queries, keys_in, values_in, grad_rows, mask):
-    inv_root = 1.0 / math.sqrt(queries.shape[1])
+    head_size = queries.shape[1]
     masked = dot(keys_in, queries, ROWS_BY_ROWS) + mask
     row_top = jnp.max(masked, axis=0, keepdims=True)
-    raised = jnp.exp2((masked - row_top) * (inv_root * math.log2(math.e)))
+    raised = jnp.exp2((masked - row_top) * exponent_scale(head_size))
     prob = raised * (1.0 / jnp.sum(raised, axis=0, keepdims=True))
     prob_grad = dot(values_in, grad_rows, ROWS_BY_ROWS)
-    row_dot = jnp.sum(prob * prob_grad, axis=0, keepdims=True)
-    score_grad = (prob * inv_root) * (prob_grad - row_dot)
-    return prob.astype(jnp.bfloat16), score_grad.astype(jnp.bfloat16)
+    return low_weights(prob, prob_grad, head_size)
 
 
 def head_grads(packed, grad_rows, doc_start):
@@ -77,7 +86,7 @@
         bias_ref[bias_head, :, span] = jnp.sum(grad, axis=0, keepdims=True)
 
 
-def chunk_kernel(packed_ref, grad_ref, start_ref, _, out_ref, bias_ref, *, first_head):
+def chunk_kernel(packed_ref, grad_ref, start_ref, _mask, _grads, out_ref, bias_ref, *, first_head):
     head_size = packed_ref.shape[2] // 3
     head = pl.program_id(0)
     grad_at = pl.multiple_of((first_head + head) * head_size, head_size)
@@ -108,7 +117,19 @@
     return jnp.sum(rows, axis=0, keepdims=True)
 
 
-def early_kernel(early_ref, grad_ref, start_ref, _, query_ref, sums_ref, bias_ref, mask_ref, *, head):
+def mask_kernel(start_ref, mask_ref):
+    key_count, query_count = mask_ref.shape
+    row_count = start_ref.shape[1]
+    first_query = row_count - query_count
+    mask_ref[...] = mask_rows(
+        start_ref[:, first_query:], first_query, row_count - key_count, key_count
+    )
+
+
+def early_kernel(
+    early_ref, late_query_ref, grad_ref, start_ref, mask_ref, _,
+    query_ref, sums_ref, bias_ref, raised_ref, prob_grad_ref, stats_ref, *, head
+):
     row_count, pack_width = early_ref.shape[1:]
     head_size = pack_width // 3
     queries, keys_in, values_in = split_pack(early_ref[0])
@@ -135,22 +156,45 @@
             sums_ref[tile, part * head_size : (part + 1) * head_size] = grad
         bias_ref[:, (part + 1) * head_size : (part + 2) * head_size] = sum(map(column_sum, grads))
     first_key = doc_start.shape[1] - mask_ref.shape[0]
-    mask_ref[...] = mask_rows(doc_start[:, row_count:], row_count, first_key, mask_ref.shape[0])
-
-
-def late_kernel(early_ref, late_ref, grad_ref, mask_ref, early_bias_ref, *refs):
+    late_grad = grad_ref[row_count:, head * head_size : (head + 1) * head_size]
+    masked = dot(keys_in[first_key:], late_query_ref[0], ROWS_BY_ROWS)
+    masked += mask_ref[: row_count - first_key]
+    row_top = jnp.max(masked, axis=0, keepdims=True)
+    raised = jnp.exp2((masked - row_top) * exponent_scale(head_size))
+    raised_ref[...] = raised
+    prob_grad_ref[...] = dot(values_in[first_key:], late_grad, ROWS_BY_ROWS)
+    stats_ref[0:1] = row_top
+    stats_ref[1:2] = column_sum(raised)
+
+
+def late_kernel(
+    early_ref, late_query_ref, late_ref, grad_ref, mask_ref, raised_ref, prob_grad_ref, stats_ref,
+    early_bias_ref, *refs
+):
     bias_parts, (query_ref, added_ref, bias_ref) = refs[:-3], refs[-3:]
     split = early_ref.shape[1]
-    first_key = split + late_ref.shape[1] - mask_ref.shape[0]
+    early_keys = raised_ref.shape[0]
+    first_key = split - early_keys
     head_size = early_ref.shape[2] // 3
     head = sum(part_ref.shape[0] for part_ref in bias_parts)
-    queries = late_ref[0, :, :head_size]
+    queries = late_query_ref[0]
     grad_rows = grad_ref[split:, head * head_size : (head + 1) * head_size]
-    keys_in, values_in = (
-        jnp.concatenate([early_ref[0, first_key:, span], late_ref[0, :, span]], axis=0)
-        for span in (slice(head_size, 2 * head_size), slice(2 * head_size, None))
-    )
-    prob_low, score_low = tile_weights(queries, keys_in, values_in, grad_rows, mask_ref[...])
+    late_keys = late_ref[0, :, :head_size]
+    scale = exponent_scale(head_size)
+    masked = dot(late_keys, queries, ROWS_BY_ROWS) + mask_ref[early_keys:]
+    early_top = stats_ref[0:1]
+    row_top = jnp.maximum(early_top, jnp.max(masked, axis=0, keepdims=True))
+    raised = jnp.exp2((masked - row_top) * scale)
+    lowered = jnp.exp2((early_top - row_top) * scale)
+    inverse = 1.0 / (stats_ref[1:2] * lowered + column_sum(raised))
+    prob = jnp.concatenate([raised_ref[...] * (lowered * inverse), raised * inverse], axis=0)
+    prob_grad = jnp.concatenate(
+        [prob_grad_ref[...], dot(late_ref[0, :, head_size:], grad_rows, ROWS_BY_ROWS)], axis=0
+    )
+    prob_low, score_low = low_weights(prob, prob_grad, head_size)
+    keys_in = jnp.concatenate(
+        [early_ref[0, first_key:, head_size : 2 * head_size], late_keys], axis=0
+    )
     query_grad = dot(score_low, keys_in, COLUMNS)
     key_grad = dot(score_low, queries, PLAIN)
     value_grad = dot(prob_low, grad_rows, PLAIN)
@@ -219,45 +263,63 @@
     )(lengths, in_vmem(first), in_vmem(rest), in_vmem(grad_rows))
 
 
-def chunk_grads(packed, grad_rows, start_row, first_head, previous):
+def chunk_grads(packed, grad_rows, start_row, mask, first_head, previous):
     chunk_heads, row_count, pack_width = packed.shape
     specs, shapes = grads_outs(chunk_heads, previous.shape[0], first_head, row_count, pack_width)
     return pl.pallas_call(
         functools.partial(chunk_kernel, first_head=first_head),
         grid=(chunk_heads,),
-        in_specs=[VMEM_SPEC, VMEM_SPEC, VMEM_SPEC, ANY_SPEC],
+        in_specs=[VMEM_SPEC] * 4 + [ANY_SPEC],
         out_specs=specs,
         out_shape=shapes,
-        input_output_aliases={3: 0},
-        compiler_params=pltpu.CompilerParams(vmem_limit_bytes=KERNEL_VMEM),
-    )(in_vmem(packed), in_vmem(grad_rows), in_vmem(start_row), previous)
-
-
-def early_grads(packed, grad_rows, start_row, head, after):
-    _, split, pack_width = packed.shape
-    row_count, head_size = grad_rows.shape[0], pack_width // 3
+        input_output_aliases={4: 0},
+        compiler_params=pltpu.CompilerParams(vmem_limit_bytes=KERNEL_VMEM),
+    )(*map(in_vmem, (packed, grad_rows, start_row, mask)), previous)
+
+
+def late_mask(start_row, split):
+    row_count = start_row.shape[1]
     longest = row_count // 2
     first_key = max(0, split + 1 - longest) // ROW_TILE * ROW_TILE
     return pl.pallas_call(
+        mask_kernel,
+        in_specs=[VMEM_SPEC],
+        out_specs=VMEM_SPEC,
+        out_shape=pltpu.VMEM((row_count - first_key, row_count - split), jnp.float32),
+        compiler_params=pltpu.CompilerParams(vmem_limit_bytes=KERNEL_VMEM),
+        name="late_mask",
+    )(in_vmem(start_row))
+
+
+def early_grads(packed, late_queries, grad_rows, start_row, mask, head, after):
+    _, split, pack_width = packed.shape
+    head_size = pack_width // 3
+    late_count = late_queries.shape[1]
+    early_keys = mask.shape[0] - late_count
+    operands = (packed, late_queries, grad_rows, start_row, mask, after)
+    shapes = (
+        ((split, head_size), jnp.bfloat16),
+        ((split, 2 * head_size), jnp.float32),
+        ((1, pack_width), jnp.float32),
+        ((early_keys, late_count), jnp.float32),
+        ((early_keys, late_count), jnp.float32),
+        ((2, late_count), jnp.float32),
+    )
+    return pl.pallas_call(
         functools.partial(early_kernel, head=head),
-        in_specs=[VMEM_SPEC] * 4,
-        out_specs=[VMEM_SPEC] * 4,
-        out_shape=[
-            pltpu.VMEM((split, head_size), jnp.bfloat16),
-            pltpu.VMEM((split, 2 * head_size), jnp.float32),
-            pltpu.VMEM((1, pack_width), jnp.float32),
-            pltpu.VMEM((row_count - first_key, row_count - split), jnp.float32),
-        ],
+        in_specs=[VMEM_SPEC] * len(operands),
+        out_specs=[VMEM_SPEC] * len(shapes),
+        out_shape=[pltpu.VMEM(*shape) for shape in shapes],
         compiler_params=pltpu.CompilerParams(vmem_limit_bytes=KERNEL_VMEM),
         name="early_grads",
-    )(*map(in_vmem, (packed, grad_rows, start_row, after)))
-
-
-def late_grads(early, late, grad_rows, mask, early_bias, bias_parts):
+    )(*map(in_vmem, operands))
+
+
+def late_grads(early, late_queries, late, grad_rows, mask, started, early_bias, bias_parts):
     head_count = 1 + sum(part.shape[0] for part in bias_parts)
     pack_width = early.shape[2]
     head_size = pack_width // 3
-    operands = [early, late, grad_rows, mask, early_bias, *bias_parts]
+    operands = [early, late_queries, late, grad_rows, mask, *started, early_bias, *bias_parts]
     return pl.pallas_call(
         late_kernel,
         in_specs=[VMEM_SPEC] * len(operands),
@@ -332,29 +394,41 @@
     section_count = lax.axis_size("section")
     mirror = [(i, section_count - 1 - i) for i in range(section_count)]
     row_count = by_head.shape[1]
-    split = row_count - row_count * 3 // 10 // ROW_TILE * ROW_TILE
+    split = row_count - TILE
     last = head_count - 1
     sizes = chunk_sizes(last)
     firsts = [sum(sizes[:i]) for i in range(len(sizes))]
-    pieces = [(first, size, 0, row_count) for first, size in zip(firsts, sizes)]
-    pieces += [(last, 1, 0, split), (last, 1, split, row_count - split)]
+    pack_width = by_head.shape[2]
+    head_size = pack_width // 3
+    late_count = row_count - split
+    pieces = [
+        ((first, 0, 0), (size, row_count, pack_width)) for first, size in zip(firsts, sizes)
+    ]
+    pieces += [
+        ((last, split, 0), (1, late_count, head_size)),
+        ((last, 0, 0), (1, split, pack_width)),
+        ((last, split, head_size), (1, late_count, pack_width - head_size)),
+    ]
     grad_rows, lengths = grad_out[0, 0], doc_lengths[0, 0]
     arrived = []
     packed = None
-    for head, heads, row, rows in pieces:
-        packed = cut(by_head, (head, row, 0), (heads, rows, by_head.shape[2]), packed)
+    for at, shape in pieces:
+        packed = cut(by_head, at, shape, packed)
         arrived.append(lax.ppermute(packed, "section", mirror))
     grad_rows = cut(grad_rows, (0, 0), grad_rows.shape, packed)
     grads, bias, start_row = first_grads(*arrived[:2], grad_rows, lengths, head_count)
+    mask = late_mask(start_row, split)
     bias_parts = [bias]
-    for first, packed in zip(firsts[2:], arrived[2:]):
-        grads, bias = chunk_grads(packed, grad_rows, start_row, first, grads)
+    for first, packed in zip(firsts[2:], arrived[2:-3]):
+        grads, bias = chunk_grads(packed, grad_rows, start_row, mask, first, grads)
         bias_parts.append(bias)
-    early, late = arrived[-2:]
-    query_early, sums, early_bias, mask = early_grads(
-        early, grad_rows, start_row, last, bias_parts[-1]
-    )
-    query_late, added, bias_own = late_grads(early, late, grad_rows, mask, early_bias, bias_parts)
+    late_queries, early, late = arrived[-3:]
+    query_early, sums, early_bias, *started = early_grads(
+        early, late_queries, grad_rows, start_row, mask, last, bias_parts[-1]
+    )
+    query_late, added, bias_own = late_grads(
+        early, late_queries, late, grad_rows, mask, started, early_bias, bias_parts
+    )
     bias_total = replica_sum(bias_own, "dp")
     grads = store_last((query_early, sums, query_late, added), grads)
     bias_grad = jnp.transpose(bias_total / lax.axis_size("dp"), (1, 0, 2))

time: 81.7 us -> 86.6 us (1.060)
  starting transfers between devices: 10.1 us -> 13 us
  Pallas kernels: 20.1 us -> 21.5 us
    ppermute x5 -> x6, starting transfers between devices: 10 us -> 13 us  [body(): arrived.append(lax.ppermute(packed, 'section', mirror))]
    pallas_call x6 -> x7, Pallas kernels: 6.58 us -> 7.29 us  [cut(): pl.pallas_call(functools.partial(cut_kernel, at=at), in_specs=in_specs, o...]
    ppermute x5 -> x6, waiting for transfers between devices: 49.3 us -> 49.8 us  [body(): arrived.append(lax.ppermute(packed, 'section', mirror))]
  transfers between devices with their start and end apart: 6 -> 7, of which waited for: 2 -> 2; matrix products, arithmetic and copies ran while one was open for 0% -> 0% of each run, Pallas kernels for 21% -> 21%
where the time goes in v8:
time: 86.6 us; the launch traced here: 86.2 us
  waiting for transfers between devices  50.2 us (58%)
  Pallas kernels  21.5 us (25%)
  starting transfers between devices  13 us (15%)
    ppermute x6, waiting for transfers between devices, body(): arrived.append(lax.ppermute(packed, 'section', mirror))  49.8 us
    ppermute x6, starting transfers between devices, body(): arrived.append(lax.ppermute(packed, 'section', mirror))  13 us
    pallas_call x1, Pallas kernels, first_grads(): pl.pallas_call(first_kernel, grid=(chunk_heads,), in_specs=[SMEM_SPEC, VM...  9.45 us
    pallas_call x7, Pallas kernels, cut(): pl.pallas_call(functools.partial(cut_kernel, at=at), in_specs=in_specs, o...  7.29 us
    pallas_call x1, Pallas kernels, chunk_grads(): pl.pallas_call(functools.partial(chunk_kernel, first_head=first_head), gr...  2.48 us
  transfers between devices with their start and end apart: 7, of which 2 were waited for; matrix products, arithmetic and copies ran while one was open for 0% of the time, Pallas kernels for 21%

profile of v8, /device:TPU:0, one launch (start us, length us, event | category | flops | bytes accessed | tf_op | source)
XLA Modules:
  0.0 86.2 jit_solution(14805310208200935213)
XLA Ops:
  0.6 1.0 %cut.7.refs_0_ = bf16[1,320,384]{2,1,0:T(8,128)(2,1)S(1)} custom-call(bf16[12,320,384]{2,1,0:T(8,128)(2,1)} %bitcast.11), custom_call_target="tpu_custom_call" | custom-call | tf_op jit(solution)/shard_map/cut/pallas_call | solution.py:364
  1.6 1.6 %cut.8.refs_0_ = bf16[8,320,384]{2,1,0:T(8,128)(2,1)S(1)} custom-call(bf16[12,320,384]{2,1,0:T(8,128)(2,1)} %bitcast.12, bf16[1,320,384]{2,1,0:T(8,128)(2,1)S(1)} %cut.7.refs_0_), custom_call_target="tpu_custom_call" | custom-call | tf_op jit(solution)/shard_map/cut/pallas_call | solution.py:364
  3.2 4.0 %collective-permute-start.3 = (bf16[8,320,384]{2,1,0:T(8,128)(2,1)S(1)}, bf16[8,320,384]{2,1,0:T(8,128)(2,1)S(1)}, u32[]{:S(2)}, u32[]{:S(2)}) collective-permute-start(bf16[8,320,384]{2,1,0:T(8,128)(2,1)S(1)} %cut.8.refs_0_), channel_id=1, source_target_pairs={{0,24},{8,16},{16,8},{24,0},{1,25},{9,17},{17,9},{25,1},{2,26},{10... | collective-permute-start | bytes 5898248 | tf_op jit(solution)/shard_map/ppermute | solution.py:417
  7.1 1.0 %cut.9.refs_0_ = bf16[2,320,384]{2,1,0:T(8,128)(2,1)S(1)} custom-call(bf16[12,320,384]{2,1,0:T(8,128)(2,1)} %bitcast.13, bf16[8,320,384]{2,1,0:T(8,128)(2,1)S(1)} %cut.8.refs_0_), custom_call_target="tpu_custom_call" | custom-call | tf_op jit(solution)/shard_map/cut/pallas_call | solution.py:364
  8.2 0.1 collective-permute-start.4
  8.3 2.9 %collective-permute-start.2 = (bf16[1,320,384]{2,1,0:T(8,128)(2,1)S(1)}, bf16[1,320,384]{2,1,0:T(8,128)(2,1)S(1)}, u32[]{:S(2)}, u32[]{:S(2)}) collective-permute-start(bf16[1,320,384]{2,1,0:T(8,128)(2,1)S(1)} %cut.7.refs_0_), channel_id=1, source_target_pairs={{0,24},{8,16},{16,8},{24,0},{1,25},{9,17},{17,9},{25,1},{2,26},{10... | collective-permute-start | bytes 737288 | tf_op jit(solution)/shard_map/ppermute | solution.py:417
  11.2 0.8 cut.10.refs_0_
  12.0 0.9 %cut.11.refs_0_ = bf16[1,192,384]{2,1,0:T(8,128)(2,1)S(1)} custom-call(bf16[12,320,384]{2,1,0:T(8,128)(2,1)} %bitcast.15, bf16[1,128,128]{2,1,0:T(8,128)(2,1)S(1)} %cut.10.refs_0_), custom_call_target="tpu_custom_call" | custom-call | tf_op jit(solution)/shard_map/cut/pallas_call | solution.py:364
  12.9 0.0 copy-start
  12.9 0.1 collective-permute-start
  13.0 0.8 cut.12.refs_0_
  13.9 2.9 %collective-permute-start.5 = (bf16[1,128,256]{2,1,0:T(8,128)(2,1)S(1)}, bf16[1,128,256]{2,1,0:T(8,128)(2,1)S(1)}, u32[]{:S(2)}, u32[]{:S(2)}) collective-permute-start(bf16[1,128,256]{2,1,0:T(8,128)(2,1)S(1)} %cut.12.refs_0_), channel_id=1, source_target_pairs={{0,24},{8,16},{16,8},{24,0},{1,25},{9,17},{17,9},{25,1},{2,26},{10... | collective-permute-start | bytes 196616 | tf_op jit(solution)/shard_map/ppermute | solution.py:417
  16.8 49.8 %collective-permute-done.2.first_ref = bf16[1,320,384]{2,1,0:T(8,128)(2,1)S(1)} collective-permute-done((bf16[1,320,384]{2,1,0:T(8,128)(2,1)S(1)}, bf16[1,320,384]{2,1,0:T(8,128)(2,1)S(1)}, u32[]{:S(2)}, u32[]{:S(2)}) %collective-permute-start.2) | collective-permute-done | bytes 245792 | tf_op jit(solution)/shard_map/ppermute | solution.py:417
  66.6 2.9 %collective-permute-start.1 = (bf16[1,128,128]{2,1,0:T(8,128)(2,1)S(1)}, bf16[1,128,128]{2,1,0:T(8,128)(2,1)S(1)}, u32[]{:S(2)}, u32[]{:S(2)}) collective-permute-start(bf16[1,128,128]{2,1,0:T(8,128)(2,1)S(1)} %cut.10.refs_0_), channel_id=1, source_target_pairs={{0,24},{8,16},{16,8},{24,0},{1,25},{9,17},{17,9},{25,1},{2,26},{10... | collective-permute-start | bytes 98312 | tf_op jit(solution)/shard_map/ppermute | solution.py:417
  69.5 1.2 %cut.13.grad_ref = bf16[320,1536]{1,0:T(8,128)(2,1)S(1)} custom-call(bf16[320,1536]{1,0:T(8,128)(2,1)} %bitcast.18, bf16[1,128,256]{2,1,0:T(8,128)(2,1)S(1)} %cut.12.refs_0_), custom_call_target="tpu_custom_call" | custom-call | tf_op jit(solution)/shard_map/cut/pallas_call | solution.py:364
  70.8 0.0 collective-permute-done.3.rest_ref
  70.8 0.0 copy-done
  70.8 9.5 %first_grads.1 = (bf16[12,320,384]{2,1,0:T(8,128)(2,1)}, f32[9,1,384]{2,1,0:T(1,128)S(1)}, s32[1,320]{1,0:T(1,128)S(1)}) custom-call(s32[8]{0:T(128)S(1)} %bitcast.10, bf16[1,320,384]{2,1,0:T(8,128)(2,1)S(1)} %collective-permute-done.2.first_ref, bf16[8,320,384]{2,1,0:T(8,128)(2,1)S(1)} %collective-permute-done.3.rest_ref, bf16[320,1536]{1,0:T(8,128)(2,1)S(1)} %cut.13.grad_ref), custom_call_target="tpu_custom_call" | custom-call | tf_op jit(solution)/shard_map/first_grads/pallas_call | solution.py:255
  80.2 0.2 late_mask.1._mask.mask_ref
  80.4 0.0 collective-permute-done.4.packed_ref
  80.4 2.5 %shard_map.50 = (bf16[12,320,384]{2,1,0:T(8,128)(2,1)}, f32[2,1,384]{2,1,0:T(1,128)S(1)}) custom-call(bf16[2,320,384]{2,1,0:T(8,128)(2,1)S(1)} %collective-permute-done.4.packed_ref, bf16[320,1536]{1,0:T(8,128)(2,1)S(1)} %cut.13.grad_ref, s32[1,320]{1,0:T(1,128)S(1)} %get-tuple-element.16.start_ref, ...), custom_call_target="tpu_custom_call", output_to_operand_aliasing={{0}: (4, {})} | custom-call | tf_op jit(solution)/shard_map/pallas_call | solution.py:269
  82.9 0.0 collective-permute-done.1.late_query_ref
  82.9 0.0 collective-permute-done.early_ref
  82.9 0.8 early_grads.1
  83.7 0.0 collective-permute-done.5.late_ref
  83.7 0.5 late_grads.1
  84.3 0.1 collective-permute-start.6
  84.3 0.7 store_last.1
  85.1 0.4 collective-permute-done.6
  85.5 0.6 multiply_bitcast_fusion
Async XLA Ops:
  3.2 67.6 %collective-permute-start.3 = (bf16[8,320,384]{2,1,0:T(8,128)(2,1)S(1)}, bf16[8,320,384]{2,1,0:T(8,128)(2,1)S(1)}, u32[]{:S(2)}, u32[]{:S(2)}) collective-permute-start(bf16[8,320,384]{2,1,0:T(8,128)(2,1)S(1)} %cut.8.refs_0_), channel_id=1, source_target_pairs={{0,24},{8,16},{16,8},{24,0},{1,25},{9,17},{17,9},{25,1},{2,26},{10... | collective-permute-start | bytes 5898248 | tf_op jit(solution)/shard_map/ppermute | solution.py:417
  8.2 72.2 %collective-permute-start.4 = (bf16[2,320,384]{2,1,0:T(8,128)(2,1)S(1)}, bf16[2,320,384]{2,1,0:T(8,128)(2,1)S(1)}, u32[]{:S(2)}, u32[]{:S(2)}) collective-permute-start(bf16[2,320,384]{2,1,0:T(8,128)(2,1)S(1)} %cut.9.refs_0_), channel_id=1, source_target_pairs={{0,24},{8,16},{16,8},{24,0},{1,25},{9,17},{17,9},{25,1},{2,26},{10... | collective-permute-start | bytes 1474568 | tf_op jit(solution)/shard_map/ppermute | solution.py:417
  8.3 58.3 %collective-permute-start.2 = (bf16[1,320,384]{2,1,0:T(8,128)(2,1)S(1)}, bf16[1,320,384]{2,1,0:T(8,128)(2,1)S(1)}, u32[]{:S(2)}, u32[]{:S(2)}) collective-permute-start(bf16[1,320,384]{2,1,0:T(8,128)(2,1)S(1)} %cut.7.refs_0_), channel_id=1, source_target_pairs={{0,24},{8,16},{16,8},{24,0},{1,25},{9,17},{17,9},{25,1},{2,26},{10... | collective-permute-start | bytes 737288 | tf_op jit(solution)/shard_map/ppermute | solution.py:417
  12.9 57.9 %copy-start = (s32[1,1,8]{2,1,0:T(1,128)S(1)}, s32[1,1,8]{2,1,0:T(1,128)}, u32[]{:S(2)}) copy-start(s32[1,1,8]{2,1,0:T(1,128)} %param.5) | copy-start | bytes 100
  12.9 70.0 %collective-permute-start = (bf16[1,192,384]{2,1,0:T(8,128)(2,1)S(1)}, bf16[1,192,384]{2,1,0:T(8,128)(2,1)S(1)}, u32[]{:S(2)}, u32[]{:S(2)}) collective-permute-start(bf16[1,192,384]{2,1,0:T(8,128)(2,1)S(1)} %cut.11.refs_0_), channel_id=1, source_target_pairs={{0,24},{8,16},{16,8},{24,0},{1,25},{9,17},{17,9},{25,1},{2,26},{10... | collective-permute-start | bytes 442376 | tf_op jit(solution)/shard_map/ppermute | solution.py:417
  13.9 69.8 %collective-permute-start.5 = (bf16[1,128,256]{2,1,0:T(8,128)(2,1)S(1)}, bf16[1,128,256]{2,1,0:T(8,128)(2,1)S(1)}, u32[]{:S(2)}, u32[]{:S(2)}) collective-permute-start(bf16[1,128,256]{2,1,0:T(8,128)(2,1)S(1)} %cut.12.refs_0_), channel_id=1, source_target_pairs={{0,24},{8,16},{16,8},{24,0},{1,25},{9,17},{17,9},{25,1},{2,26},{10... | collective-permute-start | bytes 196616 | tf_op jit(solution)/shard_map/ppermute | solution.py:417
  66.6 16.3 %collective-permute-start.1 = (bf16[1,128,128]{2,1,0:T(8,128)(2,1)S(1)}, bf16[1,128,128]{2,1,0:T(8,128)(2,1)S(1)}, u32[]{:S(2)}, u32[]{:S(2)}) collective-permute-start(bf16[1,128,128]{2,1,0:T(8,128)(2,1)S(1)} %cut.10.refs_0_), channel_id=1, source_target_pairs={{0,24},{8,16},{16,8},{24,0},{1,25},{9,17},{17,9},{25,1},{2,26},{10... | collective-permute-start | bytes 98312 | tf_op jit(solution)/shard_map/ppermute | solution.py:417
  84.3 1.3 %collective-permute-start.6 = (f32[12,1,384]{2,1,0:T(1,128)S(1)}, f32[12,1,384]{2,1,0:T(1,128)S(1)}, u32[]{:S(2)}, u32[]{:S(2)}) collective-permute-start(f32[12,1,384]{2,1,0:T(1,128)S(1)} %get-tuple-element.29), channel_id=1, source_target_pairs={{0,1},{1,0},{2,3},{3,2},{4,5},{5,4},{6,7},{7,6},{8,9},{9,8},{10,11... | collective-permute-start | bytes 55304 | tf_op jit(solution)/shard_map/ppermute | solution.py:386
